TPU v7x, 512 devices: a whole 4x8x8 slice. The times are simulated.
512 devices in a mesh: pipe: 16 (over y, core), expert: 16 (over z, x_hi), tensor: 2 (over x_lo).
Axes of the slice: x: 4 (x_hi: 2, x_lo: 2; x = x_hi * 2 + x_lo), y: 8, z: 8, core: 2. Of those that a mesh axis runs over, the one named last changes fastest.
Arguments:
- acts: bfloat16 [16, 2, 2048, 2048], P('pipe', None, 'expert', 'tensor'), may hold values from -6 to 6
- out_grad: bfloat16 [16, 2, 2048, 2048], P('pipe', None, 'expert', 'tensor'), may hold values from -4 to 4
- probs: bfloat16 [16, 2, 2048], P('pipe', None, 'expert'), may hold values from 0.099609375 to 1
- counts: int32 [16, 2, 16, 16], P('pipe', None, 'expert'), may hold values from 1 to 16, as said below
- w_gate: bfloat16 [16, 16, 1024, 512], P('pipe', 'expert', None, 'tensor'), may hold values from -0.125 to 0.125
- w_up: bfloat16 [16, 16, 1024, 512], P('pipe', 'expert', None, 'tensor'), may hold values from -0.125 to 0.125
- w_down: bfloat16 [16, 16, 512, 1024], P('pipe', 'expert', 'tensor'), may hold values from -0.25 to 0.25
Outputs:
- act_grad: bfloat16 [16, 2, 2048, 2048], P('pipe', None, 'expert', 'tensor')
- prob_grad: bfloat16 [16, 2, 2048], P('pipe', None, 'expert')
- gate_grad: bfloat16 [16, 16, 1024, 512], P('pipe', 'expert', None, 'tensor')
- up_grad: bfloat16 [16, 16, 1024, 512], P('pipe', 'expert', None, 'tensor')
- down_grad: bfloat16 [16, 16, 512, 1024], P('pipe', 'expert', 'tensor')
Inputs may be any that keep to these rules, and one draw needn't show every extreme that they name: Row [p, d, s] of counts sums to 128; for each section and direction one expert gets exactly 16 rows from every source; no count exceeds 16.
All inputs are finite; a program needn't handle non-finite values.
Results may differ from a plain program's by a relative error of at most 0.008.
Values may be sent and summed in bfloat16 or wider, within the bound.
No kernel may reach another device: no remote copies, remote signals or barrier semaphores. Data moves between devices by JAX's collectives and lax.ppermute only.
A program may use at most 64 MiB of HBM per device.

v0:
```python
import jax
import jax.numpy as jnp
from jax import lax
from jax.sharding import PartitionSpec as P


def partner(array, axis, apart):
    return lax.ppermute(array, axis, [(i, i ^ 1 << apart) for i in range(lax.axis_size(axis))])


def from_everyone(array, axis):
    peers = lax.axis_size(axis)
    return lax.all_to_all(
        jnp.broadcast_to(array[None], (peers, *array.shape)), axis, 0, 0, tiled=True
    )


def laid_out(blocks, dim):
    lengths = list(blocks.shape[1:])
    lengths[dim] *= blocks.shape[0]
    return jnp.moveaxis(blocks, 0, dim).reshape(lengths)


def gathered_copies(array, axis, dim):
    blocks = from_everyone(array, axis)
    return laid_out(blocks, dim)


def in_one_piece(arrays, axis, dim, along):
    both = jnp.concatenate(arrays, axis=along)
    result, at, done = (gathered_copies(both, axis, dim), 0, [])
    for a in arrays:
        done.append(lax.slice_in_dim(result, at, at + a.shape[along], axis=along))
        at += a.shape[along]
    return tuple(done)


def side_by_side(arrays, axis, split_dim, concat_dim, along):
    columns = [a.reshape(*a.shape[:along], -1) for a in arrays]
    both = jnp.concatenate(columns, axis=along)
    result, at, done = (
        lax.all_to_all(both, axis, split_axis=split_dim, concat_axis=concat_dim, tiled=True),
        0,
        [],
    )
    for a, column in zip(arrays, columns):
        piece = result[..., at : at + column.shape[along]]
        done.append(piece.reshape(*piece.shape[:along], *a.shape[along:]))
        at += column.shape[along]
    return tuple(done)


def split_up(array, dim, peers):
    lengths = array.shape
    blocks = array.reshape(*lengths[:dim], peers, lengths[dim] // peers, *lengths[dim + 1 :])
    return jnp.moveaxis(blocks, dim, 0)


def sum_at_owner(array, axis, dim):
    blocks = split_up(array, dim, lax.axis_size(axis))
    arrived = lax.all_to_all(blocks, axis, split_axis=0, concat_axis=0, tiled=True)
    return arrived.sum(axis=0)


def of_everyone(array, axis):
    return from_everyone(array, axis).sum(axis=0)


def silu_parts(gate):
    sigma = jax.nn.sigmoid(gate)
    return (gate * sigma, sigma * (1.0 + gate * (1.0 - sigma)))


def slot_tables(count_rows, slots):
    ends = jnp.cumsum(count_rows, axis=-1)
    starts = ends - count_rows
    position = jnp.arange(slots, dtype=jnp.int32)
    local = starts[..., None] + position
    live = position < count_rows[..., None]
    return (jnp.where(live, local, 0), live, starts, ends)


def global_slots(local, rows):
    dir_ids = jnp.arange(2, dtype=jnp.int32)[:, None, None]
    return (dir_ids * rows + local).reshape(-1)


def pack_rows(values, local, live):
    experts, slots = (local.shape[1], local.shape[2])
    rows, width = (values.shape[1], values.shape[2])
    taken = jnp.take(values.reshape(-1, width), global_slots(local, rows), axis=0)
    taken = jnp.where(live.reshape(-1)[:, None], taken, jnp.zeros_like(taken))
    return taken.reshape(2, experts, slots, width)


def pack_scalars(values, local, live):
    experts, slots = (local.shape[1], local.shape[2])
    rows = values.shape[1]
    taken = jnp.take(values.reshape(-1), global_slots(local, rows), axis=0)
    taken = jnp.where(live.reshape(-1), taken, jnp.zeros_like(taken))
    return taken.reshape(2, experts, slots)


def expert_terms(input_rows, grad_rows, prob_rows, full_gate, full_up, full_down):
    gate = jnp.dot(input_rows, full_gate, preferred_element_type=jnp.float32)
    up = jnp.dot(input_rows, full_up, preferred_element_type=jnp.float32)
    silu_value, slope = silu_parts(gate)
    act = (silu_value * up).astype(jnp.bfloat16)
    back = lax.dot_general(
        grad_rows, full_down, (((1,), (1,)), ((), ())), preferred_element_type=jnp.float32
    )
    prob_term = jnp.sum(act.astype(jnp.float32) * back, axis=1)
    scale = prob_rows.astype(jnp.float32)[:, None]
    d_gate = (scale * back * up * slope).astype(jnp.bfloat16)
    d_up = (scale * back * silu_value).astype(jnp.bfloat16)
    scaled = (scale * grad_rows.astype(jnp.float32)).astype(jnp.bfloat16)
    input_grad = lax.dot_general(
        d_gate, full_gate, (((1,), (1,)), ((), ())), preferred_element_type=jnp.float32
    )
    input_grad = input_grad + lax.dot_general(
        d_up, full_up, (((1,), (1,)), ((), ())), preferred_element_type=jnp.float32
    )
    gate_term = lax.dot_general(
        input_rows, d_gate, (((0,), (0,)), ((), ())), preferred_element_type=jnp.float32
    )
    up_term = lax.dot_general(
        input_rows, d_up, (((0,), (0,)), ((), ())), preferred_element_type=jnp.float32
    )
    down_term = lax.dot_general(
        act, scaled, (((0,), (0,)), ((), ())), preferred_element_type=jnp.float32
    )
    return (input_grad, prob_term, (gate_term, up_term, down_term))


def half_pair(first, whole, axis):
    half = whole.shape[axis] // 2
    lower = lax.slice_in_dim(whole, 0, half, axis=axis)
    higher = lax.slice_in_dim(whole, half, 2 * half, axis=axis)
    return (jnp.where(first, lower, higher), jnp.where(first, higher, lower))


def settle(keep, arrived):
    return (keep.astype(jnp.float32) + arrived.astype(jnp.float32)).astype(jnp.bfloat16)[None, None]


def on_device(acts, out_grad, probs, counts, w_gate, w_up, w_down):
    experts = lax.axis_size("expert")
    pipes = lax.axis_size("pipe")
    top_bit = pipes.bit_length() - 2
    rows = acts.shape[2]
    slots = 2 * rows // experts
    first = lax.axis_index("pipe") // (pipes // 2) == 0
    owned = (w_gate[0, 0], w_up[0, 0], w_down[0, 0])
    other = partner((owned[0], owned[1], owned[2]), "pipe", top_bit)
    full_gate = jnp.concatenate(
        [jnp.where(first, owned[0], other[0]), jnp.where(first, other[0], owned[0])], axis=0
    )
    full_up = jnp.concatenate(
        [jnp.where(first, owned[1], other[1]), jnp.where(first, other[1], owned[1])], axis=0
    )
    full_down = jnp.concatenate(
        [jnp.where(first, owned[2], other[2]), jnp.where(first, other[2], owned[2])], axis=1
    )
    local, live, starts, ends = slot_tables(counts[0, :, 0, :], slots)
    prob_slots = pack_scalars(probs[0], local, live)
    input_whole, grad_whole = in_one_piece((acts[0], out_grad[0]), "tensor", 2, 0)
    input_send = pack_rows(input_whole, local, live)
    grad_send = pack_rows(grad_whole, local, live)
    input_recv, grad_recv, prob_recv = side_by_side(
        (input_send, grad_send, prob_slots), "expert", 1, 1, 3
    )
    width = input_recv.shape[-1]
    input_flat = input_recv.reshape(-1, width)
    grad_flat = grad_recv.reshape(-1, width)
    prob_flat = prob_recv.reshape(-1)
    input_grad, prob_term, weight_terms = expert_terms(
        input_flat, grad_flat, prob_flat, full_gate, full_up, full_down
    )
    row_part = sum_at_owner(input_grad, "tensor", 1).astype(jnp.bfloat16)
    prob_sum = of_everyone(prob_term, "tensor").astype(jnp.bfloat16)
    half_width = row_part.shape[-1]
    back_rows, back_probs = side_by_side(
        (row_part.reshape(2, experts, slots, half_width), prob_sum.reshape(2, experts, slots)),
        "expert",
        1,
        1,
        3,
    )
    row_ids = jnp.arange(rows, dtype=jnp.int32)
    owner = jnp.sum((ends[:, None, :] <= row_ids[None, :, None]).astype(jnp.int32), axis=2)
    start_row = jnp.take_along_axis(starts, owner, axis=1)
    dir_ids = jnp.arange(2, dtype=jnp.int32)[:, None]
    slot_place = ((dir_ids * experts + owner) * slots + row_ids - start_row).reshape(-1)
    act_grad = jnp.take(back_rows.reshape(-1, half_width), slot_place, axis=0).reshape(
        1, 2, rows, half_width
    )
    prob_grad = jnp.take(back_probs.reshape(-1), slot_place, axis=0).reshape(1, 2, rows)
    gate_keep, gate_send = half_pair(first, weight_terms[0].astype(jnp.bfloat16), 0)
    up_keep, up_send = half_pair(first, weight_terms[1].astype(jnp.bfloat16), 0)
    down_keep, down_send = half_pair(first, weight_terms[2].astype(jnp.bfloat16), 1)
    arrived = partner((gate_send, up_send, down_send), "pipe", top_bit)
    return (
        act_grad,
        prob_grad,
        settle(gate_keep, arrived[0]),
        settle(up_keep, arrived[1]),
        settle(down_keep, arrived[2]),
    )


def solution(mesh):
    return jax.shard_map(
        on_device,
        mesh=mesh,
        in_specs=(
            P("pipe", None, "expert", "tensor"),
            P("pipe", None, "expert", "tensor"),
            P("pipe", None, "expert"),
            P("pipe", None, "expert", None),
            P("pipe", "expert", None, "tensor"),
            P("pipe", "expert", None, "tensor"),
            P("pipe", "expert", "tensor", None),
        ),
        out_specs=(
            P("pipe", None, "expert", "tensor"),
            P("pipe", None, "expert"),
            P("pipe", "expert", None, "tensor"),
            P("pipe", "expert", None, "tensor"),
            P("pipe", "expert", "tensor", None),
        ),
        check_vma=False,
    )
```

profile of v0, /device:TPU:38, one launch (start us, length us, event | category | flops | bytes accessed | tf_op | source)
XLA Modules:
  0.0 319.2 jit_solution(11325304728602738281)
XLA Ops:
  3.5 4.7 %all-to-all-start = ((bf16[2,4,128,1024]{3,2,1,0:T(8,128)(2,1)}), bf16[2,4,128,1024]{3,2,1,0:T(8,128)(2,1)S(1)}, u32[]{:S(2)}, u32[]{:S(2)}) async-start(bf16[2,4,128,1024]{3,2,1,0:T(8,128)(2,1)} %broadcast_in_dim.98), calls=%async_computation | async-start | bytes 4194304 | tf_op jit(solution)/shard_map/all_to_all | solution.py:13
  9.1 3.4 %gather_fusion = bf16[512]{0:T(512)(128)(2,1)S(1)} fusion(bf16[256]{0:T(256)(128)(2,1)S(1)} %bitcast.91, s32[1024]{0:T(1024)S(1)} %pad_clamp_fusion.1), kind=kCustom, calls=%fused_computation.2 | custom fusion | bytes 4096 | tf_op jit(solution)/shard_map/jit(_take)/gather | solution.py:99
  12.9 18.7 %all-to-all-done = bf16[2,4,128,1024]{3,2,1,0:T(8,128)(2,1)S(1)} async-done(((bf16[2,4,128,1024]{3,2,1,0:T(8,128)(2,1)}), bf16[2,4,128,1024]{3,2,1,0:T(8,128)(2,1)S(1)}, u32[]{:S(2)}, u32[]{:S(2)}) %all-to-all-start) | async-done | bytes 2097184 | tf_op jit(solution)/shard_map/all_to_all | solution.py:13
  34.5 3.3 %gather_fusion.4 = bf16[512,2048]{1,0:T(8,128)(2,1)} fusion(bf16[256,2048]{1,0:T(8,128)(2,1)S(1)} %bitcast.92, s32[1024]{0:T(1024)S(1)} %pad_clamp_fusion.2), kind=kCustom, calls=%fused_computation.clone | custom fusion | bytes 4196352 | tf_op jit(solution)/shard_map/jit(_take)/gather | solution.py:91
  37.8 3.3 %gather_fusion.5 = bf16[512,2048]{1,0:T(8,128)(2,1)} fusion(bf16[256,2048]{1,0:T(8,128)(2,1)S(1)} %bitcast.93, s32[1024]{0:T(1024)S(1)} %pad_clamp_fusion.2), kind=kCustom, calls=%fused_computation.1.clone | custom fusion | bytes 4196352 | tf_op jit(solution)/shard_map/jit(_take)/gather | solution.py:91
  41.1 2.6 select_select_fusion.1
  46.0 13.4 %all-to-all-start.1 = ((bf16[2,16,16,4097]{3,2,0,1:T(8,128)(2,1)}), bf16[2,16,16,4097]{3,2,0,1:T(8,128)(2,1)}, u32[]{:S(2)}, u32[]{:S(2)}) async-start(bf16[2,16,16,4097]{3,2,0,1:T(8,128)(2,1)} %pad_maximum_fusion), calls=%async_computation.1 | async-start | bytes 8650752 | tf_op jit(solution)/shard_map/all_to_all | solution.py:42
  61.5 7.7 %collective-permute-start.1 = (bf16[1024,256]{1,0:T(8,128)(2,1)S(1)}, bf16[1024,256]{1,0:T(8,128)(2,1)}, u32[]{:S(2)}, u32[]{:S(2)}) collective-permute-start(bf16[1024,256]{1,0:T(8,128)(2,1)S(1)} %bitcast.111), channel_id=1, source_target_pairs={{0,256},{32,288},{64,320},{96,352},{128,384},{160,416},{192,448},{... | collective-permute-start | bytes 1572872 | tf_op jit(solution)/shard_map/ppermute | solution.py:8
  71.2 14.4 %collective-permute-done = bf16[256,1024]{1,0:T(8,128)(2,1)S(1)} collective-permute-done((bf16[256,1024]{1,0:T(8,128)(2,1)S(1)}, bf16[256,1024]{1,0:T(8,128)(2,1)S(1)}, u32[]{:S(2)}, u32[]{:S(2)}) %collective-permute-start) | collective-permute-done | bytes 524320 | tf_op jit(solution)/shard_map/ppermute | solution.py:8
  86.7 19.1 %collective-permute-done.1 = bf16[1024,256]{1,0:T(8,128)(2,1)} collective-permute-done((bf16[1024,256]{1,0:T(8,128)(2,1)S(1)}, bf16[1024,256]{1,0:T(8,128)(2,1)}, u32[]{:S(2)}, u32[]{:S(2)}) %collective-permute-start.1) | collective-permute-done | bytes 524320 | tf_op jit(solution)/shard_map/ppermute | solution.py:8
  107.0 27.5 %collective-permute-done.2 = bf16[1024,256]{1,0:T(8,128)(2,1)S(1)} collective-permute-done((bf16[1024,256]{1,0:T(8,128)(2,1)S(1)}, bf16[1024,256]{1,0:T(8,128)(2,1)S(1)}, u32[]{:S(2)}, u32[]{:S(2)}) %collective-permute-start.2) | collective-permute-done | bytes 524320 | tf_op jit(solution)/shard_map/ppermute | solution.py:8
  134.5 23.0 %all-to-all-done.1 = bf16[2,16,16,4097]{3,2,0,1:T(8,128)(2,1)} async-done(((bf16[2,16,16,4097]{3,2,0,1:T(8,128)(2,1)}), bf16[2,16,16,4097]{3,2,0,1:T(8,128)(2,1)}, u32[]{:S(2)}, u32[]{:S(2)}) %all-to-all-start.1) | async-done | bytes 4195360 | tf_op jit(solution)/shard_map/all_to_all | solution.py:42
  158.8 2.7 fusion.31
  165.8 4.7 %all-to-all-start.3 = ((f32[2,1,512]{2,1,0:T(1,128)}), f32[2,1,512]{2,1,0:T(1,128)S(1)}, u32[]{:S(2)}, u32[]{:S(2)}) async-start(f32[2,1,512]{2,1,0:T(1,128)} %broadcast_in_dim.105), calls=%async_computation.3 | async-start | bytes 8192 | tf_op jit(solution)/shard_map/all_to_all | solution.py:13
  174.3 5.8 %all-to-all-start.2 = ((f32[2,512,1024]{2,1,0:T(8,128)}), f32[2,512,1024]{2,1,0:T(8,128)}, u32[]{:S(2)}, u32[]{:S(2)}) async-start(f32[2,512,1024]{2,1,0:T(8,128)} %bitcast.96), calls=%async_computation.2 | async-start | bytes 8388608 | tf_op jit(solution)/shard_map/all_to_all | solution.py:61
  180.2 2.4 gather_fusion.3
  182.9 2.4 convolution_convert_fusion
  185.6 39.8 %all-to-all-done.2 = f32[2,512,1024]{2,1,0:T(8,128)} async-done(((f32[2,512,1024]{2,1,0:T(8,128)}), f32[2,512,1024]{2,1,0:T(8,128)}, u32[]{:S(2)}, u32[]{:S(2)}) %all-to-all-start.2) | async-done | bytes 4194336 | tf_op jit(solution)/shard_map/all_to_all | solution.py:61
  225.3 2.7 reduce_sum.44
  229.3 8.2 %all-to-all-start.4 = ((bf16[2,16,16,1025]{3,2,0,1:T(8,128)(2,1)}), bf16[2,16,16,1025]{3,2,0,1:T(8,128)(2,1)S(1)}, u32[]{:S(2)}, u32[]{:S(2)}) async-start(bf16[2,16,16,1025]{3,2,0,1:T(8,128)(2,1)} %copy.68), calls=%async_computation.4 | async-start | bytes 2359296 | tf_op jit(solution)/shard_map/all_to_all | solution.py:42
  242.1 7.7 %collective-permute-start.3 = (bf16[1024,256]{1,0:T(8,128)(2,1)S(1)}, bf16[1024,256]{1,0:T(8,128)(2,1)S(1)}, u32[]{:S(2)}, u32[]{:S(2)}) collective-permute-start(bf16[1024,256]{1,0:T(8,128)(2,1)S(1)} %broadcast_select_fusion.1), channel_id=1, source_target_pairs={{0,256},{32,288},{64,320},{96,352},{128,384},{160,416},{192,448},{... | collective-permute-start | bytes 1572872 | tf_op jit(solution)/shard_map/ppermute | solution.py:8
  252.8 11.2 %collective-permute-done.5 = bf16[256,1024]{1,0:T(8,128)(2,1)S(1)} collective-permute-done((bf16[256,1024]{1,0:T(8,128)(2,1)S(1)}, bf16[256,1024]{1,0:T(8,128)(2,1)S(1)}, u32[]{:S(2)}, u32[]{:S(2)}) %collective-permute-start.5) | collective-permute-done | bytes 524320 | tf_op jit(solution)/shard_map/ppermute | solution.py:8
  265.0 19.0 %collective-permute-done.3 = bf16[1024,256]{1,0:T(8,128)(2,1)S(1)} collective-permute-done((bf16[1024,256]{1,0:T(8,128)(2,1)S(1)}, bf16[1024,256]{1,0:T(8,128)(2,1)S(1)}, u32[]{:S(2)}, u32[]{:S(2)}) %collective-permute-start.3) | collective-permute-done | bytes 524320 | tf_op jit(solution)/shard_map/ppermute | solution.py:8
  285.0 27.9 %collective-permute-done.4 = bf16[1024,256]{1,0:T(8,128)(2,1)S(1)} collective-permute-done((bf16[1024,256]{1,0:T(8,128)(2,1)S(1)}, bf16[1024,256]{1,0:T(8,128)(2,1)S(1)}, u32[]{:S(2)}, u32[]{:S(2)}) %collective-permute-start.4) | collective-permute-done | bytes 524320 | tf_op jit(solution)/shard_map/ppermute | solution.py:8
  (97 shorter events, 42.5 us)
Async XLA Ops:
  0.6 8.4 %copy-start = (bf16[1,2,128]{2,1,0:T(2,128)(2,1)S(1)}, bf16[1,2,128]{2,1,0:T(2,128)(2,1)}, u32[]{:S(2)}) copy-start(bf16[1,2,128]{2,1,0:T(2,128)(2,1)} %param.11) | copy-start | bytes 1540
  3.5 4.7 %copy-start.10 = (s32[1,2,1,16]{3,2,1,0:T(1,128)S(1)}, s32[1,2,1,16]{3,2,1,0:T(1,128)}, u32[]{:S(2)}) copy-start(s32[1,2,1,16]{3,2,1,0:T(1,128)} %param.12) | copy-start | bytes 388
  3.5 28.1 %all-to-all-start = ((bf16[2,4,128,1024]{3,2,1,0:T(8,128)(2,1)}), bf16[2,4,128,1024]{3,2,1,0:T(8,128)(2,1)S(1)}, u32[]{:S(2)}, u32[]{:S(2)}) async-start(bf16[2,4,128,1024]{3,2,1,0:T(8,128)(2,1)} %broadcast_in_dim.98), calls=%async_computation | async-start | bytes 4194304 | tf_op jit(solution)/shard_map/all_to_all | solution.py:13
  46.0 13.4 %copy-start.5 = (bf16[1,1,256,1024]{3,2,1,0:T(8,128)(2,1)S(1)}, bf16[1,1,256,1024]{3,2,1,0:T(8,128)(2,1)}, u32[]{:S(2)}) copy-start(bf16[1,1,256,1024]{3,2,1,0:T(8,128)(2,1)} %param.15) | copy-start | bytes 1572868
  46.0 15.5 %copy-start.6 = (bf16[1,1,1024,256]{3,2,1,0:T(8,128)(2,1)S(1)}, bf16[1,1,1024,256]{3,2,1,0:T(8,128)(2,1)}, u32[]{:S(2)}) copy-start(bf16[1,1,1024,256]{3,2,1,0:T(8,128)(2,1)} %param.14) | copy-start | bytes 1572868
  46.0 23.2 %copy-start.7 = (bf16[1,1,1024,256]{3,2,1,0:T(8,128)(2,1)S(1)}, bf16[1,1,1024,256]{3,2,1,0:T(8,128)(2,1)}, u32[]{:S(2)}) copy-start(bf16[1,1,1024,256]{3,2,1,0:T(8,128)(2,1)} %param.13) | copy-start | bytes 1572868
  46.0 111.5 %all-to-all-start.1 = ((bf16[2,16,16,4097]{3,2,0,1:T(8,128)(2,1)}), bf16[2,16,16,4097]{3,2,0,1:T(8,128)(2,1)}, u32[]{:S(2)}, u32[]{:S(2)}) async-start(bf16[2,16,16,4097]{3,2,0,1:T(8,128)(2,1)} %pad_maximum_fusion), calls=%async_computation.1 | async-start | bytes 8650752 | tf_op jit(solution)/shard_map/all_to_all | solution.py:42
  59.4 26.3 %collective-permute-start = (bf16[256,1024]{1,0:T(8,128)(2,1)S(1)}, bf16[256,1024]{1,0:T(8,128)(2,1)S(1)}, u32[]{:S(2)}, u32[]{:S(2)}) collective-permute-start(bf16[256,1024]{1,0:T(8,128)(2,1)S(1)} %bitcast.110), channel_id=1, source_target_pairs={{0,256},{32,288},{64,320},{96,352},{128,384},{160,416},{192,448},{... | collective-permute-start | bytes 1572872 | tf_op jit(solution)/shard_map/ppermute | solution.py:8
  61.5 44.4 %collective-permute-start.1 = (bf16[1024,256]{1,0:T(8,128)(2,1)S(1)}, bf16[1024,256]{1,0:T(8,128)(2,1)}, u32[]{:S(2)}, u32[]{:S(2)}) collective-permute-start(bf16[1024,256]{1,0:T(8,128)(2,1)S(1)} %bitcast.111), channel_id=1, source_target_pairs={{0,256},{32,288},{64,320},{96,352},{128,384},{160,416},{192,448},{... | collective-permute-start | bytes 1572872 | tf_op jit(solution)/shard_map/ppermute | solution.py:8
  69.2 65.3 %collective-permute-start.2 = (bf16[1024,256]{1,0:T(8,128)(2,1)S(1)}, bf16[1024,256]{1,0:T(8,128)(2,1)S(1)}, u32[]{:S(2)}, u32[]{:S(2)}) collective-permute-start(bf16[1024,256]{1,0:T(8,128)(2,1)S(1)} %bitcast.112), channel_id=1, source_target_pairs={{0,256},{32,288},{64,320},{96,352},{128,384},{160,416},{192,448},{... | collective-permute-start | bytes 1572872 | tf_op jit(solution)/shard_map/ppermute | solution.py:8
  161.7 1.4 copy-start.2
  161.8 2.0 copy-start.4
  163.1 1.0 copy-start.8
  163.1 1.2 copy-start.9
  165.8 8.5 %all-to-all-start.3 = ((f32[2,1,512]{2,1,0:T(1,128)}), f32[2,1,512]{2,1,0:T(1,128)S(1)}, u32[]{:S(2)}, u32[]{:S(2)}) async-start(f32[2,1,512]{2,1,0:T(1,128)} %broadcast_in_dim.105), calls=%async_computation.3 | async-start | bytes 8192 | tf_op jit(solution)/shard_map/all_to_all | solution.py:13
  174.3 51.0 %all-to-all-start.2 = ((f32[2,512,1024]{2,1,0:T(8,128)}), f32[2,512,1024]{2,1,0:T(8,128)}, u32[]{:S(2)}, u32[]{:S(2)}) async-start(f32[2,512,1024]{2,1,0:T(8,128)} %bitcast.96), calls=%async_computation.2 | async-start | bytes 8388608 | tf_op jit(solution)/shard_map/all_to_all | solution.py:61
  229.3 84.6 %all-to-all-start.4 = ((bf16[2,16,16,1025]{3,2,0,1:T(8,128)(2,1)}), bf16[2,16,16,1025]{3,2,0,1:T(8,128)(2,1)S(1)}, u32[]{:S(2)}, u32[]{:S(2)}) async-start(bf16[2,16,16,1025]{3,2,0,1:T(8,128)(2,1)} %copy.68), calls=%async_computation.4 | async-start | bytes 2359296 | tf_op jit(solution)/shard_map/all_to_all | solution.py:42
  237.5 12.3 %copy-start.3 = (bf16[2,16,16,2048]{3,2,1,0:T(8,128)(2,1)S(1)}, bf16[2,16,16,2048]{3,2,1,0:T(8,128)(2,1)}, u32[]{:S(2)}) copy-start(bf16[2,16,16,2048]{3,2,1,0:T(8,128)(2,1)} %copy-done.2) | copy-start | bytes 6291460
  237.6 26.4 %collective-permute-start.5 = (bf16[256,1024]{1,0:T(8,128)(2,1)S(1)}, bf16[256,1024]{1,0:T(8,128)(2,1)S(1)}, u32[]{:S(2)}, u32[]{:S(2)}) collective-permute-start(bf16[256,1024]{1,0:T(8,128)(2,1)S(1)} %broadcast_select_fusion.6), channel_id=1, source_target_pairs={{0,256},{32,288},{64,320},{96,352},{128,384},{160,416},{192,448},{... | collective-permute-start | bytes 1572872 | tf_op jit(solution)/shard_map/ppermute | solution.py:8
  242.1 41.9 %collective-permute-start.3 = (bf16[1024,256]{1,0:T(8,128)(2,1)S(1)}, bf16[1024,256]{1,0:T(8,128)(2,1)S(1)}, u32[]{:S(2)}, u32[]{:S(2)}) collective-permute-start(bf16[1024,256]{1,0:T(8,128)(2,1)S(1)} %broadcast_select_fusion.1), channel_id=1, source_target_pairs={{0,256},{32,288},{64,320},{96,352},{128,384},{160,416},{192,448},{... | collective-permute-start | bytes 1572872 | tf_op jit(solution)/shard_map/ppermute | solution.py:8
  250.7 62.2 %collective-permute-start.4 = (bf16[1024,256]{1,0:T(8,128)(2,1)S(1)}, bf16[1024,256]{1,0:T(8,128)(2,1)S(1)}, u32[]{:S(2)}, u32[]{:S(2)}) collective-permute-start(bf16[1024,256]{1,0:T(8,128)(2,1)S(1)} %broadcast_select_fusion), channel_id=1, source_target_pairs={{0,256},{32,288},{64,320},{96,352},{128,384},{160,416},{192,448},{... | collective-permute-start | bytes 1572872 | tf_op jit(solution)/shard_map/ppermute | solution.py:8
  317.1 2.1 copy-start.1
where the time goes:
time: 320 us; the launch traced here: 319 us
  waiting for transfers between devices  201 us (63%)
  starting transfers between devices  60.4 us (19%)
  local copies, waits for them, and re-layouts  30.9 us (10%)
  other arithmetic  16.7 us (5%)
  matrix products  9.54 us (3%)
    ppermute x6, waiting for transfers between devices, partner(): lax.ppermute(array, axis, [(i, i ^ 1 << apart) for i in range(lax.axis_si...  119 us
    all_to_all x1, waiting for transfers between devices, sum_at_owner(): lax.all_to_all(blocks, axis, split_axis=0, concat_axis=0, tiled=True)  39.8 us
    ppermute x6, starting transfers between devices, partner(): lax.ppermute(array, axis, [(i, i ^ 1 << apart) for i in range(lax.axis_si...  23.7 us
    all_to_all x2, waiting for transfers between devices, side_by_side(): lax.all_to_all(both, axis, split_axis=split_dim, concat_axis=concat_dim,...  23 us
    all_to_all x2, starting transfers between devices, side_by_side(): lax.all_to_all(both, axis, split_axis=split_dim, concat_axis=concat_dim,...  21.6 us
    all_to_all x2, waiting for transfers between devices, from_everyone(): lax.all_to_all(jnp.broadcast_to(array[None], (peers, *array.shape)), axis...  18.7 us
    all_to_all x2, starting transfers between devices, from_everyone(): lax.all_to_all(jnp.broadcast_to(array[None], (peers, *array.shape)), axis...  9.37 us
    gather x2, local copies, waits for them, and re-layouts, pack_rows(): jnp.take(values.reshape(-1, width), global_slots(local, rows), axis=0)  6.57 us
  transfers between devices with their start and end apart: 11, of which 9 were waited for; matrix products, arithmetic and copies ran while one was open for 7% of the time, Pallas kernels for 0%

commit v1 on v0

v1 whole, which is shorter than its diff:
```python
import jax
import jax.numpy as jnp
from jax import lax
from jax.experimental import pallas as pl
from jax.experimental.pallas import tpu as pltpu
from jax.sharding import PartitionSpec as P


BF = jnp.bfloat16
F32 = jnp.float32
VM = pl.BlockSpec(memory_space=pltpu.VMEM)
HB = pl.BlockSpec(memory_space=pltpu.HBM)


def dot(a, b, ca, cb):
    return lax.dot_general(a, b, (((ca,), (cb,)), ((), ())), preferred_element_type=F32)


def call(body, outs, args, in_specs, out_specs, scratch=(), flops=0):
    moved = sum(a.size * a.dtype.itemsize for a in (*args, *outs))
    return pl.pallas_call(
        body,
        out_shape=tuple(outs),
        in_specs=in_specs,
        out_specs=tuple(out_specs),
        scratch_shapes=scratch,
        cost_estimate=pl.CostEstimate(flops=flops, bytes_accessed=moved, transcendentals=0),
    )(*args)


def shape(dims, kind):
    return jax.ShapeDtypeStruct(dims, kind)


def slot_choice(count_row, slots, rows):
    experts = count_row.shape[1]
    total = experts * slots
    owner = lax.broadcasted_iota(jnp.int32, (total, experts), 0) // slots
    expert = lax.broadcasted_iota(jnp.int32, (total, experts), 1)
    count = jnp.sum(jnp.where(expert == owner, count_row, 0), axis=1, keepdims=True)
    start = jnp.sum(jnp.where(expert < owner, count_row, 0), axis=1, keepdims=True)
    place = lax.broadcasted_iota(jnp.int32, (total, 1), 0) % slots
    target = jnp.where(place < count, start + place, -1)
    return lax.broadcasted_iota(jnp.int32, (total, rows), 1) == target


def pack_body(counts_ref, values_ref, out_ref):
    dirs, rows, width = values_ref.shape
    experts, _, slots, _ = out_ref.shape
    for d in range(dirs):
        mask = slot_choice(counts_ref[d : d + 1, :], slots, rows)
        packed = dot(mask.astype(BF), values_ref[d], 1, 0).astype(BF)
        out_ref[:, d] = packed.reshape(experts, slots, width)


def pack_scaled_body(counts_ref, probs_ref, values_ref, out_ref):
    dirs, rows, width = values_ref.shape
    experts, _, slots, _ = out_ref.shape
    for d in range(dirs):
        mask = slot_choice(counts_ref[d : d + 1, :], slots, rows)
        weight = jnp.where(mask, probs_ref[d : d + 1, :].astype(F32), 0.0).astype(BF)
        packed = dot(weight, values_ref[d], 1, 0).astype(BF)
        out_ref[:, d] = packed.reshape(experts, slots, width)


def unpack_body(counts_ref, slots_ref, out_ref):
    experts, dirs, slots, width = slots_ref.shape
    rows = out_ref.shape[1]
    for d in range(dirs):
        mask = slot_choice(counts_ref[d : d + 1, :], slots, rows)
        filled = slots_ref[:, d].reshape(experts * slots, width)
        out_ref[d] = dot(mask.astype(BF), filled, 0, 0).astype(BF)


def unpack_prob_body(counts_ref, probs_ref, own_ref, other_ref, out_ref):
    dirs, rows = out_ref.shape
    experts = own_ref.shape[0]
    total = own_ref[:, 0, :] + other_ref[:, 0, :]
    slots = 2 * rows // experts
    row = lax.broadcasted_iota(jnp.int32, (slots, rows), 1)
    place = lax.broadcasted_iota(jnp.int32, (slots, rows), 0)
    for d in range(dirs):
        found = jnp.zeros((slots, rows), F32)
        start = jnp.zeros((1, 1), jnp.int32)
        for e in range(experts):
            count = counts_ref[d : d + 1, e : e + 1]
            here = (row - start == place) & (place < count)
            values = total[e : e + 1, d * slots : (d + 1) * slots].reshape(slots, 1)
            found = jnp.where(here, values, found)
            start = start + count
        summed = jnp.sum(found, axis=0, keepdims=True)
        out_ref[d : d + 1, :] = (summed / probs_ref[d : d + 1, :].astype(F32)).astype(BF)


def half_index():
    return lax.axis_index("pipe") // (lax.axis_size("pipe") // 2)


def load(copies):
    for c in copies:
        c.start()
    for c in copies:
        c.wait()


def hidden_body(own, other, wg, wgo, wu, wuo, act_ref, silu_ref, slope_ref, xs, ws, sems):
    same = (lax.axis_index("tensor") == half_index()).astype(jnp.int32)
    load([
        pltpu.make_async_copy(own, xs.at[1 - same], sems.at[0]),
        pltpu.make_async_copy(other, xs.at[same], sems.at[1]),
        pltpu.make_async_copy(wg, ws.at[0], sems.at[2]),
        pltpu.make_async_copy(wgo, ws.at[1], sems.at[3]),
        pltpu.make_async_copy(wu, ws.at[2], sems.at[4]),
        pltpu.make_async_copy(wuo, ws.at[3], sems.at[5]),
    ])
    gate = dot(xs[0], ws[0], 1, 0) + dot(xs[1], ws[1], 1, 0)
    up = dot(xs[0], ws[2], 1, 0) + dot(xs[1], ws[3], 1, 0)
    sigma = jax.nn.sigmoid(gate)
    silu = gate * sigma
    act_ref[...] = (silu * up).astype(BF)
    silu_ref[...] = silu
    slope_ref[...] = up * (sigma * (1.0 + gate * (1.0 - sigma)))


def slope_body(
    own, other, wd, wdo, xown, xother, act, silu, slope,
    dg_ref, du_ref, prob_ref, down_ref, gate_ref, up_ref,
    gs, xs, ws, sems,
):
    same = (lax.axis_index("tensor") == half_index()).astype(jnp.int32)

    @pl.when(same == 1)
    def _():
        pltpu.make_async_copy(xother, xs, sems.at[4]).start()

    @pl.when(same == 0)
    def _():
        pltpu.make_async_copy(xown, xs, sems.at[4]).start()

    load([
        pltpu.make_async_copy(own, gs.at[1 - same], sems.at[0]),
        pltpu.make_async_copy(other, gs.at[same], sems.at[1]),
        pltpu.make_async_copy(wd, ws.at[0], sems.at[2]),
        pltpu.make_async_copy(wdo, ws.at[1], sems.at[3]),
    ])
    pltpu.make_async_copy(xown, xs, sems.at[4]).wait()
    back = dot(gs[0], ws[0], 1, 1) + dot(gs[1], ws[1], 1, 1)
    hidden = act[...]
    dg = (back * slope[...]).astype(BF)
    du = (back * silu[...]).astype(BF)
    dg_ref[...] = dg
    du_ref[...] = du
    term = hidden.astype(F32) * back
    high = term.astype(BF)
    low = (term - high.astype(F32)).astype(BF)
    ones = jnp.ones((8, term.shape[1]), BF)
    prob = dot(ones, high, 1, 1) + dot(ones, low, 1, 1)
    blocks = prob_ref.shape[0]
    width = prob.shape[1] // blocks
    prob_ref[...] = jnp.zeros_like(prob_ref)
    for s in range(blocks):
        prob_ref[s, :, 0:width] = prob[:, s * width : (s + 1) * width]
    down_ref[...] = dot(hidden, gs[1], 0, 0).astype(BF)
    gate_ref[...] = dot(xs[...], dg, 0, 0).astype(BF)
    up_ref[...] = dot(xs[...], du, 0, 0).astype(BF)


def input_body(dg, du, wg, wgo, wu, wuo, keep_ref, send_ref, ws, sems):
    same = (lax.axis_index("tensor") == half_index()).astype(jnp.int32)
    load([
        pltpu.make_async_copy(wg, ws.at[1 - same], sems.at[0]),
        pltpu.make_async_copy(wgo, ws.at[same], sems.at[1]),
        pltpu.make_async_copy(wu, ws.at[3 - same], sems.at[2]),
        pltpu.make_async_copy(wuo, ws.at[2 + same], sems.at[3]),
    ])
    send_ref[...] = (dot(dg[...], ws[1], 1, 1) + dot(du[...], ws[3], 1, 1)).astype(BF)
    keep_ref[...] = dot(dg[...], ws[0], 1, 1) + dot(du[...], ws[2], 1, 1)


def keep_body(own, other, xown, xother, act, dg, du, gate_ref, up_ref, down_ref, xs, gs, sems):
    same = lax.axis_index("tensor") == half_index()

    @pl.when(same)
    def _():
        pltpu.make_async_copy(xown, xs, sems.at[0]).start()
        pltpu.make_async_copy(own, gs, sems.at[1]).start()

    @pl.when(jnp.logical_not(same))
    def _():
        pltpu.make_async_copy(xother, xs, sems.at[0]).start()
        pltpu.make_async_copy(other, gs, sems.at[1]).start()

    pltpu.make_async_copy(xown, xs, sems.at[0]).wait()
    pltpu.make_async_copy(own, gs, sems.at[1]).wait()
    gate_ref[...] = dot(xs[...], dg[...], 0, 0)
    up_ref[...] = dot(xs[...], du[...], 0, 0)
    down_ref[...] = dot(act[...], gs[...], 0, 0)


def settle(keep, arrived):
    return (keep + arrived.astype(F32)).astype(BF)[None, None]


def on_device(acts, out_grad, probs, counts, w_gate, w_up, w_down):
    experts = lax.axis_size("expert")
    pipes = lax.axis_size("pipe")
    dirs, rows, width = acts.shape[1:]
    slots = 2 * rows // experts
    total = dirs * experts * slots
    hidden = w_gate.shape[3]
    mirror = [(i, (i + pipes // 2) % pipes) for i in range(pipes)]
    swap = [(0, 1), (1, 0)]
    count_rows = counts[0, :, 0, :]
    wg, wu, wd = (w_gate[0, 0], w_up[0, 0], w_down[0, 0])
    packed = shape((experts, dirs, slots, width), BF)
    work = 2 * dirs * experts * slots * rows * width

    (x_send,) = call(pack_body, [packed], (count_rows, acts[0]), [VM, VM], [VM], flops=work)
    (g_send,) = call(
        pack_scaled_body, [packed], (count_rows, probs[0], out_grad[0]), [VM, VM, VM], [VM], flops=work
    )
    x_own = lax.all_to_all(x_send, "expert", 0, 0, tiled=True).reshape(total, width)
    g_own = lax.all_to_all(g_send, "expert", 0, 0, tiled=True).reshape(total, width)
    wgo = lax.ppermute(wg, "pipe", mirror)
    wuo = lax.ppermute(wu, "pipe", mirror)
    wdo = lax.ppermute(wd, "pipe", mirror)
    x_other = lax.ppermute(x_own, "tensor", swap)
    g_other = lax.ppermute(g_own, "tensor", swap)

    sems = pltpu.SemaphoreType.DMA
    one = 2 * total * width * hidden
    act, silu, slope = call(
        hidden_body,
        [shape((total, hidden), BF), shape((total, hidden), F32), shape((total, hidden), F32)],
        (x_own, x_other, wg, wgo, wu, wuo),
        [HB] * 6,
        [VM] * 3,
        [pltpu.VMEM((2, total, width), BF), pltpu.VMEM((4, width, hidden), BF), sems((6,))],
        4 * one,
    )
    dg, du, prob, down_send, gate_send, up_send = call(
        slope_body,
        [
            shape((total, hidden), BF),
            shape((total, hidden), BF),
            shape((experts, 8, 128), F32),
            shape((hidden, width), BF),
            shape((width, hidden), BF),
            shape((width, hidden), BF),
        ],
        (g_own, g_other, wd, wdo, x_own, x_other, act, silu, slope),
        [HB] * 6 + [VM] * 3,
        [VM] * 6,
        [
            pltpu.VMEM((2, total, width), BF),
            pltpu.VMEM((total, width), BF),
            pltpu.VMEM((2, hidden, width), BF),
            sems((5,)),
        ],
        5 * one,
    )
    down_got = lax.ppermute(down_send, "pipe", mirror)
    gate_got = lax.ppermute(gate_send, "pipe", mirror)
    up_got = lax.ppermute(up_send, "pipe", mirror)
    row_keep, row_send = call(
        input_body,
        [shape((total, width), F32), shape((total, width), BF)],
        (dg, du, wg, wgo, wu, wuo),
        [VM] * 2 + [HB] * 4,
        [VM] * 2,
        [pltpu.VMEM((4, width, hidden), BF), sems((4,))],
        4 * one,
    )
    row_got = lax.ppermute(row_send, "tensor", swap)
    prob_own = lax.all_to_all(prob, "expert", 0, 0, tiled=True)
    prob_other = lax.ppermute(prob_own, "tensor", swap)
    gate_keep, up_keep, down_keep = call(
        keep_body,
        [shape((width, hidden), F32), shape((width, hidden), F32), shape((hidden, width), F32)],
        (g_own, g_other, x_own, x_other, act, dg, du),
        [HB] * 4 + [VM] * 3,
        [VM] * 3,
        [pltpu.VMEM((total, width), BF), pltpu.VMEM((total, width), BF), sems((2,))],
        3 * one,
    )
    (prob_grad,) = call(
        unpack_prob_body,
        [shape((dirs, rows), BF)],
        (count_rows, probs[0], prob_own, prob_other),
        [VM] * 4,
        [VM],
    )
    row_sum = (row_keep + row_got.astype(F32)).astype(BF).reshape(experts, dirs, slots, width)
    row_back = lax.all_to_all(row_sum, "expert", 0, 0, tiled=True)
    (act_grad,) = call(
        unpack_body, [shape((dirs, rows, width), BF)], (count_rows, row_back), [VM, VM], [VM], flops=work
    )
    return (
        act_grad[None],
        prob_grad[None],
        settle(gate_keep, gate_got),
        settle(up_keep, up_got),
        settle(down_keep, down_got),
    )


def solution(mesh):
    return jax.shard_map(
        on_device,
        mesh=mesh,
        in_specs=(
            P("pipe", None, "expert", "tensor"),
            P("pipe", None, "expert", "tensor"),
            P("pipe", None, "expert"),
            P("pipe", None, "expert", None),
            P("pipe", "expert", None, "tensor"),
            P("pipe", "expert", None, "tensor"),
            P("pipe", "expert", "tensor", None),
        ),
        out_specs=(
            P("pipe", None, "expert", "tensor"),
            P("pipe", None, "expert"),
            P("pipe", "expert", None, "tensor"),
            P("pipe", "expert", None, "tensor"),
            P("pipe", "expert", "tensor", None),
        ),
        check_vma=False,
    )
```

time: 320 us -> 279 us (0.87)
  the two profiles are of different devices: /device:TPU:38 before, /device:TPU:47 now
where the time goes in v1:
time: 279 us
  waiting for transfers between devices  151 us (54%)
  starting transfers between devices  84 us (30%)
  Pallas kernels  31.7 us (11%)
  other arithmetic  7.11 us (3%)
  local copies, waits for them, and re-layouts  4.2 us (2%)
    pallas_call x8, Pallas kernels, call(): pl.pallas_call(body, out_shape=tuple(outs), in_specs=in_specs, out_specs=...  31.7 us
    ppermute x1, waiting for transfers between devices, on_device(): gate_got = lax.ppermute(gate_send, 'pipe', mirror)  28.7 us
    ppermute x1, waiting for transfers between devices, on_device(): wuo = lax.ppermute(wu, 'pipe', mirror)  23.2 us
    all_to_all x1, waiting for transfers between devices, on_device(): lax.all_to_all(x_send, 'expert', 0, 0, tiled=True).reshape(total, width)  21.7 us
    all_to_all x1, waiting for transfers between devices, on_device(): lax.all_to_all(g_send, 'expert', 0, 0, tiled=True).reshape(total, width)  21 us
    ppermute x1, waiting for transfers between devices, on_device(): wdo = lax.ppermute(wd, 'pipe', mirror)  15.2 us
    all_to_all x1, starting transfers between devices, on_device(): row_back = lax.all_to_all(row_sum, 'expert', 0, 0, tiled=True)  14.7 us
    ppermute x1, waiting for transfers between devices, on_device(): wgo = lax.ppermute(wg, 'pipe', mirror)  13 us
  transfers between devices with their start and end apart: 14, of which 10 were waited for; matrix products, arithmetic and copies ran while one was open for 3% of the time, Pallas kernels for 5%

profile of v1, /device:TPU:47, one launch (start us, length us, event | category | flops | bytes accessed | tf_op | source)
XLA Modules:
  0.0 278.5 jit_solution(10524200796692498755)
XLA Ops:
  3.2 12.7 %all-to-all-start.1 = ((bf16[16,2,16,1024]{3,2,1,0:T(8,128)(2,1)}), bf16[16,2,16,1024]{3,2,1,0:T(8,128)(2,1)S(1)}, u32[]{:S(2)}, u32[]{:S(2)}) async-start(bf16[16,2,16,1024]{3,2,1,0:T(8,128)(2,1)} %shard_map.111), calls=%async_computation.1 | async-start | bytes 2097152 | tf_op jit(solution)/shard_map/all_to_all | solution.py:222
  18.6 21.7 %all-to-all-done.1 = bf16[16,2,16,1024]{3,2,1,0:T(8,128)(2,1)S(1)} async-done(((bf16[16,2,16,1024]{3,2,1,0:T(8,128)(2,1)}), bf16[16,2,16,1024]{3,2,1,0:T(8,128)(2,1)S(1)}, u32[]{:S(2)}, u32[]{:S(2)}) %all-to-all-start.1) | async-done | bytes 1048608 | tf_op jit(solution)/shard_map/all_to_all | solution.py:222
  40.3 8.9 %all-to-all-start = ((bf16[16,2,16,1024]{3,2,1,0:T(8,128)(2,1)}), bf16[16,2,16,1024]{3,2,1,0:T(8,128)(2,1)S(1)}, u32[]{:S(2)}, u32[]{:S(2)}) async-start(bf16[16,2,16,1024]{3,2,1,0:T(8,128)(2,1)} %shard_map.110), calls=%async_computation | async-start | bytes 2097152 | tf_op jit(solution)/shard_map/all_to_all | solution.py:223
  51.6 21.0 %all-to-all-done = bf16[16,2,16,1024]{3,2,1,0:T(8,128)(2,1)S(1)} async-done(((bf16[16,2,16,1024]{3,2,1,0:T(8,128)(2,1)}), bf16[16,2,16,1024]{3,2,1,0:T(8,128)(2,1)S(1)}, u32[]{:S(2)}, u32[]{:S(2)}) %all-to-all-start) | async-done | bytes 1048608 | tf_op jit(solution)/shard_map/all_to_all | solution.py:223
  75.0 2.6 collective-permute-start.3
  77.6 6.6 %collective-permute-start.4 = (bf16[1024,256]{1,0:T(8,128)(2,1)}, bf16[1024,256]{1,0:T(8,128)(2,1)S(1)}, u32[]{:S(2)}, u32[]{:S(2)}) collective-permute-start(bf16[1024,256]{1,0:T(8,128)(2,1)} %bitcast.33), channel_id=1, source_target_pairs={{0,256},{32,288},{64,320},{96,352},{128,384},{160,416},{192,448},{... | collective-permute-start | bytes 1572872 | tf_op jit(solution)/shard_map/ppermute | solution.py:225
  84.2 2.6 collective-permute-start.1
  86.9 13.0 %collective-permute-done.3.wgo = bf16[1024,256]{1,0:T(8,128)(2,1)S(1)} collective-permute-done((bf16[1024,256]{1,0:T(8,128)(2,1)}, bf16[1024,256]{1,0:T(8,128)(2,1)S(1)}, u32[]{:S(2)}, u32[]{:S(2)}) %collective-permute-start.3) | collective-permute-done | bytes 524320 | tf_op jit(solution)/shard_map/ppermute | solution.py:224
  100.7 23.2 %collective-permute-done.4.wuo = bf16[1024,256]{1,0:T(8,128)(2,1)S(1)} collective-permute-done((bf16[1024,256]{1,0:T(8,128)(2,1)}, bf16[1024,256]{1,0:T(8,128)(2,1)S(1)}, u32[]{:S(2)}, u32[]{:S(2)}) %collective-permute-start.4) | collective-permute-done | bytes 524320 | tf_op jit(solution)/shard_map/ppermute | solution.py:225
  125.7 4.5 %shard_map.112 = (bf16[512,256]{1,0:T(8,128)(2,1)}, f32[512,256]{1,0:T(8,128)}, f32[512,256]{1,0:T(8,128)}) custom-call(bf16[512,1024]{1,0:T(8,128)(2,1)} %bitcast.19, bf16[512,1024]{1,0:T(8,128)(2,1)} %copy-done.2, bf16[1024,256]{1,0:T(8,128)(2,1)} %bitcast.31, bf16[1024,256]{1,0:T(8,128)(2,1)} %copy-done.6, bf16[1024,256]{1,0:T(8,128)(2,1)} %bitcast.34, ...), custom_call_target="tpu_custom_call" | custom-call | flops 1073741824 | bytes 5505024 | tf_op jit(solution)/shard_map/pallas_call | solution.py:21
  130.2 15.2 %collective-permute-done.1.wdo = bf16[256,1024]{1,0:T(8,128)(2,1)} collective-permute-done((bf16[256,1024]{1,0:T(8,128)(2,1)}, bf16[256,1024]{1,0:T(8,128)(2,1)}, u32[]{:S(2)}, u32[]{:S(2)}) %collective-permute-start.1) | collective-permute-done | bytes 524320 | tf_op jit(solution)/shard_map/ppermute | solution.py:226
  145.4 7.1 %shard_map.113 = (bf16[512,256]{1,0:T(8,128)(2,1)}, bf16[512,256]{1,0:T(8,128)(2,1)}, f32[16,8,128]{2,1,0:T(8,128)}, bf16[256,1024]{1,0:T(8,128)(2,1)}, bf16[102...) custom-call(bf16[512,1024]{1,0:T(8,128)(2,1)} %bitcast.23, bf16[512,1024]{1,0:T(8,128)(2,1)} %collective-permute-done.other, ...), custom_call_target="tpu_custom_call" | custom-call | flops 1342177280 | bytes 8716288 | tf_op jit(solution)/shard_map/pallas_call | solution.py:21
  152.6 5.2 %shard_map.114 = (f32[512,1024]{1,0:T(8,128)}, bf16[512,1024]{1,0:T(8,128)(2,1)}) custom-call(bf16[512,256]{1,0:T(8,128)(2,1)} %get-tuple-element.22.dg, bf16[512,256]{1,0:T(8,128)(2,1)} %get-tuple-element.23.du, bf16[1024,256]{1,0:T(8,128)(2,1)} %bitcast.32, bf16[1024,256]{1,0:T(8,128)(2,1)} %copy-done.6, bf16[1024,256]{1,0:T(8,128)(2,1)} %bitcast.35, ...), custom_call_target="tpu_custom_call" | custom-call | flops 1073741824 | bytes 5767168 | tf_op jit(solution)/shard_map/pallas_call | solution.py:21
  157.8 5.5 %collective-permute-start.5 = (bf16[512,1024]{1,0:T(8,128)(2,1)}, bf16[512,1024]{1,0:T(8,128)(2,1)S(1)}, u32[]{:S(2)}, u32[]{:S(2)}) collective-permute-start(bf16[512,1024]{1,0:T(8,128)(2,1)} %get-tuple-element.25), channel_id=1, source_target_pairs={{0,1},{1,0},{2,3},{3,2},{4,5},{5,4},{6,7},{7,6},{8,9},{9,8},{10,11... | collective-permute-start | bytes 3145736 | tf_op jit(solution)/shard_map/ppermute | solution.py:274
  163.3 11.9 %all-to-all-start.3 = ((f32[16,8,128]{2,1,0:T(8,128)}), f32[16,8,128]{2,1,0:T(8,128)S(1)}, u32[]{:S(2)}, u32[]{:S(2)}) async-start(f32[16,8,128]{2,1,0:T(8,128)} %get-tuple-element.26), calls=%async_computation.3 | async-start | bytes 131072 | tf_op jit(solution)/shard_map/all_to_all | solution.py:275
  175.2 8.0 %collective-permute-done.5 = bf16[512,1024]{1,0:T(8,128)(2,1)S(1)} collective-permute-done((bf16[512,1024]{1,0:T(8,128)(2,1)}, bf16[512,1024]{1,0:T(8,128)(2,1)S(1)}, u32[]{:S(2)}, u32[]{:S(2)}) %collective-permute-start.5) | collective-permute-done | bytes 1048608 | tf_op jit(solution)/shard_map/ppermute | solution.py:274
  183.2 2.9 %add_convert_fusion = bf16[512,1024]{1,0:T(8,128)(2,1)} fusion(f32[512,1024]{1,0:T(8,128)} %get-tuple-element.24, bf16[512,1024]{1,0:T(8,128)(2,1)S(1)} %collective-permute-done.5), kind=kLoop, calls=%fused_computation | loop fusion | flops 1572864 | bytes 4194304 | tf_op jit(solution)/shard_map/convert_element_type | solution.py:293
  186.9 14.7 %all-to-all-start.2 = ((bf16[16,2,16,1024]{3,2,1,0:T(8,128)(2,1)}), bf16[16,2,16,1024]{3,2,1,0:T(8,128)(2,1)S(1)}, u32[]{:S(2)}, u32[]{:S(2)}) async-start(bf16[16,2,16,1024]{3,2,1,0:T(8,128)(2,1)} %bitcast.9), calls=%async_computation.2 | async-start | bytes 2097152 | tf_op jit(solution)/shard_map/all_to_all | solution.py:294
  203.5 7.3 %collective-permute-start.8 = (bf16[1024,256]{1,0:T(8,128)(2,1)}, bf16[1024,256]{1,0:T(8,128)(2,1)S(1)}, u32[]{:S(2)}, u32[]{:S(2)}) collective-permute-start(bf16[1024,256]{1,0:T(8,128)(2,1)} %get-tuple-element.30), channel_id=1, source_target_pairs={{0,256},{32,288},{64,320},{96,352},{128,384},{160,416},{192,448},{... | collective-permute-start | bytes 1572872 | tf_op jit(solution)/shard_map/ppermute | solution.py:264
  215.3 5.2 %shard_map.117 = (f32[1024,256]{1,0:T(8,128)}, f32[1024,256]{1,0:T(8,128)}, f32[256,1024]{1,0:T(8,128)}) custom-call(bf16[512,1024]{1,0:T(8,128)(2,1)} %bitcast.24, bf16[512,1024]{1,0:T(8,128)(2,1)} %collective-permute-done.other, bf16[512,1024]{1,0:T(8,128)(2,1)} %bitcast.21, bf16[512,1024]{1,0:T(8,128)(2,1)} %copy-done.2, ...), custom_call_target="tpu_custom_call" | custom-call | flops 805306368 | bytes 8126464 | tf_op jit(solution)/shard_map/pallas_call | solution.py:21
  222.7 28.7 %collective-permute-done.7 = bf16[1024,256]{1,0:T(8,128)(2,1)} collective-permute-done((bf16[1024,256]{1,0:T(8,128)(2,1)}, bf16[1024,256]{1,0:T(8,128)(2,1)}, u32[]{:S(2)}, u32[]{:S(2)}) %collective-permute-start.7) | collective-permute-done | bytes 524320 | tf_op jit(solution)/shard_map/ppermute | solution.py:263
  253.7 8.8 %collective-permute-done.8 = bf16[1024,256]{1,0:T(8,128)(2,1)S(1)} collective-permute-done((bf16[1024,256]{1,0:T(8,128)(2,1)}, bf16[1024,256]{1,0:T(8,128)(2,1)S(1)}, u32[]{:S(2)}, u32[]{:S(2)}) %collective-permute-start.8) | collective-permute-done | bytes 524320 | tf_op jit(solution)/shard_map/ppermute | solution.py:264
  263.4 10.3 %collective-permute-done.9 = bf16[256,1024]{1,0:T(8,128)(2,1)S(1)} collective-permute-done((bf16[256,1024]{1,0:T(8,128)(2,1)}, bf16[256,1024]{1,0:T(8,128)(2,1)S(1)}, u32[]{:S(2)}, u32[]{:S(2)}) %collective-permute-start.9) | collective-permute-done | bytes 524320 | tf_op jit(solution)/shard_map/ppermute | solution.py:262
  275.7 2.8 %shard_map.115 = bf16[2,128,1024]{2,1,0:T(8,128)(2,1)} custom-call(s32[2,16]{1,0:T(2,128)} %bitcast.39, bf16[16,2,16,1024]{3,2,1,0:T(8,128)(2,1)} %copy-done.3), custom_call_target="tpu_custom_call" | custom-call | flops 134217728 | bytes 1572992 | tf_op jit(solution)/shard_map/pallas_call | solution.py:21
  (36 shorter events, 27.3 us)
Async XLA Ops:
  3.2 37.0 %all-to-all-start.1 = ((bf16[16,2,16,1024]{3,2,1,0:T(8,128)(2,1)}), bf16[16,2,16,1024]{3,2,1,0:T(8,128)(2,1)S(1)}, u32[]{:S(2)}, u32[]{:S(2)}) async-start(bf16[16,2,16,1024]{3,2,1,0:T(8,128)(2,1)} %shard_map.111), calls=%async_computation.1 | async-start | bytes 2097152 | tf_op jit(solution)/shard_map/all_to_all | solution.py:222
  40.3 84.4 %copy-start = (bf16[16,2,16,1024]{3,2,1,0:T(8,128)(2,1)}, bf16[16,2,16,1024]{3,2,1,0:T(8,128)(2,1)S(1)}, u32[]{:S(2)}) copy-start(bf16[16,2,16,1024]{3,2,1,0:T(8,128)(2,1)S(1)} %all-to-all-done.1) | copy-start | bytes 3145732
  40.3 32.3 %all-to-all-start = ((bf16[16,2,16,1024]{3,2,1,0:T(8,128)(2,1)}), bf16[16,2,16,1024]{3,2,1,0:T(8,128)(2,1)S(1)}, u32[]{:S(2)}, u32[]{:S(2)}) async-start(bf16[16,2,16,1024]{3,2,1,0:T(8,128)(2,1)} %shard_map.110), calls=%async_computation | async-start | bytes 2097152 | tf_op jit(solution)/shard_map/all_to_all | solution.py:223
  49.1 75.6 %collective-permute-start.2 = (bf16[512,1024]{1,0:T(8,128)(2,1)S(1)}, bf16[512,1024]{1,0:T(8,128)(2,1)S(1)}, u32[]{:S(2)}, u32[]{:S(2)}) collective-permute-start(bf16[512,1024]{1,0:T(8,128)(2,1)S(1)} %bitcast.18), channel_id=1, source_target_pairs={{0,1},{1,0},{2,3},{3,2},{4,5},{5,4},{6,7},{7,6},{8,9},{9,8},{10,11... | collective-permute-start | bytes 3145736 | tf_op jit(solution)/shard_map/ppermute | solution.py:227
  72.5 57.7 %copy-start.1 = (bf16[16,2,16,1024]{3,2,1,0:T(8,128)(2,1)}, bf16[16,2,16,1024]{3,2,1,0:T(8,128)(2,1)S(1)}, u32[]{:S(2)}) copy-start(bf16[16,2,16,1024]{3,2,1,0:T(8,128)(2,1)S(1)} %all-to-all-done) | copy-start | bytes 3145732
  72.5 72.9 %collective-permute-start = (bf16[512,1024]{1,0:T(8,128)(2,1)S(1)}, bf16[512,1024]{1,0:T(8,128)(2,1)}, u32[]{:S(2)}, u32[]{:S(2)}) collective-permute-start(bf16[512,1024]{1,0:T(8,128)(2,1)S(1)} %bitcast.22), channel_id=1, source_target_pairs={{0,1},{1,0},{2,3},{3,2},{4,5},{5,4},{6,7},{7,6},{8,9},{9,8},{10,11... | collective-permute-start | bytes 3145736 | tf_op jit(solution)/shard_map/ppermute | solution.py:228
  75.0 24.9 %collective-permute-start.3 = (bf16[1024,256]{1,0:T(8,128)(2,1)}, bf16[1024,256]{1,0:T(8,128)(2,1)S(1)}, u32[]{:S(2)}, u32[]{:S(2)}) collective-permute-start(bf16[1024,256]{1,0:T(8,128)(2,1)} %bitcast.30), channel_id=1, source_target_pairs={{0,256},{32,288},{64,320},{96,352},{128,384},{160,416},{192,448},{... | collective-permute-start | bytes 1572872 | tf_op jit(solution)/shard_map/ppermute | solution.py:224
  77.6 46.2 %collective-permute-start.4 = (bf16[1024,256]{1,0:T(8,128)(2,1)}, bf16[1024,256]{1,0:T(8,128)(2,1)S(1)}, u32[]{:S(2)}, u32[]{:S(2)}) collective-permute-start(bf16[1024,256]{1,0:T(8,128)(2,1)} %bitcast.33), channel_id=1, source_target_pairs={{0,256},{32,288},{64,320},{96,352},{128,384},{160,416},{192,448},{... | collective-permute-start | bytes 1572872 | tf_op jit(solution)/shard_map/ppermute | solution.py:225
  84.2 61.2 %collective-permute-start.1 = (bf16[256,1024]{1,0:T(8,128)(2,1)}, bf16[256,1024]{1,0:T(8,128)(2,1)}, u32[]{:S(2)}, u32[]{:S(2)}) collective-permute-start(bf16[256,1024]{1,0:T(8,128)(2,1)} %bitcast.26), channel_id=1, source_target_pairs={{0,256},{32,288},{64,320},{96,352},{128,384},{160,416},{192,448},{... | collective-permute-start | bytes 1572872 | tf_op jit(solution)/shard_map/ppermute | solution.py:226
  99.9 0.8 copy-start.6
  123.9 0.8 copy-start.7
  124.7 1.0 copy-start.2
  157.8 25.4 %collective-permute-start.5 = (bf16[512,1024]{1,0:T(8,128)(2,1)}, bf16[512,1024]{1,0:T(8,128)(2,1)S(1)}, u32[]{:S(2)}, u32[]{:S(2)}) collective-permute-start(bf16[512,1024]{1,0:T(8,128)(2,1)} %get-tuple-element.25), channel_id=1, source_target_pairs={{0,1},{1,0},{2,3},{3,2},{4,5},{5,4},{6,7},{7,6},{8,9},{9,8},{10,11... | collective-permute-start | bytes 3145736 | tf_op jit(solution)/shard_map/ppermute | solution.py:274
  163.3 23.6 %all-to-all-start.3 = ((f32[16,8,128]{2,1,0:T(8,128)}), f32[16,8,128]{2,1,0:T(8,128)S(1)}, u32[]{:S(2)}, u32[]{:S(2)}) async-start(f32[16,8,128]{2,1,0:T(8,128)} %get-tuple-element.26), calls=%async_computation.3 | async-start | bytes 131072 | tf_op jit(solution)/shard_map/all_to_all | solution.py:275
  186.9 33.5 %copy-start.8 = (f32[16,8,128]{2,1,0:T(8,128)}, f32[16,8,128]{2,1,0:T(8,128)S(1)}, u32[]{:S(2)}) copy-start(f32[16,8,128]{2,1,0:T(8,128)S(1)} %all-to-all-done.3.own_ref) | copy-start | bytes 196612
  186.9 87.8 %all-to-all-start.2 = ((bf16[16,2,16,1024]{3,2,1,0:T(8,128)(2,1)}), bf16[16,2,16,1024]{3,2,1,0:T(8,128)(2,1)S(1)}, u32[]{:S(2)}, u32[]{:S(2)}) async-start(bf16[16,2,16,1024]{3,2,1,0:T(8,128)(2,1)} %bitcast.9), calls=%async_computation.2 | async-start | bytes 2097152 | tf_op jit(solution)/shard_map/all_to_all | solution.py:294
  201.6 49.8 %collective-permute-start.7 = (bf16[1024,256]{1,0:T(8,128)(2,1)}, bf16[1024,256]{1,0:T(8,128)(2,1)}, u32[]{:S(2)}, u32[]{:S(2)}) collective-permute-start(bf16[1024,256]{1,0:T(8,128)(2,1)} %get-tuple-element.28), channel_id=1, source_target_pairs={{0,256},{32,288},{64,320},{96,352},{128,384},{160,416},{192,448},{... | collective-permute-start | bytes 1572872 | tf_op jit(solution)/shard_map/ppermute | solution.py:263
  203.5 59.0 %collective-permute-start.8 = (bf16[1024,256]{1,0:T(8,128)(2,1)}, bf16[1024,256]{1,0:T(8,128)(2,1)S(1)}, u32[]{:S(2)}, u32[]{:S(2)}) collective-permute-start(bf16[1024,256]{1,0:T(8,128)(2,1)} %get-tuple-element.30), channel_id=1, source_target_pairs={{0,256},{32,288},{64,320},{96,352},{128,384},{160,416},{192,448},{... | collective-permute-start | bytes 1572872 | tf_op jit(solution)/shard_map/ppermute | solution.py:264
  210.8 63.0 %collective-permute-start.9 = (bf16[256,1024]{1,0:T(8,128)(2,1)}, bf16[256,1024]{1,0:T(8,128)(2,1)S(1)}, u32[]{:S(2)}, u32[]{:S(2)}) collective-permute-start(bf16[256,1024]{1,0:T(8,128)(2,1)} %get-tuple-element.32), channel_id=1, source_target_pairs={{0,256},{32,288},{64,320},{96,352},{128,384},{160,416},{192,448},{... | collective-permute-start | bytes 1572872 | tf_op jit(solution)/shard_map/ppermute | solution.py:262
  212.7 7.7 %collective-permute-start.6 = (f32[16,8,128]{2,1,0:T(8,128)S(1)}, f32[16,8,128]{2,1,0:T(8,128)S(1)}, u32[]{:S(2)}, u32[]{:S(2)}) collective-permute-start(f32[16,8,128]{2,1,0:T(8,128)S(1)} %all-to-all-done.3.own_ref), channel_id=1, source_target_pairs={{0,1},{1,0},{2,3},{3,2},{4,5},{5,4},{6,7},{7,6},{8,9},{9,8},{10,11... | collective-permute-start | bytes 196616 | tf_op jit(solution)/shard_map/ppermute | solution.py:276
  220.4 42.1 %copy-start.5 = (f32[1024,256]{1,0:T(8,128)S(1)}, f32[1024,256]{1,0:T(8,128)}, u32[]{:S(2)}) copy-start(f32[1024,256]{1,0:T(8,128)} %get-tuple-element.29) | copy-start | bytes 3145732
  220.4 0.6 copy-start.9
  251.4 22.4 %copy-start.4 = (f32[256,1024]{1,0:T(8,128)S(1)}, f32[256,1024]{1,0:T(8,128)}, u32[]{:S(2)}) copy-start(f32[256,1024]{1,0:T(8,128)} %get-tuple-element.31) | copy-start | bytes 3145732
  274.7 1.0 copy-start.3

commit v2 on v1

v2 whole, which is shorter than its diff:
```python
import jax
import jax.numpy as jnp
from jax import lax
from jax.experimental import pallas as pl
from jax.experimental.pallas import tpu as pltpu
from jax.sharding import PartitionSpec as P


BF = jnp.bfloat16
F32 = jnp.float32
VM = pl.BlockSpec(memory_space=pltpu.VMEM)


def dot(a, b, ca, cb):
    return lax.dot_general(a, b, (((ca,), (cb,)), ((), ())), preferred_element_type=F32)


def call(body, outs, args, in_specs, out_specs, scratch=(), flops=0):
    moved = sum(a.size * a.dtype.itemsize for a in (*args, *outs))
    return pl.pallas_call(
        body,
        out_shape=tuple(outs),
        in_specs=in_specs,
        out_specs=tuple(out_specs),
        scratch_shapes=scratch,
        cost_estimate=pl.CostEstimate(flops=flops, bytes_accessed=moved, transcendentals=0),
    )(*args)


def shape(dims, kind):
    return jax.ShapeDtypeStruct(dims, kind)


def slot_choice(count_row, slots, rows):
    experts = count_row.shape[1]
    total = experts * slots
    owner = lax.broadcasted_iota(jnp.int32, (total, experts), 0) // slots
    expert = lax.broadcasted_iota(jnp.int32, (total, experts), 1)
    count = jnp.sum(jnp.where(expert == owner, count_row, 0), axis=1, keepdims=True)
    start = jnp.sum(jnp.where(expert < owner, count_row, 0), axis=1, keepdims=True)
    place = lax.broadcasted_iota(jnp.int32, (total, 1), 0) % slots
    target = jnp.where(place < count, start + place, -1)
    return lax.broadcasted_iota(jnp.int32, (total, rows), 1) == target


def pack_body(counts_ref, values_ref, out_ref):
    dirs, rows, width = values_ref.shape
    experts, _, slots, _ = out_ref.shape
    for d in range(dirs):
        mask = slot_choice(counts_ref[d : d + 1, :], slots, rows)
        packed = dot(mask.astype(BF), values_ref[d], 1, 0).astype(BF)
        out_ref[:, d] = packed.reshape(experts, slots, width)


def pack_scaled_body(counts_ref, probs_ref, values_ref, out_ref):
    dirs, rows, width = values_ref.shape
    experts, _, slots, _ = out_ref.shape
    for d in range(dirs):
        mask = slot_choice(counts_ref[d : d + 1, :], slots, rows)
        weight = jnp.where(mask, probs_ref[d : d + 1, :].astype(F32), 0.0).astype(BF)
        packed = dot(weight, values_ref[d], 1, 0).astype(BF)
        out_ref[:, d] = packed.reshape(experts, slots, width)


def unpack_body(counts_ref, slots_ref, out_ref):
    experts, dirs, slots, width = slots_ref.shape
    rows = out_ref.shape[1]
    for d in range(dirs):
        mask = slot_choice(counts_ref[d : d + 1, :], slots, rows)
        filled = slots_ref[:, d].reshape(experts * slots, width)
        out_ref[d] = dot(mask.astype(BF), filled, 0, 0).astype(BF)


def unpack_prob_body(counts_ref, probs_ref, own_ref, other_ref, out_ref):
    dirs, rows = out_ref.shape
    experts = own_ref.shape[0]
    total = own_ref[:, 0, :] + other_ref[:, 0, :]
    slots = 2 * rows // experts
    row = lax.broadcasted_iota(jnp.int32, (slots, rows), 1)
    place = lax.broadcasted_iota(jnp.int32, (slots, rows), 0)
    for d in range(dirs):
        found = jnp.zeros((slots, rows), F32)
        start = jnp.zeros((1, 1), jnp.int32)
        for e in range(experts):
            count = counts_ref[d : d + 1, e : e + 1]
            here = (row - start == place) & (place < count)
            values = total[e : e + 1, d * slots : (d + 1) * slots].reshape(slots, 1)
            found = jnp.where(here, values, found)
            start = start + count
        summed = jnp.sum(found, axis=0, keepdims=True)
        out_ref[d : d + 1, :] = (summed / probs_ref[d : d + 1, :].astype(F32)).astype(BF)


def keeps_low():
    half = lax.axis_index("pipe") // (lax.axis_size("pipe") // 2)
    group = (lax.axis_index("tensor") + lax.axis_index("expert")) % 2
    return half == group


def sides(own_ref, other_ref):
    blocks, _, rows, width = own_ref.shape

    def rows_of(ref, side):
        return ref[:, side].reshape(blocks * rows, width)

    return (
        jnp.concatenate([rows_of(own_ref, 0), rows_of(other_ref, 1)], axis=0),
        jnp.concatenate([rows_of(other_ref, 0), rows_of(own_ref, 1)], axis=0),
    )


def weight_sides(same, own_ref, other_ref):
    own, other = (own_ref[...], other_ref[...])
    return (jnp.where(same, own, other), jnp.where(same, other, own))


def hidden_body(own, other, wg, wgo, wu, wuo, act_ref, act_t_ref, silu_ref, slope_ref, send_ref, keep_ref):
    same = keeps_low()
    xa, xb = sides(own, other)
    wga, wgb = weight_sides(same, wg, wgo)
    wua, wub = weight_sides(same, wu, wuo)
    gate = dot(xa, wga, 1, 0) + dot(xb, wgb, 1, 0)
    up = dot(xa, wua, 1, 0) + dot(xb, wub, 1, 0)
    sigma = jax.nn.sigmoid(gate)
    silu = gate * sigma
    act = (silu * up).astype(BF)
    act_ref[...] = act
    act_t_ref[...] = act.T
    silu_ref[...] = silu
    slope_ref[...] = up * (sigma * (1.0 + gate * (1.0 - sigma)))
    send_ref[...] = jnp.where(same, xb, xa).T
    keep_ref[...] = jnp.where(same, xa, xb).T


def slope_body(own, other, wd, wdo, act, act_t, silu, slope, d_ref, prob_ref, down_ref):
    same = keeps_low()
    ga, gb = sides(own, other)
    wda, wdb = weight_sides(same, wd, wdo)
    down_ref[...] = dot(act_t[...], jnp.where(same, gb, ga), 1, 0).astype(BF)
    back = dot(ga, wda, 1, 1) + dot(gb, wdb, 1, 1)
    hidden = back.shape[1]
    d_ref[:, 0:hidden] = (back * slope[...]).astype(BF)
    d_ref[:, hidden : 2 * hidden] = (back * silu[...]).astype(BF)
    term = act[...].astype(F32) * back
    high = term.astype(BF)
    low = (term - high.astype(F32)).astype(BF)
    ones = jnp.ones((8, hidden), BF)
    prob = dot(ones, high, 1, 1) + dot(ones, low, 1, 1)
    blocks = prob_ref.shape[0]
    width = prob.shape[1] // blocks
    prob_ref[...] = jnp.zeros_like(prob_ref)
    for i in range(blocks):
        side, z = divmod(i, blocks // 2)
        prob_ref[2 * z + side, :, 0:width] = prob[:, i * width : (i + 1) * width]


def row_terms(d, wg, wgo, wu, wuo, out_ref, swapped):
    wga, wgb = weight_sides(keeps_low(), wg, wgo)
    wua, wub = weight_sides(keeps_low(), wu, wuo)
    blocks, _, rows, width = out_ref.shape
    half = blocks * rows
    hidden = wga.shape[1]
    for side in range(2):
        first = side == (1 if swapped else 0)
        part = pl.ds(side * half, half)
        term = dot(d[part, 0:hidden], wga if first else wgb, 1, 1)
        term = term + dot(d[part, hidden : 2 * hidden], wua if first else wub, 1, 1)
        out_ref[:, side] = term.astype(out_ref.dtype).reshape(blocks, rows, width)


def row_send_body(d, wg, wgo, wu, wuo, out_ref):
    row_terms(d, wg, wgo, wu, wuo, out_ref, True)


def grad_send_body(x_t, d, out_ref):
    both = dot(x_t[...], d[...], 1, 0).astype(BF)
    hidden = out_ref.shape[2]
    out_ref[0] = both[:, :hidden]
    out_ref[1] = both[:, hidden:]


def keep_body(own, other, x_t, act_t, d, wg, wgo, wu, wuo, row_ref, grad_ref, down_ref):
    row_terms(d, wg, wgo, wu, wuo, row_ref, False)
    ga, gb = sides(own, other)
    both = dot(x_t[...], d[...], 1, 0)
    hidden = grad_ref.shape[2]
    grad_ref[0] = both[:, :hidden]
    grad_ref[1] = both[:, hidden:]
    down_ref[...] = dot(act_t[...], jnp.where(keeps_low(), ga, gb), 1, 0)


def dispatch(array):
    experts = lax.axis_size("expert")
    groups = [[2 * e + (e + g) % 2 for e in range(experts)] for g in range(2)]
    return lax.all_to_all(
        array, ("expert", "tensor"), 0, 0, axis_index_groups=groups, tiled=True
    )


def settle(keep, arrived):
    return (keep + arrived.astype(F32)).astype(BF)[None, None]


def on_device(acts, out_grad, probs, counts, w_gate, w_up, w_down):
    experts = lax.axis_size("expert")
    pipes = lax.axis_size("pipe")
    dirs, rows, width = acts.shape[1:]
    slots = 2 * rows // experts
    total = dirs * experts * slots
    hidden = w_gate.shape[3]
    wg, wu, wd = (w_gate[0, 0], w_up[0, 0], w_down[0, 0])
    count_rows = counts[0, :, 0, :]
    packed = shape((experts, dirs, slots, width), BF)
    sided = shape((experts // 2, 2, dirs * slots, width), BF)
    work = 2 * dirs * experts * slots * rows * width
    one = 2 * total * width * hidden

    def mirror(array):
        return lax.ppermute(array, "pipe", [(i, (i + pipes // 2) % pipes) for i in range(pipes)])

    def swap(array):
        return lax.ppermute(array, "tensor", [(0, 1), (1, 0)])

    def kernel(body, outs, args, flops):
        return call(body, outs, args, [VM] * len(args), [VM] * len(outs), (), flops)

    (x_send,) = kernel(pack_body, [packed], (count_rows, acts[0]), work)
    x_own = dispatch(x_send).reshape(sided.shape)
    wgo = mirror(wg)
    (g_send,) = kernel(pack_scaled_body, [packed], (count_rows, probs[0], out_grad[0]), work)
    g_own = dispatch(g_send).reshape(sided.shape)
    wuo = mirror(wu)
    wdo = mirror(wd)
    x_other = swap(x_own)
    g_other = swap(g_own)
    act, act_t, silu, slope, x_send_t, x_keep_t = kernel(
        hidden_body,
        [
            shape((total, hidden), BF),
            shape((hidden, total), BF),
            shape((total, hidden), F32),
            shape((total, hidden), F32),
            shape((width, total), BF),
            shape((width, total), BF),
        ],
        (x_own, x_other, wg, wgo, wu, wuo),
        4 * one,
    )
    d, prob, down_send = kernel(
        slope_body,
        [shape((total, 2 * hidden), BF), shape((experts, 8, 128), F32), shape((hidden, width), BF)],
        (g_own, g_other, wd, wdo, act, act_t, silu, slope),
        3 * one,
    )
    down_got = mirror(down_send)
    (row_send,) = kernel(row_send_body, [sided], (d, wg, wgo, wu, wuo), 2 * one)
    row_got = swap(row_send)
    (grad_send,) = kernel(grad_send_body, [shape((2, width, hidden), BF)], (x_send_t, d), 2 * one)
    grad_got = mirror(grad_send)
    prob_own = dispatch(prob)
    row_keep, grad_keep, down_keep = kernel(
        keep_body,
        [shape(sided.shape, F32), shape((2, width, hidden), F32), shape((hidden, width), F32)],
        (g_own, g_other, x_keep_t, act_t, d, wg, wgo, wu, wuo),
        5 * one,
    )
    prob_other = swap(prob_own)
    row_sum = (row_keep + row_got.astype(F32)).astype(BF).reshape(packed.shape)
    row_back = dispatch(row_sum)
    (prob_grad,) = kernel(
        unpack_prob_body, [shape((dirs, rows), BF)], (count_rows, probs[0], prob_own, prob_other), 0
    )
    (act_grad,) = kernel(
        unpack_body, [shape((dirs, rows, width), BF)], (count_rows, row_back), work
    )
    return (
        act_grad[None],
        prob_grad[None],
        settle(grad_keep[0], grad_got[0]),
        settle(grad_keep[1], grad_got[1]),
        settle(down_keep, down_got),
    )


def solution(mesh):
    return jax.shard_map(
        on_device,
        mesh=mesh,
        in_specs=(
            P("pipe", None, "expert", "tensor"),
            P("pipe", None, "expert", "tensor"),
            P("pipe", None, "expert"),
            P("pipe", None, "expert", None),
            P("pipe", "expert", None, "tensor"),
            P("pipe", "expert", None, "tensor"),
            P("pipe", "expert", "tensor", None),
        ),
        out_specs=(
            P("pipe", None, "expert", "tensor"),
            P("pipe", None, "expert"),
            P("pipe", "expert", None, "tensor"),
            P("pipe", "expert", None, "tensor"),
            P("pipe", "expert", "tensor", None),
        ),
        check_vma=False,
    )
```

time: 279 us -> 280 us (level)
  the two profiles are of different devices: /device:TPU:47 before, /device:TPU:45 now
where the time goes in v2:
time: 280 us; the launch traced here: 279 us
  waiting for transfers between devices  156 us (56%)
  starting transfers between devices  79.8 us (28%)
  Pallas kernels  32.1 us (11%)
  other arithmetic  7.66 us (3%)
    ppermute x5, waiting for transfers between devices, mirror(): lax.ppermute(array, 'pipe', [(i, (i + pipes // 2) % pipes) for i in range...  110 us
    all_to_all x4, starting transfers between devices, dispatch(): lax.all_to_all(array, ('expert', 'tensor'), 0, 0, axis_index_groups=group...  42.8 us
    all_to_all x4, waiting for transfers between devices, dispatch(): lax.all_to_all(array, ('expert', 'tensor'), 0, 0, axis_index_groups=group...  39.9 us
    pallas_call x9, Pallas kernels, call(): pl.pallas_call(body, out_shape=tuple(outs), in_specs=in_specs, out_specs=...  32.1 us
    ppermute x5, starting transfers between devices, mirror(): lax.ppermute(array, 'pipe', [(i, (i + pipes // 2) % pipes) for i in range...  21 us
    ppermute x4, starting transfers between devices, swap(): return lax.ppermute(array, 'tensor', [(0, 1), (1, 0)])  15.9 us
    ppermute x4, waiting for transfers between devices, swap(): return lax.ppermute(array, 'tensor', [(0, 1), (1, 0)])  6.3 us
  transfers between devices with their start and end apart: 13, of which 8 were waited for; matrix products, arithmetic and copies ran while one was open for 3% of the time, Pallas kernels for 7%

profile of v2, /device:TPU:45, one launch (start us, length us, event | category | flops | bytes accessed | tf_op | source)
XLA Modules:
  0.0 278.6 jit_solution(16488117660056988222)
XLA Ops:
  3.2 11.2 %all-to-all-start.1 = ((bf16[16,2,16,1024]{3,2,1,0:T(8,128)(2,1)}), bf16[16,2,16,1024]{3,2,1,0:T(8,128)(2,1)}, u32[]{:S(2)}, u32[]{:S(2)}) async-start(bf16[16,2,16,1024]{3,2,1,0:T(8,128)(2,1)} %shard_map.111), calls=%async_computation.1 | async-start | bytes 2097152 | tf_op jit(solution)/shard_map/all_to_all | solution.py:195
  17.2 21.7 %all-to-all-done.1 = bf16[16,2,16,1024]{3,2,1,0:T(8,128)(2,1)} async-done(((bf16[16,2,16,1024]{3,2,1,0:T(8,128)(2,1)}), bf16[16,2,16,1024]{3,2,1,0:T(8,128)(2,1)}, u32[]{:S(2)}, u32[]{:S(2)}) %all-to-all-start.1) | async-done | bytes 1048608 | tf_op jit(solution)/shard_map/all_to_all | solution.py:195
  38.9 7.4 %all-to-all-start = ((bf16[16,2,16,1024]{3,2,1,0:T(8,128)(2,1)}), bf16[16,2,16,1024]{3,2,1,0:T(8,128)(2,1)S(1)}, u32[]{:S(2)}, u32[]{:S(2)}) async-start(bf16[16,2,16,1024]{3,2,1,0:T(8,128)(2,1)} %shard_map.110), calls=%async_computation | async-start | bytes 2097152 | tf_op jit(solution)/shard_map/all_to_all | solution.py:195
  46.2 5.2 %collective-permute-start.1 = (bf16[8,2,32,1024]{3,2,1,0:T(8,128)(2,1)}, bf16[8,2,32,1024]{3,2,1,0:T(8,128)(2,1)}, u32[]{:S(2)}, u32[]{:S(2)}) collective-permute-start(bf16[8,2,32,1024]{3,2,1,0:T(8,128)(2,1)} %bitcast.5.own), channel_id=1, source_target_pairs={{0,1},{1,0},{2,3},{3,2},{4,5},{5,4},{6,7},{7,6},{8,9},{9,8},{10,11... | collective-permute-start | bytes 3145736 | tf_op jit(solution)/shard_map/ppermute | solution.py:222
  51.5 18.2 %all-to-all-done = bf16[16,2,16,1024]{3,2,1,0:T(8,128)(2,1)S(1)} async-done(((bf16[16,2,16,1024]{3,2,1,0:T(8,128)(2,1)}), bf16[16,2,16,1024]{3,2,1,0:T(8,128)(2,1)S(1)}, u32[]{:S(2)}, u32[]{:S(2)}) %all-to-all-start) | async-done | bytes 1048608 | tf_op jit(solution)/shard_map/all_to_all | solution.py:195
  69.6 5.2 %collective-permute-start = (bf16[8,2,32,1024]{3,2,1,0:T(8,128)(2,1)S(1)}, bf16[8,2,32,1024]{3,2,1,0:T(8,128)(2,1)}, u32[]{:S(2)}, u32[]{:S(2)}) collective-permute-start(bf16[8,2,32,1024]{3,2,1,0:T(8,128)(2,1)S(1)} %bitcast.18), channel_id=1, source_target_pairs={{0,1},{1,0},{2,3},{3,2},{4,5},{5,4},{6,7},{7,6},{8,9},{9,8},{10,11... | collective-permute-start | bytes 3145736 | tf_op jit(solution)/shard_map/ppermute | solution.py:222
  77.5 6.6 %collective-permute-start.3 = (bf16[1024,256]{1,0:T(8,128)(2,1)S(1)}, bf16[1024,256]{1,0:T(8,128)(2,1)S(1)}, u32[]{:S(2)}, u32[]{:S(2)}) collective-permute-start(bf16[1024,256]{1,0:T(8,128)(2,1)S(1)} %bitcast.28), channel_id=1, source_target_pairs={{0,256},{32,288},{64,320},{96,352},{128,384},{160,416},{192,448},{... | collective-permute-start | bytes 1572872 | tf_op jit(solution)/shard_map/ppermute | solution.py:219
  86.7 12.9 %collective-permute-done.2.wgo = bf16[1024,256]{1,0:T(8,128)(2,1)S(1)} collective-permute-done((bf16[1024,256]{1,0:T(8,128)(2,1)S(1)}, bf16[1024,256]{1,0:T(8,128)(2,1)S(1)}, u32[]{:S(2)}, u32[]{:S(2)}) %collective-permute-start.2) | collective-permute-done | bytes 524320 | tf_op jit(solution)/shard_map/ppermute | solution.py:219
  99.6 24.0 %collective-permute-done.3.wuo = bf16[1024,256]{1,0:T(8,128)(2,1)S(1)} collective-permute-done((bf16[1024,256]{1,0:T(8,128)(2,1)S(1)}, bf16[1024,256]{1,0:T(8,128)(2,1)S(1)}, u32[]{:S(2)}, u32[]{:S(2)}) %collective-permute-start.3) | collective-permute-done | bytes 524320 | tf_op jit(solution)/shard_map/ppermute | solution.py:219
  124.5 5.4 %shard_map.112 = (bf16[512,256]{1,0:T(8,128)(2,1)}, bf16[256,512]{1,0:T(8,128)(2,1)}, f32[512,256]{1,0:T(8,128)}, f32[512,256]{1,0:T(8,128)}, bf16[1024,512]{1,0:T(8,128)(2,1)}, /*index=5*/bf16[1024,512]{1,0:T(8,128)(2,1)}) custom-call(bf16[8,2,32,1024]{3,2,1,0:T(8,128)(2,1)} %bitcast.5.own, bf16[8,2,32,1024]{3,2,1,0:T(8,128)(2,1)} %collective-permute-done.1.other, ...), custom_call_target="tpu_custom_call" | custom-call | flops 1073741824 | bytes 7864320 | tf_op jit(solution)/shard_map/pallas_call | solution.py:20
  129.9 17.9 %collective-permute-done.4.wdo = bf16[256,1024]{1,0:T(8,128)(2,1)} collective-permute-done((bf16[256,1024]{1,0:T(8,128)(2,1)}, bf16[256,1024]{1,0:T(8,128)(2,1)}, u32[]{:S(2)}, u32[]{:S(2)}) %collective-permute-start.4) | collective-permute-done | bytes 524320 | tf_op jit(solution)/shard_map/ppermute | solution.py:219
  147.8 4.6 %shard_map.113 = (bf16[512,512]{1,0:T(8,128)(2,1)}, f32[16,8,128]{2,1,0:T(8,128)}, bf16[256,1024]{1,0:T(8,128)(2,1)}) custom-call(bf16[8,2,32,1024]{3,2,1,0:T(8,128)(2,1)} %bitcast.19, bf16[8,2,32,1024]{3,2,1,0:T(8,128)(2,1)} %collective-permute-done.other, bf16[256,1024]{1,0:T(8,128)(2,1)} %bitcast.31, bf16[256,1024]{1,0:T(8,128)(2,1)} %collective-permute-done.4.wdo, ...), custom_call_target="tpu_custom_call" | custom-call | flops 805306368 | bytes 5832704 | tf_op jit(solution)/shard_map/pallas_call | solution.py:20
  152.4 3.4 %shard_map.115 = bf16[8,2,32,1024]{3,2,1,0:T(8,128)(2,1)} custom-call(bf16[512,512]{1,0:T(8,128)(2,1)} %get-tuple-element.22.d, bf16[1024,256]{1,0:T(8,128)(2,1)} %bitcast.22, bf16[1024,256]{1,0:T(8,128)(2,1)} %copy-done.3, bf16[1024,256]{1,0:T(8,128)(2,1)} %bitcast.26, bf16[1024,256]{1,0:T(8,128)(2,1)} %copy-done.4), custom_call_target="tpu_custom_call" | custom-call | flops 536870912 | bytes 3670016 | tf_op jit(solution)/shard_map/pallas_call | solution.py:20
  158.1 11.0 %all-to-all-start.3 = ((f32[16,8,128]{2,1,0:T(8,128)}), f32[16,8,128]{2,1,0:T(8,128)S(1)}, u32[]{:S(2)}, u32[]{:S(2)}) async-start(f32[16,8,128]{2,1,0:T(8,128)} %get-tuple-element.24), calls=%async_computation.3 | async-start | bytes 131072 | tf_op jit(solution)/shard_map/all_to_all | solution.py:195
  169.1 5.8 %shard_map.114 = (f32[8,2,32,1024]{3,2,1,0:T(8,128)}, f32[2,1024,256]{2,1,0:T(8,128)}, f32[256,1024]{1,0:T(8,128)}) custom-call(bf16[8,2,32,1024]{3,2,1,0:T(8,128)(2,1)} %bitcast.20, bf16[8,2,32,1024]{3,2,1,0:T(8,128)(2,1)} %collective-permute-done.other, bf16[1024,512]{1,0:T(8,128)(2,1)} %get-tuple-element.17.x_t, ...), custom_call_target="tpu_custom_call" | custom-call | flops 1342177280 | bytes 11272192 | tf_op jit(solution)/shard_map/pallas_call | solution.py:20
  174.9 4.2 %collective-permute-done.5 = bf16[8,2,32,1024]{3,2,1,0:T(8,128)(2,1)S(1)} collective-permute-done((bf16[8,2,32,1024]{3,2,1,0:T(8,128)(2,1)}, bf16[8,2,32,1024]{3,2,1,0:T(8,128)(2,1)S(1)}, u32[]{:S(2)}, u32[]{:S(2)}) %collective-permute-start.5) | collective-permute-done | bytes 1048608 | tf_op jit(solution)/shard_map/ppermute | solution.py:222
  179.2 2.9 %add_convert_fusion = bf16[8,2,32,1024]{3,2,1,0:T(8,128)(2,1)} fusion(f32[8,2,32,1024]{3,2,1,0:T(8,128)} %get-tuple-element.23, bf16[8,2,32,1024]{3,2,1,0:T(8,128)(2,1)S(1)} %collective-permute-done.5), kind=kLoop, calls=%fused_computation | loop fusion | flops 1572864 | bytes 4194304 | tf_op jit(solution)/shard_map/convert_element_type | solution.py:268
  182.1 13.2 %all-to-all-start.2 = ((bf16[16,2,16,1024]{3,2,1,0:T(8,128)(2,1)}), bf16[16,2,16,1024]{3,2,1,0:T(8,128)(2,1)S(1)}, u32[]{:S(2)}, u32[]{:S(2)}) async-start(bf16[16,2,16,1024]{3,2,1,0:T(8,128)(2,1)} %bitcast.9), calls=%async_computation.2 | async-start | bytes 2097152 | tf_op jit(solution)/shard_map/all_to_all | solution.py:195
  195.3 3.0 %shard_map.118 = bf16[2,1024,256]{2,1,0:T(8,128)(2,1)} custom-call(bf16[1024,512]{1,0:T(8,128)(2,1)} %get-tuple-element.26.x_t, bf16[512,512]{1,0:T(8,128)(2,1)} %get-tuple-element.22.d), custom_call_target="tpu_custom_call" | custom-call | flops 536870912 | bytes 2621440 | tf_op jit(solution)/shard_map/pallas_call | solution.py:20
  200.2 7.3 %collective-permute-start.8 = (bf16[256,1024]{1,0:T(8,128)(2,1)}, bf16[256,1024]{1,0:T(8,128)(2,1)}, u32[]{:S(2)}, u32[]{:S(2)}) collective-permute-start(bf16[256,1024]{1,0:T(8,128)(2,1)} %get-tuple-element.28), channel_id=1, source_target_pairs={{0,256},{32,288},{64,320},{96,352},{128,384},{160,416},{192,448},{... | collective-permute-start | bytes 1572872 | tf_op jit(solution)/shard_map/ppermute | solution.py:219
  207.5 3.3 %collective-permute-start.6 = (f32[16,8,128]{2,1,0:T(8,128)S(1)}, f32[16,8,128]{2,1,0:T(8,128)S(1)}, u32[]{:S(2)}, u32[]{:S(2)}) collective-permute-start(f32[16,8,128]{2,1,0:T(8,128)S(1)} %all-to-all-done.3.own_ref), channel_id=1, source_target_pairs={{0,1},{1,0},{2,3},{3,2},{4,5},{5,4},{6,7},{7,6},{8,9},{9,8},{10,11... | collective-permute-start | bytes 196616 | tf_op jit(solution)/shard_map/ppermute | solution.py:222
  215.1 55.0 %collective-permute-done.8 = bf16[256,1024]{1,0:T(8,128)(2,1)} collective-permute-done((bf16[256,1024]{1,0:T(8,128)(2,1)}, bf16[256,1024]{1,0:T(8,128)(2,1)}, u32[]{:S(2)}, u32[]{:S(2)}) %collective-permute-start.8) | collective-permute-done | bytes 524320 | tf_op jit(solution)/shard_map/ppermute | solution.py:219
  272.1 2.8 fusion.1
  275.8 2.8 %shard_map.116 = bf16[2,128,1024]{2,1,0:T(8,128)(2,1)} custom-call(s32[2,16]{1,0:T(2,128)} %bitcast.37, bf16[16,2,16,1024]{3,2,1,0:T(8,128)(2,1)} %copy-done.5), custom_call_target="tpu_custom_call" | custom-call | flops 134217728 | bytes 1572992 | tf_op jit(solution)/shard_map/pallas_call | solution.py:20
  (32 shorter events, 22.8 us)
Async XLA Ops:
  3.2 35.6 %all-to-all-start.1 = ((bf16[16,2,16,1024]{3,2,1,0:T(8,128)(2,1)}), bf16[16,2,16,1024]{3,2,1,0:T(8,128)(2,1)}, u32[]{:S(2)}, u32[]{:S(2)}) async-start(bf16[16,2,16,1024]{3,2,1,0:T(8,128)(2,1)} %shard_map.111), calls=%async_computation.1 | async-start | bytes 2097152 | tf_op jit(solution)/shard_map/all_to_all | solution.py:195
  14.4 60.4 %copy-start.1 = (bf16[1,1,1024,256]{3,2,1,0:T(8,128)(2,1)S(1)}, bf16[1,1,1024,256]{3,2,1,0:T(8,128)(2,1)}, u32[]{:S(2)}) copy-start(bf16[1,1,1024,256]{3,2,1,0:T(8,128)(2,1)} %param.11) | copy-start | bytes 1572868
  14.5 63.1 %copy-start.2 = (bf16[1,1,1024,256]{3,2,1,0:T(8,128)(2,1)S(1)}, bf16[1,1,1024,256]{3,2,1,0:T(8,128)(2,1)}, u32[]{:S(2)}) copy-start(bf16[1,1,1024,256]{3,2,1,0:T(8,128)(2,1)} %param.12) | copy-start | bytes 1572868
  38.9 30.8 %all-to-all-start = ((bf16[16,2,16,1024]{3,2,1,0:T(8,128)(2,1)}), bf16[16,2,16,1024]{3,2,1,0:T(8,128)(2,1)S(1)}, u32[]{:S(2)}, u32[]{:S(2)}) async-start(bf16[16,2,16,1024]{3,2,1,0:T(8,128)(2,1)} %shard_map.110), calls=%async_computation | async-start | bytes 2097152 | tf_op jit(solution)/shard_map/all_to_all | solution.py:195
  46.2 77.5 %collective-permute-start.1 = (bf16[8,2,32,1024]{3,2,1,0:T(8,128)(2,1)}, bf16[8,2,32,1024]{3,2,1,0:T(8,128)(2,1)}, u32[]{:S(2)}, u32[]{:S(2)}) collective-permute-start(bf16[8,2,32,1024]{3,2,1,0:T(8,128)(2,1)} %bitcast.5.own), channel_id=1, source_target_pairs={{0,1},{1,0},{2,3},{3,2},{4,5},{5,4},{6,7},{7,6},{8,9},{9,8},{10,11... | collective-permute-start | bytes 3145736 | tf_op jit(solution)/shard_map/ppermute | solution.py:222
  69.6 60.3 %copy-start = (bf16[16,2,16,1024]{3,2,1,0:T(8,128)(2,1)}, bf16[16,2,16,1024]{3,2,1,0:T(8,128)(2,1)S(1)}, u32[]{:S(2)}) copy-start(bf16[16,2,16,1024]{3,2,1,0:T(8,128)(2,1)S(1)} %all-to-all-done) | copy-start | bytes 3145732
  69.6 78.2 %collective-permute-start = (bf16[8,2,32,1024]{3,2,1,0:T(8,128)(2,1)S(1)}, bf16[8,2,32,1024]{3,2,1,0:T(8,128)(2,1)}, u32[]{:S(2)}, u32[]{:S(2)}) collective-permute-start(bf16[8,2,32,1024]{3,2,1,0:T(8,128)(2,1)S(1)} %bitcast.18), channel_id=1, source_target_pairs={{0,1},{1,0},{2,3},{3,2},{4,5},{5,4},{6,7},{7,6},{8,9},{9,8},{10,11... | collective-permute-start | bytes 3145736 | tf_op jit(solution)/shard_map/ppermute | solution.py:222
  74.9 24.7 %collective-permute-start.2 = (bf16[1024,256]{1,0:T(8,128)(2,1)S(1)}, bf16[1024,256]{1,0:T(8,128)(2,1)S(1)}, u32[]{:S(2)}, u32[]{:S(2)}) collective-permute-start(bf16[1024,256]{1,0:T(8,128)(2,1)S(1)} %bitcast.24), channel_id=1, source_target_pairs={{0,256},{32,288},{64,320},{96,352},{128,384},{160,416},{192,448},{... | collective-permute-start | bytes 1572872 | tf_op jit(solution)/shard_map/ppermute | solution.py:219
  77.5 46.1 %collective-permute-start.3 = (bf16[1024,256]{1,0:T(8,128)(2,1)S(1)}, bf16[1024,256]{1,0:T(8,128)(2,1)S(1)}, u32[]{:S(2)}, u32[]{:S(2)}) collective-permute-start(bf16[1024,256]{1,0:T(8,128)(2,1)S(1)} %bitcast.28), channel_id=1, source_target_pairs={{0,256},{32,288},{64,320},{96,352},{128,384},{160,416},{192,448},{... | collective-permute-start | bytes 1572872 | tf_op jit(solution)/shard_map/ppermute | solution.py:219
  84.1 63.7 %collective-permute-start.4 = (bf16[256,1024]{1,0:T(8,128)(2,1)}, bf16[256,1024]{1,0:T(8,128)(2,1)}, u32[]{:S(2)}, u32[]{:S(2)}) collective-permute-start(bf16[256,1024]{1,0:T(8,128)(2,1)} %bitcast.30), channel_id=1, source_target_pairs={{0,256},{32,288},{64,320},{96,352},{128,384},{160,416},{192,448},{... | collective-permute-start | bytes 1572872 | tf_op jit(solution)/shard_map/ppermute | solution.py:219
  99.6 24.1 %copy-start.3 = (bf16[1024,256]{1,0:T(8,128)(2,1)}, bf16[1024,256]{1,0:T(8,128)(2,1)S(1)}, u32[]{:S(2)}) copy-start(bf16[1024,256]{1,0:T(8,128)(2,1)S(1)} %collective-permute-done.2.wgo) | copy-start | bytes 1572868
  123.7 0.8 copy-start.4
  155.8 23.3 %collective-permute-start.5 = (bf16[8,2,32,1024]{3,2,1,0:T(8,128)(2,1)}, bf16[8,2,32,1024]{3,2,1,0:T(8,128)(2,1)S(1)}, u32[]{:S(2)}, u32[]{:S(2)}) collective-permute-start(bf16[8,2,32,1024]{3,2,1,0:T(8,128)(2,1)} %shard_map.115), channel_id=1, source_target_pairs={{0,1},{1,0},{2,3},{3,2},{4,5},{5,4},{6,7},{7,6},{8,9},{9,8},{10,11... | collective-permute-start | bytes 3145736 | tf_op jit(solution)/shard_map/ppermute | solution.py:222
  158.1 24.0 %all-to-all-start.3 = ((f32[16,8,128]{2,1,0:T(8,128)}), f32[16,8,128]{2,1,0:T(8,128)S(1)}, u32[]{:S(2)}, u32[]{:S(2)}) async-start(f32[16,8,128]{2,1,0:T(8,128)} %get-tuple-element.24), calls=%async_computation.3 | async-start | bytes 131072 | tf_op jit(solution)/shard_map/all_to_all | solution.py:195
  182.1 25.4 %copy-start.7 = (f32[16,8,128]{2,1,0:T(8,128)}, f32[16,8,128]{2,1,0:T(8,128)S(1)}, u32[]{:S(2)}) copy-start(f32[16,8,128]{2,1,0:T(8,128)S(1)} %all-to-all-done.3.own_ref) | copy-start | bytes 196612
  182.1 88.0 %copy-start.6 = (f32[256,1024]{1,0:T(8,128)S(1)}, f32[256,1024]{1,0:T(8,128)}, u32[]{:S(2)}) copy-start(f32[256,1024]{1,0:T(8,128)} %get-tuple-element.27) | copy-start | bytes 3145732
  182.1 92.7 %all-to-all-start.2 = ((bf16[16,2,16,1024]{3,2,1,0:T(8,128)(2,1)}), bf16[16,2,16,1024]{3,2,1,0:T(8,128)(2,1)S(1)}, u32[]{:S(2)}, u32[]{:S(2)}) async-start(bf16[16,2,16,1024]{3,2,1,0:T(8,128)(2,1)} %bitcast.9), calls=%async_computation.2 | async-start | bytes 2097152 | tf_op jit(solution)/shard_map/all_to_all | solution.py:195
  198.3 73.7 %collective-permute-start.7 = (bf16[2,1024,256]{2,1,0:T(8,128)(2,1)}, bf16[2,1024,256]{2,1,0:T(8,128)(2,1)S(1)}, u32[]{:S(2)}, u32[]{:S(2)}) collective-permute-start(bf16[2,1024,256]{2,1,0:T(8,128)(2,1)} %shard_map.118), channel_id=1, source_target_pairs={{0,256},{32,288},{64,320},{96,352},{128,384},{160,416},{192,448},{... | collective-permute-start | bytes 3145736 | tf_op jit(solution)/shard_map/ppermute | solution.py:219
  200.2 69.8 %collective-permute-start.8 = (bf16[256,1024]{1,0:T(8,128)(2,1)}, bf16[256,1024]{1,0:T(8,128)(2,1)}, u32[]{:S(2)}, u32[]{:S(2)}) collective-permute-start(bf16[256,1024]{1,0:T(8,128)(2,1)} %get-tuple-element.28), channel_id=1, source_target_pairs={{0,256},{32,288},{64,320},{96,352},{128,384},{160,416},{192,448},{... | collective-permute-start | bytes 1572872 | tf_op jit(solution)/shard_map/ppermute | solution.py:219
  207.5 5.3 %collective-permute-start.6 = (f32[16,8,128]{2,1,0:T(8,128)S(1)}, f32[16,8,128]{2,1,0:T(8,128)S(1)}, u32[]{:S(2)}, u32[]{:S(2)}) collective-permute-start(f32[16,8,128]{2,1,0:T(8,128)S(1)} %all-to-all-done.3.own_ref), channel_id=1, source_target_pairs={{0,1},{1,0},{2,3},{3,2},{4,5},{5,4},{6,7},{7,6},{8,9},{9,8},{10,11... | collective-permute-start | bytes 196616 | tf_op jit(solution)/shard_map/ppermute | solution.py:222
  212.8 0.6 copy-start.8
  274.8 1.0 copy-start.5

commit v3 on v2

v3 whole, which is shorter than its diff:
```python
import jax
import jax.numpy as jnp
from jax import lax
from jax.experimental import pallas as pl
from jax.experimental.pallas import tpu as pltpu
from jax.sharding import PartitionSpec as P


BF = jnp.bfloat16
F32 = jnp.float32
VM = pl.BlockSpec(memory_space=pltpu.VMEM)
ANY = pl.BlockSpec(memory_space=pl.ANY)
LANES = 128


def dot(a, b, ca, cb):
    return lax.dot_general(a, b, (((ca,), (cb,)), ((), ())), preferred_element_type=F32)


def call(body, outs, args, in_specs, out_specs, scratch=(), flops=0, limit=None):
    moved = sum(a.size * a.dtype.itemsize for a in (*args, *outs))
    return pl.pallas_call(
        body,
        out_shape=tuple(outs),
        in_specs=in_specs,
        out_specs=tuple(out_specs),
        scratch_shapes=scratch,
        compiler_params=pltpu.CompilerParams(vmem_limit_bytes=limit),
        cost_estimate=pl.CostEstimate(flops=flops, bytes_accessed=moved, transcendentals=0),
    )(*args)


def shape(dims, kind):
    return jax.ShapeDtypeStruct(dims, kind)


def slot_choice(count_row, slots, rows):
    experts = count_row.shape[1]
    total = experts * slots
    owner = lax.broadcasted_iota(jnp.int32, (total, experts), 0) // slots
    expert = lax.broadcasted_iota(jnp.int32, (total, experts), 1)
    count = jnp.sum(jnp.where(expert == owner, count_row, 0), axis=1, keepdims=True)
    start = jnp.sum(jnp.where(expert < owner, count_row, 0), axis=1, keepdims=True)
    place = lax.broadcasted_iota(jnp.int32, (total, 1), 0) % slots
    target = jnp.where(place < count, start + place, -1)
    return lax.broadcasted_iota(jnp.int32, (total, rows), 1) == target


def pack_body(counts_ref, values_ref, out_ref):
    dirs, rows, width = values_ref.shape
    experts, _, slots, _ = out_ref.shape
    for d in range(dirs):
        mask = slot_choice(counts_ref[d : d + 1, :], slots, rows)
        packed = dot(mask.astype(BF), values_ref[d], 1, 0).astype(BF)
        out_ref[:, d] = packed.reshape(experts, slots, width)


def pack_scaled_body(counts_ref, probs_ref, values_ref, out_ref):
    dirs, rows, width = values_ref.shape
    experts, _, slots, _ = out_ref.shape
    for d in range(dirs):
        mask = slot_choice(counts_ref[d : d + 1, :], slots, rows)
        weight = jnp.where(mask, probs_ref[d : d + 1, :].astype(F32), 0.0).astype(BF)
        packed = dot(weight, values_ref[d], 1, 0).astype(BF)
        out_ref[:, d] = packed.reshape(experts, slots, width)


def unpack_body(counts_ref, probs_ref, filled, out_ref, prob_ref, slots_ref, sem):
    copy = pltpu.make_async_copy(filled, slots_ref, sem)
    copy.start()
    experts, slots, _ = slots_ref.shape
    dirs, rows, width = out_ref.shape
    masks = [
        slot_choice(counts_ref[d : d + 1, :], slots, rows).astype(BF) for d in range(dirs)
    ]
    copy.wait()
    terms = slots_ref[:, :, dirs * width :].reshape(experts * slots, LANES)
    for d in range(dirs):
        part = slots_ref[:, :, d * width : (d + 1) * width].reshape(experts * slots, width)
        out_ref[d] = dot(masks[d], part, 0, 0).astype(BF)
        found = dot(terms, masks[d], 0, 0)[d : d + 1, :]
        prob_ref[d : d + 1, :] = (found / probs_ref[d : d + 1, :].astype(F32)).astype(BF)


def keeps_low():
    half = lax.axis_index("pipe") // (lax.axis_size("pipe") // 2)
    group = (lax.axis_index("tensor") + lax.axis_index("expert")) % 2
    return half == group


def row_copies(own, other, low, high, sems):
    return [
        pltpu.make_async_copy(own.at[:, 0], low.at[0], sems.at[0]),
        pltpu.make_async_copy(other.at[:, 1], low.at[1], sems.at[1]),
        pltpu.make_async_copy(other.at[:, 0], high.at[0], sems.at[2]),
        pltpu.make_async_copy(own.at[:, 1], high.at[1], sems.at[3]),
    ]


def flat(ref):
    sides, blocks, rows, width = ref.shape
    return ref[...].reshape(sides * blocks * rows, width)


def weight_sides(same, own_ref, other_ref):
    own, other = (own_ref[...], other_ref[...])
    return (jnp.where(same, own, other), jnp.where(same, other, own))


def hidden_body(
    own, other, wg, wgo, wu, wuo, act_ref, act_t_ref, silu_ref, slope_ref, send_ref, keep_ref, low, high, sems
):
    copies = row_copies(own, other, low, high, sems)
    for c in copies:
        c.start()
    same = keeps_low()
    wga, wgb = weight_sides(same, wg, wgo)
    wua, wub = weight_sides(same, wu, wuo)
    for c in copies:
        c.wait()
    xa, xb = (flat(low), flat(high))
    gate = dot(xa, wga, 1, 0) + dot(xb, wgb, 1, 0)
    up = dot(xa, wua, 1, 0) + dot(xb, wub, 1, 0)
    sigma = jax.nn.sigmoid(gate)
    silu = gate * sigma
    act = (silu * up).astype(BF)
    act_ref[...] = act
    act_t_ref[...] = act.T
    silu_ref[...] = silu
    slope_ref[...] = up * (sigma * (1.0 + gate * (1.0 - sigma)))
    send_ref[...] = jnp.where(same, xb, xa).T
    keep_ref[...] = jnp.where(same, xa, xb).T


def half_copies(own, other, wanted_low, buffer, sems):
    @pl.when(wanted_low)
    def _():
        pltpu.make_async_copy(own.at[:, 0], buffer.at[0], sems.at[0]).start()
        pltpu.make_async_copy(other.at[:, 1], buffer.at[1], sems.at[1]).start()

    @pl.when(jnp.logical_not(wanted_low))
    def _():
        pltpu.make_async_copy(other.at[:, 0], buffer.at[0], sems.at[0]).start()
        pltpu.make_async_copy(own.at[:, 1], buffer.at[1], sems.at[1]).start()

    return [
        pltpu.make_async_copy(own.at[:, 0], buffer.at[0], sems.at[0]),
        pltpu.make_async_copy(own.at[:, 1], buffer.at[1], sems.at[1]),
    ]


def down_body(own, other, act_t, down_ref, half, sems):
    for c in half_copies(own, other, jnp.logical_not(keeps_low()), half, sems):
        c.wait()
    down_ref[...] = dot(act_t[...], flat(half), 1, 0).astype(BF)


def row_terms(d, gate_sides, up_sides, prob, out_ref, swapped):
    blocks, _, slots, lanes = out_ref.shape
    width = gate_sides[0].shape[0]
    dirs = lanes // width
    half = blocks * dirs * slots
    hidden = gate_sides[0].shape[1]
    lane = lax.broadcasted_iota(jnp.int32, (blocks, slots, LANES), 2)
    for side in range(2):
        use = side ^ swapped
        part = d[side * half : (side + 1) * half]
        term = dot(part[:, :hidden], gate_sides[use], 1, 1) + dot(part[:, hidden:], up_sides[use], 1, 1)
        term = term.astype(out_ref.dtype).reshape(blocks, dirs, slots, width)
        spread = jnp.broadcast_to(prob[side * half : (side + 1) * half], (half, LANES))
        spread = spread.reshape(blocks, dirs, slots, LANES)
        extra = jnp.zeros((blocks, slots, LANES), F32)
        for k in range(dirs):
            out_ref[:, side, :, k * width : (k + 1) * width] = term[:, k]
            extra = jnp.where(lane == k, spread[:, k], extra)
        out_ref[:, side, :, dirs * width :] = extra.astype(out_ref.dtype)


def slope_body(
    own, other, wd, wdo, act, silu, slope, wg, wgo, wu, wuo, d_ref, prob_ref, row_ref, low, high, sems
):
    copies = row_copies(own, other, low, high, sems)
    for c in copies:
        c.start()
    same = keeps_low()
    wda, wdb = weight_sides(same, wd, wdo)
    for c in copies:
        c.wait()
    back = dot(flat(low), wda, 1, 1) + dot(flat(high), wdb, 1, 1)
    d_gate = (back * slope[...]).astype(BF)
    d_up = (back * silu[...]).astype(BF)
    d = jnp.concatenate([d_gate, d_up], axis=1)
    d_ref[...] = d
    prob = jnp.sum(act[...].astype(F32) * back, axis=1, keepdims=True)
    prob_ref[...] = jnp.broadcast_to(prob, prob_ref.shape)
    row_terms(d, weight_sides(same, wg, wgo), weight_sides(same, wu, wuo), prob, row_ref, 1)


def grad_send_body(x_t, d, out_ref):
    both = dot(x_t[...], d[...], 1, 0).astype(BF)
    hidden = out_ref.shape[2]
    out_ref[0] = both[:, :hidden]
    out_ref[1] = both[:, hidden:]


def keep_body(
    own, other, x_t, act_t, d, prob, wg, wgo, wu, wuo, row_ref, grad_ref, down_ref, half, sems
):
    same = keeps_low()
    waits = half_copies(own, other, same, half, sems)
    row_terms(
        d[...], weight_sides(same, wg, wgo), weight_sides(same, wu, wuo), prob[:, 0:1], row_ref, 0
    )
    both = dot(x_t[...], d[...], 1, 0)
    hidden = grad_ref.shape[2]
    grad_ref[0] = both[:, :hidden]
    grad_ref[1] = both[:, hidden:]
    for c in waits:
        c.wait()
    down_ref[...] = dot(act_t[...], flat(half), 1, 0)


def dispatch(array):
    experts = lax.axis_size("expert")
    groups = [[2 * e + (e + g) % 2 for e in range(experts)] for g in range(2)]
    return lax.all_to_all(
        array, ("expert", "tensor"), 0, 0, axis_index_groups=groups, tiled=True
    )


def settle(keep, arrived):
    return (keep + arrived.astype(F32)).astype(BF)[None, None]


def on_device(acts, out_grad, probs, counts, w_gate, w_up, w_down):
    experts = lax.axis_size("expert")
    pipes = lax.axis_size("pipe")
    dirs, rows, width = acts.shape[1:]
    slots = 2 * rows // experts
    total = dirs * experts * slots
    hidden = w_gate.shape[3]
    wg, wu, wd = (w_gate[0, 0], w_up[0, 0], w_down[0, 0])
    count_rows = counts[0, :, 0, :]
    packed = shape((experts, dirs, slots, width), BF)
    sided = shape((experts // 2, 2, dirs * slots, width), BF)
    work = 2 * dirs * experts * slots * rows * width
    one = 2 * total * width * hidden

    def mirror(array):
        return lax.ppermute(array, "pipe", [(i, (i + pipes // 2) % pipes) for i in range(pipes)])

    def swap(array):
        return lax.ppermute(array, "tensor", [(0, 1), (1, 0)])

    late = ("down", "slope", "gradsend", "keep", "unpack")

    def kernel(name, body, outs, args, flops, in_place=(), scratch=()):
        limit = 24 * 1024 * 1024 if name in late else None
        specs = [ANY if i in in_place else VM for i in range(len(args))]
        return call(body, outs, args, specs, [VM] * len(outs), scratch, flops, limit)

    side_rows = pltpu.VMEM((2, experts // 2, dirs * slots, width), BF)
    sems = pltpu.SemaphoreType.DMA
    carried = (experts // 2, 2, slots, dirs * width + LANES)

    (x_send,) = kernel("packx", pack_body, [packed], (count_rows, acts[0]), work)
    x_own = dispatch(x_send).reshape(sided.shape)
    wgo = mirror(wg)
    (g_send,) = kernel("packg", pack_scaled_body, [packed], (count_rows, probs[0], out_grad[0]), work)
    g_own = dispatch(g_send).reshape(sided.shape)
    wuo = mirror(wu)
    wdo = mirror(wd)
    x_other = swap(x_own)
    g_other = swap(g_own)
    act, act_t, silu, slope, x_send_t, x_keep_t = kernel(
        "hidden",
        hidden_body,
        [
            shape((total, hidden), BF),
            shape((hidden, total), BF),
            shape((total, hidden), F32),
            shape((total, hidden), F32),
            shape((width, total), BF),
            shape((width, total), BF),
        ],
        (x_own, x_other, wg, wgo, wu, wuo),
        4 * one,
        (0, 1),
        (side_rows, side_rows, sems((4,))),
    )
    (down_send,) = kernel(
        "down",
        down_body,
        [shape((hidden, width), BF)],
        (g_own, g_other, act_t),
        one,
        (0, 1),
        (side_rows, sems((2,))),
    )
    down_got = mirror(down_send)
    d, prob, row_send = kernel(
        "slope",
        slope_body,
        [shape((total, 2 * hidden), BF), shape((total, LANES), F32), shape(carried, BF)],
        (g_own, g_other, wd, wdo, act, silu, slope, wg, wgo, wu, wuo),
        4 * one,
        (0, 1),
        (side_rows, side_rows, sems((4,))),
    )
    row_got = swap(row_send)
    (grad_send,) = kernel(
        "gradsend", grad_send_body, [shape((2, width, hidden), BF)], (x_send_t, d), 2 * one
    )
    grad_got = mirror(grad_send)
    row_keep, grad_keep, down_keep = kernel(
        "keep",
        keep_body,
        [shape(carried, F32), shape((2, width, hidden), F32), shape((hidden, width), F32)],
        (g_own, g_other, x_keep_t, act_t, d, prob, wg, wgo, wu, wuo),
        5 * one,
        (0, 1),
        (side_rows, sems((2,))),
    )
    row_sum = (row_keep + row_got.astype(F32)).astype(BF).reshape(experts, *carried[2:])
    row_back = dispatch(row_sum)
    act_grad, prob_grad = kernel(
        "unpack",
        unpack_body,
        [shape((dirs, rows, width), BF), shape((dirs, rows), BF)],
        (count_rows, probs[0], row_back),
        work,
        (2,),
        (pltpu.VMEM(row_back.shape, BF), sems(())),
    )
    return (
        act_grad[None],
        prob_grad[None],
        settle(grad_keep[0], grad_got[0]),
        settle(grad_keep[1], grad_got[1]),
        settle(down_keep, down_got),
    )


def solution(mesh):
    return jax.shard_map(
        on_device,
        mesh=mesh,
        in_specs=(
            P("pipe", None, "expert", "tensor"),
            P("pipe", None, "expert", "tensor"),
            P("pipe", None, "expert"),
            P("pipe", None, "expert", None),
            P("pipe", "expert", None, "tensor"),
            P("pipe", "expert", None, "tensor"),
            P("pipe", "expert", "tensor", None),
        ),
        out_specs=(
            P("pipe", None, "expert", "tensor"),
            P("pipe", None, "expert"),
            P("pipe", "expert", None, "tensor"),
            P("pipe", "expert", None, "tensor"),
            P("pipe", "expert", "tensor", None),
        ),
        check_vma=False,
    )
```

time: 280 us -> 277 us (0.989)
  waiting for transfers between devices: 156 us -> 175 us
  starting transfers between devices: 79.8 us -> 65.5 us
  Pallas kernels: 32.1 us -> 21.6 us
  local copies, waits for them, and re-layouts: 2.43 us -> 9.24 us
  other arithmetic: 7.66 us -> 3.38 us
    ppermute x4 -> x3, waiting for transfers between devices: 6.3 us -> 19.2 us  [swap(): return lax.ppermute(array, 'tensor', [(0, 1), (1, 0)])]
    all_to_all x4 -> x3, starting transfers between devices: 42.8 us -> 31.7 us  [dispatch(): lax.all_to_all(array, ('expert', 'tensor'), 0, 0, axis_index_groups=group...]
    pallas_call x9 -> x8, Pallas kernels: 32.1 us -> 21.6 us  [call(): pl.pallas_call(body, out_shape=tuple(outs), in_specs=in_specs, out_specs=...]
    unnamed x18 -> x38, local copies, waits for them, and re-layouts: 2.43 us -> 9.24 us
    ppermute x5, waiting for transfers between devices: 110 us -> 116 us  [mirror(): lax.ppermute(array, 'pipe', [(i, (i + pipes // 2) % pipes) for i in range...]
    ppermute x4 -> x3, starting transfers between devices: 15.9 us -> 12.7 us  [swap(): return lax.ppermute(array, 'tensor', [(0, 1), (1, 0)])]
    all_to_all x4 -> x3, waiting for transfers between devices: 39.9 us -> 39.9 us  [dispatch(): lax.all_to_all(array, ('expert', 'tensor'), 0, 0, axis_index_groups=group...]
  transfers between devices with their start and end apart: 13 -> 11, of which waited for: 8 -> 7; matrix products, arithmetic and copies ran while one was open for 3% -> 1% of each run, Pallas kernels for 7% -> 5%
where the time goes in v3:
time: 277 us; the launch traced here: 276 us
  waiting for transfers between devices  175 us (63%)
  starting transfers between devices  65.5 us (24%)
  Pallas kernels  21.6 us (8%)
  local copies, waits for them, and re-layouts  9.24 us (3%)
  other arithmetic  3.38 us (1%)
    ppermute x5, waiting for transfers between devices, mirror(): lax.ppermute(array, 'pipe', [(i, (i + pipes // 2) % pipes) for i in range...  116 us
    all_to_all x3, waiting for transfers between devices, dispatch(): lax.all_to_all(array, ('expert', 'tensor'), 0, 0, axis_index_groups=group...  39.9 us
    all_to_all x3, starting transfers between devices, dispatch(): lax.all_to_all(array, ('expert', 'tensor'), 0, 0, axis_index_groups=group...  31.7 us
    pallas_call x8, Pallas kernels, call(): pl.pallas_call(body, out_shape=tuple(outs), in_specs=in_specs, out_specs=...  21.6 us
    ppermute x5, starting transfers between devices, mirror(): lax.ppermute(array, 'pipe', [(i, (i + pipes // 2) % pipes) for i in range...  21.2 us
    ppermute x3, waiting for transfers between devices, swap(): return lax.ppermute(array, 'tensor', [(0, 1), (1, 0)])  19.2 us
    ppermute x3, starting transfers between devices, swap(): return lax.ppermute(array, 'tensor', [(0, 1), (1, 0)])  12.7 us
    unnamed x38, local copies, waits for them, and re-layouts  9.24 us
  transfers between devices with their start and end apart: 11, of which 7 were waited for; matrix products, arithmetic and copies ran while one was open for 1% of the time, Pallas kernels for 5%

profile of v3, /device:TPU:45, one launch (start us, length us, event | category | flops | bytes accessed | tf_op | source)
XLA Modules:
  0.0 275.5 jit_solution(7234688599436931766)
XLA Ops:
  0.6 2.6 shard_map.111
  3.2 11.2 %all-to-all-start.1 = ((bf16[16,2,16,1024]{3,2,1,0:T(8,128)(2,1)}), bf16[16,2,16,1024]{3,2,1,0:T(8,128)(2,1)}, u32[]{:S(2)}, u32[]{:S(2)}) async-start(bf16[16,2,16,1024]{3,2,1,0:T(8,128)(2,1)} %shard_map.111), calls=%async_computation.1 | async-start | bytes 2097152 | tf_op jit(solution)/shard_map/all_to_all | solution.py:226
  14.5 2.6 shard_map.110
  17.1 21.8 %all-to-all-done.1 = bf16[16,2,16,1024]{3,2,1,0:T(8,128)(2,1)} async-done(((bf16[16,2,16,1024]{3,2,1,0:T(8,128)(2,1)}), bf16[16,2,16,1024]{3,2,1,0:T(8,128)(2,1)}, u32[]{:S(2)}, u32[]{:S(2)}) %all-to-all-start.1) | async-done | bytes 1048608 | tf_op jit(solution)/shard_map/all_to_all | solution.py:226
  38.9 7.4 %all-to-all-start = ((bf16[16,2,16,1024]{3,2,1,0:T(8,128)(2,1)}), bf16[16,2,16,1024]{3,2,1,0:T(8,128)(2,1)S(1)}, u32[]{:S(2)}, u32[]{:S(2)}) async-start(bf16[16,2,16,1024]{3,2,1,0:T(8,128)(2,1)} %shard_map.110), calls=%async_computation | async-start | bytes 2097152 | tf_op jit(solution)/shard_map/all_to_all | solution.py:226
  46.2 5.2 %collective-permute-start.1 = (bf16[8,2,32,1024]{3,2,1,0:T(8,128)(2,1)}, bf16[8,2,32,1024]{3,2,1,0:T(8,128)(2,1)}, u32[]{:S(2)}, u32[]{:S(2)}) collective-permute-start(bf16[8,2,32,1024]{3,2,1,0:T(8,128)(2,1)} %bitcast.5.own), channel_id=1, source_target_pairs={{0,1},{1,0},{2,3},{3,2},{4,5},{5,4},{6,7},{7,6},{8,9},{9,8},{10,11... | collective-permute-start | bytes 3145736 | tf_op jit(solution)/shard_map/ppermute | solution.py:253
  51.5 18.2 %all-to-all-done = bf16[16,2,16,1024]{3,2,1,0:T(8,128)(2,1)S(1)} async-done(((bf16[16,2,16,1024]{3,2,1,0:T(8,128)(2,1)}), bf16[16,2,16,1024]{3,2,1,0:T(8,128)(2,1)S(1)}, u32[]{:S(2)}, u32[]{:S(2)}) %all-to-all-start) | async-done | bytes 1048608 | tf_op jit(solution)/shard_map/all_to_all | solution.py:226
  69.6 5.2 %collective-permute-start = (bf16[8,2,32,1024]{3,2,1,0:T(8,128)(2,1)S(1)}, bf16[8,2,32,1024]{3,2,1,0:T(8,128)(2,1)S(1)}, u32[]{:S(2)}, u32[]{:S(2)}) collective-permute-start(bf16[8,2,32,1024]{3,2,1,0:T(8,128)(2,1)S(1)} %bitcast.18), channel_id=1, source_target_pairs={{0,1},{1,0},{2,3},{3,2},{4,5},{5,4},{6,7},{7,6},{8,9},{9,8},{10,11... | collective-permute-start | bytes 3145736 | tf_op jit(solution)/shard_map/ppermute | solution.py:253
  74.9 2.6 collective-permute-start.2
  77.5 6.6 %collective-permute-start.3 = (bf16[1024,256]{1,0:T(8,128)(2,1)}, bf16[1024,256]{1,0:T(8,128)(2,1)S(1)}, u32[]{:S(2)}, u32[]{:S(2)}) collective-permute-start(bf16[1024,256]{1,0:T(8,128)(2,1)} %bitcast.7.wu), channel_id=1, source_target_pairs={{0,256},{32,288},{64,320},{96,352},{128,384},{160,416},{192,448},{... | collective-permute-start | bytes 1572872 | tf_op jit(solution)/shard_map/ppermute | solution.py:250
  84.1 2.6 collective-permute-start.4
  86.7 13.1 %collective-permute-done.2.wgo = bf16[1024,256]{1,0:T(8,128)(2,1)S(1)} collective-permute-done((bf16[1024,256]{1,0:T(8,128)(2,1)}, bf16[1024,256]{1,0:T(8,128)(2,1)S(1)}, u32[]{:S(2)}, u32[]{:S(2)}) %collective-permute-start.2) | collective-permute-done | bytes 524320 | tf_op jit(solution)/shard_map/ppermute | solution.py:250
  99.8 24.0 %collective-permute-done.3.wuo = bf16[1024,256]{1,0:T(8,128)(2,1)S(1)} collective-permute-done((bf16[1024,256]{1,0:T(8,128)(2,1)}, bf16[1024,256]{1,0:T(8,128)(2,1)S(1)}, u32[]{:S(2)}, u32[]{:S(2)}) %collective-permute-start.3) | collective-permute-done | bytes 524320 | tf_op jit(solution)/shard_map/ppermute | solution.py:250
  124.7 6.3 %shard_map.112 = (bf16[512,256]{1,0:T(8,128)(2,1)}, bf16[256,512]{1,0:T(8,128)(2,1)}, f32[512,256]{1,0:T(8,128)}, f32[512,256]{1,0:T(8,128)}, bf16[1024,512]{1,0:T(8,128)(2,1)}, /*index=5*/bf16[1024,512]{1,0:T(8,128)(2,1)}) custom-call(bf16[8,2,32,1024]{3,2,1,0:T(8,128)(2,1)} %bitcast.5.own, bf16[8,2,32,1024]{3,2,1,0:T(8,128)(2,1)} %collective-permute-done.1.other, ...), custom_call_target="tpu_custom_call" | custom-call | flops 1073741824 | bytes 7864320 | tf_op jit(solution)/shard_map/pallas_call | solution.py:22
  130.9 17.1 %collective-permute-done.4.wdo = bf16[256,1024]{1,0:T(8,128)(2,1)} collective-permute-done((bf16[256,1024]{1,0:T(8,128)(2,1)}, bf16[256,1024]{1,0:T(8,128)(2,1)}, u32[]{:S(2)}, u32[]{:S(2)}) %collective-permute-start.4) | collective-permute-done | bytes 524320 | tf_op jit(solution)/shard_map/ppermute | solution.py:250
  154.2 4.1 %shard_map.113 = (bf16[512,512]{1,0:T(8,128)(2,1)S(1)}, f32[512,128]{1,0:T(8,128)S(1)}, bf16[8,2,16,2176]{3,2,1,0:T(8,128)(2,1)S(1)}) custom-call(bf16[8,2,32,1024]{3,2,1,0:T(8,128)(2,1)S(1)} %bitcast.19, bf16[8,2,32,1024]{3,2,1,0:T(8,128)(2,1)S(1)} %collective-permute-done.other, bf16[256,1024]{1,0:T(8,128)(2,1)S(1)} %bitcast.23, ...), custom_call_target="tpu_custom_call" | custom-call | flops 1073741824 | bytes 8454144 | tf_op jit(solution)/shard_map/pallas_call | solution.py:22
  158.3 2.2 collective-permute-start.5
  160.6 3.0 %shard_map.114 = (f32[8,2,16,2176]{3,2,1,0:T(8,128)S(1)}, f32[2,1024,256]{2,1,0:T(8,128)S(1)}, f32[256,1024]{1,0:T(8,128)S(1)}) custom-call(bf16[8,2,32,1024]{3,2,1,0:T(8,128)(2,1)S(1)} %bitcast.20, bf16[8,2,32,1024]{3,2,1,0:T(8,128)(2,1)S(1)} %collective-permute-done.other, bf16[1024,512]{1,0:T(8,128)(2,1)S(1)} %copy-done.11, ...), custom_call_target="tpu_custom_call" | custom-call | flops 1342177280 | bytes 11665408 | tf_op jit(solution)/shard_map/pallas_call | solution.py:22
  163.6 19.2 %collective-permute-done.5 = bf16[8,2,16,2176]{3,2,1,0:T(8,128)(2,1)S(1)} collective-permute-done((bf16[8,2,16,2176]{3,2,1,0:T(8,128)(2,1)S(1)}, bf16[8,2,16,2176]{3,2,1,0:T(8,128)(2,1)S(1)}, u32[]{:S(2)}, u32[]{:S(2)}) %collective-permute-start.5) | collective-permute-done | bytes 1114144 | tf_op jit(solution)/shard_map/ppermute | solution.py:253
  184.0 13.1 %all-to-all-start.2 = ((bf16[16,16,2176]{2,1,0:T(8,128)(2,1)}), bf16[16,16,2176]{2,1,0:T(8,128)(2,1)S(1)}, u32[]{:S(2)}, u32[]{:S(2)}) async-start(bf16[16,16,2176]{2,1,0:T(8,128)(2,1)} %bitcast.29), calls=%async_computation.2 | async-start | bytes 2228224 | tf_op jit(solution)/shard_map/all_to_all | solution.py:226
  200.1 2.1 collective-permute-start.6
  202.7 7.3 %collective-permute-start.7 = (bf16[256,1024]{1,0:T(8,128)(2,1)S(1)}, bf16[256,1024]{1,0:T(8,128)(2,1)S(1)}, u32[]{:S(2)}, u32[]{:S(2)}) collective-permute-start(bf16[256,1024]{1,0:T(8,128)(2,1)S(1)} %shard_map.117), channel_id=1, source_target_pairs={{0,256},{32,288},{64,320},{96,352},{128,384},{160,416},{192,448},{... | collective-permute-start | bytes 1572872 | tf_op jit(solution)/shard_map/ppermute | solution.py:250
  210.0 61.6 %collective-permute-done.7 = bf16[256,1024]{1,0:T(8,128)(2,1)S(1)} collective-permute-done((bf16[256,1024]{1,0:T(8,128)(2,1)S(1)}, bf16[256,1024]{1,0:T(8,128)(2,1)S(1)}, u32[]{:S(2)}, u32[]{:S(2)}) %collective-permute-start.7) | collective-permute-done | bytes 524320 | tf_op jit(solution)/shard_map/ppermute | solution.py:250
  273.9 1.7 shard_map.115
  (47 shorter events, 13.9 us)
Async XLA Ops:
  3.2 35.6 %all-to-all-start.1 = ((bf16[16,2,16,1024]{3,2,1,0:T(8,128)(2,1)}), bf16[16,2,16,1024]{3,2,1,0:T(8,128)(2,1)}, u32[]{:S(2)}, u32[]{:S(2)}) async-start(bf16[16,2,16,1024]{3,2,1,0:T(8,128)(2,1)} %shard_map.111), calls=%async_computation.1 | async-start | bytes 2097152 | tf_op jit(solution)/shard_map/all_to_all | solution.py:226
  38.9 30.8 %all-to-all-start = ((bf16[16,2,16,1024]{3,2,1,0:T(8,128)(2,1)}), bf16[16,2,16,1024]{3,2,1,0:T(8,128)(2,1)S(1)}, u32[]{:S(2)}, u32[]{:S(2)}) async-start(bf16[16,2,16,1024]{3,2,1,0:T(8,128)(2,1)} %shard_map.110), calls=%async_computation | async-start | bytes 2097152 | tf_op jit(solution)/shard_map/all_to_all | solution.py:226
  46.2 77.7 %collective-permute-start.1 = (bf16[8,2,32,1024]{3,2,1,0:T(8,128)(2,1)}, bf16[8,2,32,1024]{3,2,1,0:T(8,128)(2,1)}, u32[]{:S(2)}, u32[]{:S(2)}) collective-permute-start(bf16[8,2,32,1024]{3,2,1,0:T(8,128)(2,1)} %bitcast.5.own), channel_id=1, source_target_pairs={{0,1},{1,0},{2,3},{3,2},{4,5},{5,4},{6,7},{7,6},{8,9},{9,8},{10,11... | collective-permute-start | bytes 3145736 | tf_op jit(solution)/shard_map/ppermute | solution.py:253
  69.6 78.4 %collective-permute-start = (bf16[8,2,32,1024]{3,2,1,0:T(8,128)(2,1)S(1)}, bf16[8,2,32,1024]{3,2,1,0:T(8,128)(2,1)S(1)}, u32[]{:S(2)}, u32[]{:S(2)}) collective-permute-start(bf16[8,2,32,1024]{3,2,1,0:T(8,128)(2,1)S(1)} %bitcast.18), channel_id=1, source_target_pairs={{0,1},{1,0},{2,3},{3,2},{4,5},{5,4},{6,7},{7,6},{8,9},{9,8},{10,11... | collective-permute-start | bytes 3145736 | tf_op jit(solution)/shard_map/ppermute | solution.py:253
  74.9 24.9 %collective-permute-start.2 = (bf16[1024,256]{1,0:T(8,128)(2,1)}, bf16[1024,256]{1,0:T(8,128)(2,1)S(1)}, u32[]{:S(2)}, u32[]{:S(2)}) collective-permute-start(bf16[1024,256]{1,0:T(8,128)(2,1)} %bitcast.6.wg), channel_id=1, source_target_pairs={{0,256},{32,288},{64,320},{96,352},{128,384},{160,416},{192,448},{... | collective-permute-start | bytes 1572872 | tf_op jit(solution)/shard_map/ppermute | solution.py:250
  77.5 46.3 %collective-permute-start.3 = (bf16[1024,256]{1,0:T(8,128)(2,1)}, bf16[1024,256]{1,0:T(8,128)(2,1)S(1)}, u32[]{:S(2)}, u32[]{:S(2)}) collective-permute-start(bf16[1024,256]{1,0:T(8,128)(2,1)} %bitcast.7.wu), channel_id=1, source_target_pairs={{0,256},{32,288},{64,320},{96,352},{128,384},{160,416},{192,448},{... | collective-permute-start | bytes 1572872 | tf_op jit(solution)/shard_map/ppermute | solution.py:250
  84.1 63.9 %collective-permute-start.4 = (bf16[256,1024]{1,0:T(8,128)(2,1)}, bf16[256,1024]{1,0:T(8,128)(2,1)}, u32[]{:S(2)}, u32[]{:S(2)}) collective-permute-start(bf16[256,1024]{1,0:T(8,128)(2,1)} %bitcast.22), channel_id=1, source_target_pairs={{0,256},{32,288},{64,320},{96,352},{128,384},{160,416},{192,448},{... | collective-permute-start | bytes 1572872 | tf_op jit(solution)/shard_map/ppermute | solution.py:250
  99.8 24.1 %copy-start = (bf16[1024,256]{1,0:T(8,128)(2,1)}, bf16[1024,256]{1,0:T(8,128)(2,1)S(1)}, u32[]{:S(2)}) copy-start(bf16[1024,256]{1,0:T(8,128)(2,1)S(1)} %collective-permute-done.2.wgo) | copy-start | bytes 1572868
  148.0 1.0 copy-start.1
  149.0 1.0 copy-start.3
  154.2 6.4 %copy-start.11 = (bf16[1024,512]{1,0:T(8,128)(2,1)S(1)}, bf16[1024,512]{1,0:T(8,128)(2,1)}, u32[]{:S(2)}) copy-start(bf16[1024,512]{1,0:T(8,128)(2,1)} %get-tuple-element.19.x_t) | copy-start | bytes 3145732
  154.2 6.4 %copy-start.12 = (bf16[256,512]{1,0:T(8,128)(2,1)S(1)}, bf16[256,512]{1,0:T(8,128)(2,1)}, u32[]{:S(2)}) copy-start(bf16[256,512]{1,0:T(8,128)(2,1)} %get-tuple-element.20.act_t) | copy-start | bytes 786436
  158.3 5.3 %copy-start.4 = (bf16[512,512]{1,0:T(8,128)(2,1)}, bf16[512,512]{1,0:T(8,128)(2,1)S(1)}, u32[]{:S(2)}) copy-start(bf16[512,512]{1,0:T(8,128)(2,1)S(1)} %get-tuple-element.24.d) | copy-start | bytes 1572868
  158.3 24.5 %collective-permute-start.5 = (bf16[8,2,16,2176]{3,2,1,0:T(8,128)(2,1)S(1)}, bf16[8,2,16,2176]{3,2,1,0:T(8,128)(2,1)S(1)}, u32[]{:S(2)}, u32[]{:S(2)}) collective-permute-start(bf16[8,2,16,2176]{3,2,1,0:T(8,128)(2,1)S(1)} %get-tuple-element.27), channel_id=1, source_target_pairs={{0,1},{1,0},{2,3},{3,2},{4,5},{5,4},{6,7},{7,6},{8,9},{9,8},{10,11... | collective-permute-start | bytes 3342344 | tf_op jit(solution)/shard_map/ppermute | solution.py:253
  163.6 20.4 %copy-start.6 = (f32[2,1024,256]{2,1,0:T(8,128)}, f32[2,1024,256]{2,1,0:T(8,128)S(1)}, u32[]{:S(2)}) copy-start(f32[2,1024,256]{2,1,0:T(8,128)S(1)} %get-tuple-element.30) | copy-start | bytes 6291460
  163.6 20.4 %copy-start.9 = (f32[256,1024]{1,0:T(8,128)}, f32[256,1024]{1,0:T(8,128)S(1)}, u32[]{:S(2)}) copy-start(f32[256,1024]{1,0:T(8,128)S(1)} %get-tuple-element.32) | copy-start | bytes 3145732
  184.0 89.8 %all-to-all-start.2 = ((bf16[16,16,2176]{2,1,0:T(8,128)(2,1)}), bf16[16,16,2176]{2,1,0:T(8,128)(2,1)S(1)}, u32[]{:S(2)}, u32[]{:S(2)}) async-start(bf16[16,16,2176]{2,1,0:T(8,128)(2,1)} %bitcast.29), calls=%async_computation.2 | async-start | bytes 2228224 | tf_op jit(solution)/shard_map/all_to_all | solution.py:226
  198.2 1.2 copy-start.8
  199.4 72.3 %copy-start.10 = (f32[256,1024]{1,0:T(8,128)S(1)}, f32[256,1024]{1,0:T(8,128)}, u32[]{:S(2)}) copy-start(f32[256,1024]{1,0:T(8,128)} %copy-done.9) | copy-start | bytes 3145732
  200.1 72.5 %copy-start.7 = (f32[2,1024,256]{2,1,0:T(8,128)S(1)}, f32[2,1024,256]{2,1,0:T(8,128)}, u32[]{:S(2)}) copy-start(f32[2,1024,256]{2,1,0:T(8,128)} %copy-done.6) | copy-start | bytes 6291460
  200.1 72.5 %collective-permute-start.6 = (bf16[2,1024,256]{2,1,0:T(8,128)(2,1)S(1)}, bf16[2,1024,256]{2,1,0:T(8,128)(2,1)S(1)}, u32[]{:S(2)}, u32[]{:S(2)}) collective-permute-start(bf16[2,1024,256]{2,1,0:T(8,128)(2,1)S(1)} %shard_map.116), channel_id=1, source_target_pairs={{0,256},{32,288},{64,320},{96,352},{128,384},{160,416},{192,448},{... | collective-permute-start | bytes 3145736 | tf_op jit(solution)/shard_map/ppermute | solution.py:250
  202.7 68.9 %collective-permute-start.7 = (bf16[256,1024]{1,0:T(8,128)(2,1)S(1)}, bf16[256,1024]{1,0:T(8,128)(2,1)S(1)}, u32[]{:S(2)}, u32[]{:S(2)}) collective-permute-start(bf16[256,1024]{1,0:T(8,128)(2,1)S(1)} %shard_map.117), channel_id=1, source_target_pairs={{0,256},{32,288},{64,320},{96,352},{128,384},{160,416},{192,448},{... | collective-permute-start | bytes 1572872 | tf_op jit(solution)/shard_map/ppermute | solution.py:250
  272.6 1.2 copy-start.17
  272.6 1.2 copy-start.18
  (6 other events, 5.9 us)

commit v4 on v3

--- a/solution.py
+++ b/solution.py
@@ -82,8 +82,12 @@
         prob_ref[d : d + 1, :] = (found / probs_ref[d : d + 1, :].astype(F32)).astype(BF)
 
 
+def half_index():
+    return lax.axis_index("pipe") // (lax.axis_size("pipe") // 2)
+
+
 def keeps_low():
-    half = lax.axis_index("pipe") // (lax.axis_size("pipe") // 2)
+    half = half_index()
     group = (lax.axis_index("tensor") + lax.axis_index("expert")) % 2
     return half == group
 
@@ -108,7 +112,7 @@
 
 
 def hidden_body(
-    own, other, wg, wgo, wu, wuo, act_ref, act_t_ref, silu_ref, slope_ref, send_ref, keep_ref, low, high, sems
+    own, other, wg, wgo, wu, wuo, act_ref, act_t_ref, silu_ref, slope_ref, keep_ref, low, high, sems
 ):
     copies = row_copies(own, other, low, high, sems)
     for c in copies:
@@ -128,7 +132,6 @@
     act_t_ref[...] = act.T
     silu_ref[...] = silu
     slope_ref[...] = up * (sigma * (1.0 + gate * (1.0 - sigma)))
-    send_ref[...] = jnp.where(same, xb, xa).T
     keep_ref[...] = jnp.where(same, xa, xb).T
 
 
@@ -196,11 +199,46 @@
     row_terms(d, weight_sides(same, wg, wgo), weight_sides(same, wu, wuo), prob, row_ref, 1)
 
 
-def grad_send_body(x_t, d, out_ref):
-    both = dot(x_t[...], d[...], 1, 0).astype(BF)
-    hidden = out_ref.shape[2]
-    out_ref[0] = both[:, :hidden]
-    out_ref[1] = both[:, hidden:]
+def piece_body(counts_ref, values_ref, other_ref, out_ref):
+    rows = other_ref.shape[0]
+    experts = counts_ref.shape[1]
+    straight = lax.axis_index("tensor") != half_index()
+    out_ref[0:rows] = jnp.where(straight, values_ref[0], other_ref[...])
+    out_ref[rows:] = jnp.zeros((out_ref.shape[0] - rows, out_ref.shape[1]), BF)
+    count = jnp.where(straight, counts_ref[0:1, :], counts_ref[1:2, :])
+    padded = jnp.broadcast_to(count.astype(F32), (out_ref.shape[0] - rows, experts))
+    out_ref[rows:, 0:experts] = padded.astype(BF)
+
+
+def pack_piece_body(piece_ref, out_ref):
+    experts, slots, width = out_ref.shape
+    rows = slots * experts // 2
+    count = piece_ref[rows:, :].astype(F32)[0:1, 0:experts].astype(jnp.int32)
+    mask = slot_choice(count, slots, rows)
+    packed = dot(mask.astype(BF), piece_ref[0:rows, :], 1, 0).astype(BF)
+    out_ref[...] = packed.reshape(experts, slots, width)
+
+
+def turn_body(own, other, out_ref, buffer, sems):
+    d = 1 - keeps_low().astype(jnp.int32)
+    copies = [
+        pltpu.make_async_copy(own.at[:, 0], buffer.at[0, :, d], sems.at[0]),
+        pltpu.make_async_copy(other.at[:, 0], buffer.at[0, :, 1 - d], sems.at[1]),
+        pltpu.make_async_copy(own.at[:, 1], buffer.at[1, :, 1 - d], sems.at[2]),
+        pltpu.make_async_copy(other.at[:, 1], buffer.at[1, :, d], sems.at[3]),
+    ]
+    for c in copies:
+        c.start()
+    for c in copies:
+        c.wait()
+    out_ref[...] = buffer[...].reshape(out_ref.shape[1], out_ref.shape[0]).T
+
+
+def final_body(x_t, d, keep, gate_ref, up_ref):
+    both = dot(x_t[...], d[...], 1, 0)
+    hidden = gate_ref.shape[1]
+    gate_ref[...] = (keep[0] + both[:, :hidden]).astype(BF)
+    up_ref[...] = (keep[1] + both[:, hidden:]).astype(BF)
 
 
 def keep_body(
@@ -252,7 +290,7 @@
     def swap(array):
         return lax.ppermute(array, "tensor", [(0, 1), (1, 0)])
 
-    late = ("down", "slope", "gradsend", "keep", "unpack")
+    late = ("hidden", "down", "slope", "keep", "turn", "final", "unpack")
 
     def kernel(name, body, outs, args, flops, in_place=(), scratch=()):
         limit = 24 * 1024 * 1024 if name in late else None
@@ -269,10 +307,18 @@
     (g_send,) = kernel("packg", pack_scaled_body, [packed], (count_rows, probs[0], out_grad[0]), work)
     g_own = dispatch(g_send).reshape(sided.shape)
     wuo = mirror(wu)
+    x_second = swap(acts[0, 1])
+    (piece,) = kernel(
+        "piece", piece_body, [shape((rows + 16, width), BF)], (count_rows, acts[0], x_second), 0
+    )
+    piece_got = mirror(piece)
+    (m_send,) = kernel("packm", pack_piece_body, [shape((experts, slots, width), BF)], (piece_got,), work // 4)
+    m_own = dispatch(m_send).reshape(experts // 2, 2, slots, width)
+    m_other = swap(m_own)
     wdo = mirror(wd)
     x_other = swap(x_own)
     g_other = swap(g_own)
-    act, act_t, silu, slope, x_send_t, x_keep_t = kernel(
+    act, act_t, silu, slope, x_keep_t = kernel(
         "hidden",
         hidden_body,
         [
@@ -280,7 +326,6 @@
             shape((hidden, total), BF),
             shape((total, hidden), F32),
             shape((total, hidden), F32),
-            shape((width, total), BF),
             shape((width, total), BF),
         ],
         (x_own, x_other, wg, wgo, wu, wuo),
@@ -308,10 +353,16 @@
         (side_rows, side_rows, sems((4,))),
     )
     row_got = swap(row_send)
-    (grad_send,) = kernel(
-        "gradsend", grad_send_body, [shape((2, width, hidden), BF)], (x_send_t, d), 2 * one
-    )
-    grad_got = mirror(grad_send)
+    d_got = mirror(d)
+    (m_t,) = kernel(
+        "turn",
+        turn_body,
+        [shape((width, total), BF)],
+        (m_own, m_other),
+        0,
+        (0, 1),
+        (pltpu.VMEM((2, experts // 2, dirs, slots, width), BF), sems((4,))),
+    )
     row_keep, grad_keep, down_keep = kernel(
         "keep",
         keep_body,
@@ -320,6 +371,13 @@
         5 * one,
         (0, 1),
         (side_rows, sems((2,))),
+    )
+    gate_grad, up_grad = kernel(
+        "final",
+        final_body,
+        [shape((width, hidden), BF), shape((width, hidden), BF)],
+        (m_t, d_got, grad_keep),
+        2 * one,
     )
     row_sum = (row_keep + row_got.astype(F32)).astype(BF).reshape(experts, *carried[2:])
     row_back = dispatch(row_sum)
@@ -335,8 +393,8 @@
     return (
         act_grad[None],
         prob_grad[None],
-        settle(grad_keep[0], grad_got[0]),
-        settle(grad_keep[1], grad_got[1]),
+        gate_grad[None, None],
+        up_grad[None, None],
         settle(down_keep, down_got),
     )
 

time: 277 us -> 294 us (1.061)
  the two profiles are of different devices: /device:TPU:45 before, /device:TPU:13 now
where the time goes in v4:
time: 294 us; the launch traced here: 293 us
  waiting for transfers between devices  161 us (55%)
  starting transfers between devices  94.3 us (32%)
  Pallas kernels  23.2 us (8%)
  local copies, waits for them, and re-layouts  10.2 us (3%)
  other arithmetic  3.42 us (1%)
    ppermute x6, waiting for transfers between devices, mirror(): lax.ppermute(array, 'pipe', [(i, (i + pipes // 2) % pipes) for i in range...  92.6 us
    all_to_all x4, waiting for transfers between devices, dispatch(): lax.all_to_all(array, ('expert', 'tensor'), 0, 0, axis_index_groups=group...  42.4 us
    all_to_all x4, starting transfers between devices, dispatch(): lax.all_to_all(array, ('expert', 'tensor'), 0, 0, axis_index_groups=group...  42.3 us
    ppermute x6, starting transfers between devices, mirror(): lax.ppermute(array, 'pipe', [(i, (i + pipes // 2) % pipes) for i in range...  32.5 us
    ppermute x5, waiting for transfers between devices, swap(): return lax.ppermute(array, 'tensor', [(0, 1), (1, 0)])  25.5 us
    pallas_call x11, Pallas kernels, call(): pl.pallas_call(body, out_shape=tuple(outs), in_specs=in_specs, out_specs=...  23.2 us
    ppermute x5, starting transfers between devices, swap(): return lax.ppermute(array, 'tensor', [(0, 1), (1, 0)])  19.5 us
    unnamed x40, local copies, waits for them, and re-layouts  10.2 us
  transfers between devices with their start and end apart: 15, of which 11 were waited for; matrix products, arithmetic and copies ran while one was open for 1% of the time, Pallas kernels for 5%

profile of v4, /device:TPU:13, one launch (start us, length us, event | category | flops | bytes accessed | tf_op | source)
XLA Modules:
  0.0 292.6 jit_solution(17350969938821042476)
XLA Ops:
  3.3 11.2 %all-to-all-start.1 = ((bf16[16,2,16,1024]{3,2,1,0:T(8,128)(2,1)}), bf16[16,2,16,1024]{3,2,1,0:T(8,128)(2,1)}, u32[]{:S(2)}, u32[]{:S(2)}) async-start(bf16[16,2,16,1024]{3,2,1,0:T(8,128)(2,1)} %shard_map.111), calls=%async_computation.1 | async-start | bytes 2097152 | tf_op jit(solution)/shard_map/all_to_all | solution.py:264
  17.1 21.8 %all-to-all-done.1 = bf16[16,2,16,1024]{3,2,1,0:T(8,128)(2,1)} async-done(((bf16[16,2,16,1024]{3,2,1,0:T(8,128)(2,1)}), bf16[16,2,16,1024]{3,2,1,0:T(8,128)(2,1)}, u32[]{:S(2)}, u32[]{:S(2)}) %all-to-all-start.1) | async-done | bytes 1048608 | tf_op jit(solution)/shard_map/all_to_all | solution.py:264
  38.9 7.3 %all-to-all-start = ((bf16[16,2,16,1024]{3,2,1,0:T(8,128)(2,1)}), bf16[16,2,16,1024]{3,2,1,0:T(8,128)(2,1)S(1)}, u32[]{:S(2)}, u32[]{:S(2)}) async-start(bf16[16,2,16,1024]{3,2,1,0:T(8,128)(2,1)} %shard_map.110), calls=%async_computation | async-start | bytes 2097152 | tf_op jit(solution)/shard_map/all_to_all | solution.py:264
  46.3 5.2 %collective-permute-start.1 = (bf16[8,2,32,1024]{3,2,1,0:T(8,128)(2,1)}, bf16[8,2,32,1024]{3,2,1,0:T(8,128)(2,1)}, u32[]{:S(2)}, u32[]{:S(2)}) collective-permute-start(bf16[8,2,32,1024]{3,2,1,0:T(8,128)(2,1)} %bitcast.5.own), channel_id=1, source_target_pairs={{0,1},{1,0},{2,3},{3,2},{4,5},{5,4},{6,7},{7,6},{8,9},{9,8},{10,11... | collective-permute-start | bytes 3145736 | tf_op jit(solution)/shard_map/ppermute | solution.py:291
  51.5 18.2 %all-to-all-done = bf16[16,2,16,1024]{3,2,1,0:T(8,128)(2,1)S(1)} async-done(((bf16[16,2,16,1024]{3,2,1,0:T(8,128)(2,1)}), bf16[16,2,16,1024]{3,2,1,0:T(8,128)(2,1)S(1)}, u32[]{:S(2)}, u32[]{:S(2)}) %all-to-all-start) | async-done | bytes 1048608 | tf_op jit(solution)/shard_map/all_to_all | solution.py:264
  69.7 5.2 %collective-permute-start = (bf16[8,2,32,1024]{3,2,1,0:T(8,128)(2,1)S(1)}, bf16[8,2,32,1024]{3,2,1,0:T(8,128)(2,1)S(1)}, u32[]{:S(2)}, u32[]{:S(2)}) collective-permute-start(bf16[8,2,32,1024]{3,2,1,0:T(8,128)(2,1)S(1)} %bitcast.19), channel_id=1, source_target_pairs={{0,1},{1,0},{2,3},{3,2},{4,5},{5,4},{6,7},{7,6},{8,9},{9,8},{10,11... | collective-permute-start | bytes 3145736 | tf_op jit(solution)/shard_map/ppermute | solution.py:291
  74.9 6.5 %collective-permute-start.2 = (bf16[1024,256]{1,0:T(8,128)(2,1)S(1)}, bf16[1024,256]{1,0:T(8,128)(2,1)S(1)}, u32[]{:S(2)}, u32[]{:S(2)}) collective-permute-start(bf16[1024,256]{1,0:T(8,128)(2,1)S(1)} %bitcast.23), channel_id=1, source_target_pairs={{0,256},{32,288},{64,320},{96,352},{128,384},{160,416},{192,448},{... | collective-permute-start | bytes 1572872 | tf_op jit(solution)/shard_map/ppermute | solution.py:288
  81.5 2.6 collective-permute-start.3
  84.2 6.7 %collective-permute-start.4 = (bf16[256,1024]{1,0:T(8,128)(2,1)}, bf16[256,1024]{1,0:T(8,128)(2,1)S(1)}, u32[]{:S(2)}, u32[]{:S(2)}) collective-permute-start(bf16[256,1024]{1,0:T(8,128)(2,1)} %bitcast.31), channel_id=1, source_target_pairs={{0,256},{32,288},{64,320},{96,352},{128,384},{160,416},{192,448},{... | collective-permute-start | bytes 1572872 | tf_op jit(solution)/shard_map/ppermute | solution.py:288
  90.8 8.4 %collective-permute-done.2.wgo = bf16[1024,256]{1,0:T(8,128)(2,1)S(1)} collective-permute-done((bf16[1024,256]{1,0:T(8,128)(2,1)S(1)}, bf16[1024,256]{1,0:T(8,128)(2,1)S(1)}, u32[]{:S(2)}, u32[]{:S(2)}) %collective-permute-start.2) | collective-permute-done | bytes 524320 | tf_op jit(solution)/shard_map/ppermute | solution.py:288
  99.3 24.1 %collective-permute-done.3.wuo = bf16[1024,256]{1,0:T(8,128)(2,1)S(1)} collective-permute-done((bf16[1024,256]{1,0:T(8,128)(2,1)S(1)}, bf16[1024,256]{1,0:T(8,128)(2,1)S(1)}, u32[]{:S(2)}, u32[]{:S(2)}) %collective-permute-start.3) | collective-permute-done | bytes 524320 | tf_op jit(solution)/shard_map/ppermute | solution.py:288
  123.4 3.1 %shard_map.112 = (bf16[512,256]{1,0:T(8,128)(2,1)S(1)}, bf16[256,512]{1,0:T(8,128)(2,1)S(1)}, f32[512,256]{1,0:T(8,128)S(1)}, f32[512,256]{1,0:T(8,128)S(1)}, bf16[1024,512]{1,0:T(8,128)(2,1)S(1)}) custom-call(bf16[8,2,32,1024]{3,2,1,0:T(8,128)(2,1)} %bitcast.5.own, bf16[8,2,32,1024]{3,2,1,0:T(8,128)(2,1)} %collective-permute-done.1.other, ...), custom_call_target="tpu_custom_call" | custom-call | flops 1073741824 | bytes 6815744 | tf_op jit(solution)/shard_map/pallas_call | solution.py:22
  127.5 20.0 %collective-permute-done.4.wdo = bf16[256,1024]{1,0:T(8,128)(2,1)S(1)} collective-permute-done((bf16[256,1024]{1,0:T(8,128)(2,1)}, bf16[256,1024]{1,0:T(8,128)(2,1)S(1)}, u32[]{:S(2)}, u32[]{:S(2)}) %collective-permute-start.4) | collective-permute-done | bytes 524320 | tf_op jit(solution)/shard_map/ppermute | solution.py:288
  147.5 3.7 %shard_map.113 = (bf16[512,512]{1,0:T(8,128)(2,1)S(1)}, f32[512,128]{1,0:T(8,128)S(1)}, bf16[8,2,16,2176]{3,2,1,0:T(8,128)(2,1)}) custom-call(bf16[8,2,32,1024]{3,2,1,0:T(8,128)(2,1)S(1)} %bitcast.20, bf16[8,2,32,1024]{3,2,1,0:T(8,128)(2,1)S(1)} %collective-permute-done.other, bf16[256,1024]{1,0:T(8,128)(2,1)S(1)} %bitcast.32, ...), custom_call_target="tpu_custom_call" | custom-call | flops 1073741824 | bytes 8454144 | tf_op jit(solution)/shard_map/pallas_call | solution.py:22
  154.9 3.1 %collective-permute-start.6 = (bf16[128,1024]{1,0:T(8,128)(2,1)S(1)}, bf16[128,1024]{1,0:T(8,128)(2,1)}, u32[]{:S(2)}, u32[]{:S(2)}) collective-permute-start(bf16[128,1024]{1,0:T(8,128)(2,1)S(1)} %slice_bitcast_fusion), channel_id=1, source_target_pairs={{0,1},{1,0},{2,3},{3,2},{4,5},{5,4},{6,7},{7,6},{8,9},{9,8},{10,11... | collective-permute-start | bytes 786440 | tf_op jit(solution)/shard_map/ppermute | solution.py:291
  158.0 24.8 %collective-permute-done.6.other_ref = bf16[128,1024]{1,0:T(8,128)(2,1)} collective-permute-done((bf16[128,1024]{1,0:T(8,128)(2,1)S(1)}, bf16[128,1024]{1,0:T(8,128)(2,1)}, u32[]{:S(2)}, u32[]{:S(2)}) %collective-permute-start.6) | collective-permute-done | bytes 262176 | tf_op jit(solution)/shard_map/ppermute | solution.py:291
  184.7 7.3 %collective-permute-start.7 = (bf16[144,1024]{1,0:T(8,128)(2,1)}, bf16[144,1024]{1,0:T(8,128)(2,1)}, u32[]{:S(2)}, u32[]{:S(2)}) collective-permute-start(bf16[144,1024]{1,0:T(8,128)(2,1)} %shard_map.116), channel_id=1, source_target_pairs={{0,256},{32,288},{64,320},{96,352},{128,384},{160,416},{192,448},{... | collective-permute-start | bytes 884744 | tf_op jit(solution)/shard_map/ppermute | solution.py:288
  192.1 7.3 %collective-permute-done.7.piece_ref = bf16[144,1024]{1,0:T(8,128)(2,1)} collective-permute-done((bf16[144,1024]{1,0:T(8,128)(2,1)}, bf16[144,1024]{1,0:T(8,128)(2,1)}, u32[]{:S(2)}, u32[]{:S(2)}) %collective-permute-start.7) | collective-permute-done | bytes 294944 | tf_op jit(solution)/shard_map/ppermute | solution.py:288
  201.6 17.6 %all-to-all-start.3 = ((bf16[16,16,1024]{2,1,0:T(8,128)(2,1)}), bf16[16,16,1024]{2,1,0:T(8,128)(2,1)}, u32[]{:S(2)}, u32[]{:S(2)}) async-start(bf16[16,16,1024]{2,1,0:T(8,128)(2,1)} %shard_map.117), calls=%async_computation.3 | async-start | bytes 1048576 | tf_op jit(solution)/shard_map/all_to_all | solution.py:264
  233.6 6.1 %all-to-all-start.2 = ((bf16[16,16,2176]{2,1,0:T(8,128)(2,1)}), bf16[16,16,2176]{2,1,0:T(8,128)(2,1)S(1)}, u32[]{:S(2)}, u32[]{:S(2)}) async-start(bf16[16,16,2176]{2,1,0:T(8,128)(2,1)} %bitcast.39), calls=%async_computation.2 | async-start | bytes 2228224 | tf_op jit(solution)/shard_map/all_to_all | solution.py:264
  239.7 3.7 %collective-permute-start.8 = (bf16[8,2,16,1024]{3,2,1,0:T(8,128)(2,1)}, bf16[8,2,16,1024]{3,2,1,0:T(8,128)(2,1)S(1)}, u32[]{:S(2)}, u32[]{:S(2)}) collective-permute-start(bf16[8,2,16,1024]{3,2,1,0:T(8,128)(2,1)} %bitcast.13.own), channel_id=1, source_target_pairs={{0,1},{1,0},{2,3},{3,2},{4,5},{5,4},{6,7},{7,6},{8,9},{9,8},{10,11... | collective-permute-start | bytes 1572872 | tf_op jit(solution)/shard_map/ppermute | solution.py:291
  243.5 7.1 %collective-permute-start.9 = (bf16[512,512]{1,0:T(8,128)(2,1)}, bf16[512,512]{1,0:T(8,128)(2,1)S(1)}, u32[]{:S(2)}, u32[]{:S(2)}) collective-permute-start(bf16[512,512]{1,0:T(8,128)(2,1)} %copy-done.13), channel_id=1, source_target_pairs={{0,256},{32,288},{64,320},{96,352},{128,384},{160,416},{192,448},{... | collective-permute-start | bytes 1572872 | tf_op jit(solution)/shard_map/ppermute | solution.py:288
  255.5 23.3 %collective-permute-done.9.d = bf16[512,512]{1,0:T(8,128)(2,1)S(1)} collective-permute-done((bf16[512,512]{1,0:T(8,128)(2,1)}, bf16[512,512]{1,0:T(8,128)(2,1)S(1)}, u32[]{:S(2)}, u32[]{:S(2)}) %collective-permute-start.9) | collective-permute-done | bytes 524320 | tf_op jit(solution)/shard_map/ppermute | solution.py:288
  280.4 9.5 %collective-permute-done.10 = bf16[256,1024]{1,0:T(8,128)(2,1)S(1)} collective-permute-done((bf16[256,1024]{1,0:T(8,128)(2,1)S(1)}, bf16[256,1024]{1,0:T(8,128)(2,1)S(1)}, u32[]{:S(2)}, u32[]{:S(2)}) %collective-permute-start.10) | collective-permute-done | bytes 524320 | tf_op jit(solution)/shard_map/ppermute | solution.py:288
  (60 shorter events, 37.6 us)
Async XLA Ops:
  3.3 35.6 %all-to-all-start.1 = ((bf16[16,2,16,1024]{3,2,1,0:T(8,128)(2,1)}), bf16[16,2,16,1024]{3,2,1,0:T(8,128)(2,1)}, u32[]{:S(2)}, u32[]{:S(2)}) async-start(bf16[16,2,16,1024]{3,2,1,0:T(8,128)(2,1)} %shard_map.111), calls=%async_computation.1 | async-start | bytes 2097152 | tf_op jit(solution)/shard_map/all_to_all | solution.py:264
  17.1 57.8 %copy-start = (bf16[1,1,1024,256]{3,2,1,0:T(8,128)(2,1)S(1)}, bf16[1,1,1024,256]{3,2,1,0:T(8,128)(2,1)}, u32[]{:S(2)}) copy-start(bf16[1,1,1024,256]{3,2,1,0:T(8,128)(2,1)} %param.11) | copy-start | bytes 1572868
  17.1 64.4 %copy-start.1 = (bf16[1,1,1024,256]{3,2,1,0:T(8,128)(2,1)S(1)}, bf16[1,1,1024,256]{3,2,1,0:T(8,128)(2,1)}, u32[]{:S(2)}) copy-start(bf16[1,1,1024,256]{3,2,1,0:T(8,128)(2,1)} %param.12) | copy-start | bytes 1572868
  38.9 30.8 %all-to-all-start = ((bf16[16,2,16,1024]{3,2,1,0:T(8,128)(2,1)}), bf16[16,2,16,1024]{3,2,1,0:T(8,128)(2,1)S(1)}, u32[]{:S(2)}, u32[]{:S(2)}) async-start(bf16[16,2,16,1024]{3,2,1,0:T(8,128)(2,1)} %shard_map.110), calls=%async_computation | async-start | bytes 2097152 | tf_op jit(solution)/shard_map/all_to_all | solution.py:264
  46.3 77.1 %collective-permute-start.1 = (bf16[8,2,32,1024]{3,2,1,0:T(8,128)(2,1)}, bf16[8,2,32,1024]{3,2,1,0:T(8,128)(2,1)}, u32[]{:S(2)}, u32[]{:S(2)}) collective-permute-start(bf16[8,2,32,1024]{3,2,1,0:T(8,128)(2,1)} %bitcast.5.own), channel_id=1, source_target_pairs={{0,1},{1,0},{2,3},{3,2},{4,5},{5,4},{6,7},{7,6},{8,9},{9,8},{10,11... | collective-permute-start | bytes 3145736 | tf_op jit(solution)/shard_map/ppermute | solution.py:291
  69.7 77.8 %collective-permute-start = (bf16[8,2,32,1024]{3,2,1,0:T(8,128)(2,1)S(1)}, bf16[8,2,32,1024]{3,2,1,0:T(8,128)(2,1)S(1)}, u32[]{:S(2)}, u32[]{:S(2)}) collective-permute-start(bf16[8,2,32,1024]{3,2,1,0:T(8,128)(2,1)S(1)} %bitcast.19), channel_id=1, source_target_pairs={{0,1},{1,0},{2,3},{3,2},{4,5},{5,4},{6,7},{7,6},{8,9},{9,8},{10,11... | collective-permute-start | bytes 3145736 | tf_op jit(solution)/shard_map/ppermute | solution.py:291
  74.9 24.3 %collective-permute-start.2 = (bf16[1024,256]{1,0:T(8,128)(2,1)S(1)}, bf16[1024,256]{1,0:T(8,128)(2,1)S(1)}, u32[]{:S(2)}, u32[]{:S(2)}) collective-permute-start(bf16[1024,256]{1,0:T(8,128)(2,1)S(1)} %bitcast.23), channel_id=1, source_target_pairs={{0,256},{32,288},{64,320},{96,352},{128,384},{160,416},{192,448},{... | collective-permute-start | bytes 1572872 | tf_op jit(solution)/shard_map/ppermute | solution.py:288
  81.5 41.9 %collective-permute-start.3 = (bf16[1024,256]{1,0:T(8,128)(2,1)S(1)}, bf16[1024,256]{1,0:T(8,128)(2,1)S(1)}, u32[]{:S(2)}, u32[]{:S(2)}) collective-permute-start(bf16[1024,256]{1,0:T(8,128)(2,1)S(1)} %bitcast.27), channel_id=1, source_target_pairs={{0,256},{32,288},{64,320},{96,352},{128,384},{160,416},{192,448},{... | collective-permute-start | bytes 1572872 | tf_op jit(solution)/shard_map/ppermute | solution.py:288
  84.1 63.3 %copy-start.12 = (bf16[1,1,256,1024]{3,2,1,0:T(8,128)(2,1)S(1)}, bf16[1,1,256,1024]{3,2,1,0:T(8,128)(2,1)}, u32[]{:S(2)}) copy-start(bf16[1,1,256,1024]{3,2,1,0:T(8,128)(2,1)} %param.13) | copy-start | bytes 1572868
  84.2 63.3 %collective-permute-start.4 = (bf16[256,1024]{1,0:T(8,128)(2,1)}, bf16[256,1024]{1,0:T(8,128)(2,1)S(1)}, u32[]{:S(2)}, u32[]{:S(2)}) collective-permute-start(bf16[256,1024]{1,0:T(8,128)(2,1)} %bitcast.31), channel_id=1, source_target_pairs={{0,256},{32,288},{64,320},{96,352},{128,384},{160,416},{192,448},{... | collective-permute-start | bytes 1572872 | tf_op jit(solution)/shard_map/ppermute | solution.py:288
  99.3 48.2 %copy-start.2 = (bf16[1024,256]{1,0:T(8,128)(2,1)}, bf16[1024,256]{1,0:T(8,128)(2,1)S(1)}, u32[]{:S(2)}) copy-start(bf16[1024,256]{1,0:T(8,128)(2,1)S(1)} %collective-permute-done.2.wgo) | copy-start | bytes 1572868
  123.4 24.1 %copy-start.4 = (bf16[1024,256]{1,0:T(8,128)(2,1)}, bf16[1024,256]{1,0:T(8,128)(2,1)S(1)}, u32[]{:S(2)}) copy-start(bf16[1024,256]{1,0:T(8,128)(2,1)S(1)} %collective-permute-done.3.wuo) | copy-start | bytes 1572868
  152.7 76.0 %collective-permute-start.5 = (bf16[8,2,16,2176]{3,2,1,0:T(8,128)(2,1)}, bf16[8,2,16,2176]{3,2,1,0:T(8,128)(2,1)}, u32[]{:S(2)}, u32[]{:S(2)}) collective-permute-start(bf16[8,2,16,2176]{3,2,1,0:T(8,128)(2,1)} %get-tuple-element.28), channel_id=1, source_target_pairs={{0,1},{1,0},{2,3},{3,2},{4,5},{5,4},{6,7},{7,6},{8,9},{9,8},{10,11... | collective-permute-start | bytes 3342344 | tf_op jit(solution)/shard_map/ppermute | solution.py:291
  154.9 27.9 %collective-permute-start.6 = (bf16[128,1024]{1,0:T(8,128)(2,1)S(1)}, bf16[128,1024]{1,0:T(8,128)(2,1)}, u32[]{:S(2)}, u32[]{:S(2)}) collective-permute-start(bf16[128,1024]{1,0:T(8,128)(2,1)S(1)} %slice_bitcast_fusion), channel_id=1, source_target_pairs={{0,1},{1,0},{2,3},{3,2},{4,5},{5,4},{6,7},{7,6},{8,9},{9,8},{10,11... | collective-permute-start | bytes 786440 | tf_op jit(solution)/shard_map/ppermute | solution.py:291
  184.7 14.7 %collective-permute-start.7 = (bf16[144,1024]{1,0:T(8,128)(2,1)}, bf16[144,1024]{1,0:T(8,128)(2,1)}, u32[]{:S(2)}, u32[]{:S(2)}) collective-permute-start(bf16[144,1024]{1,0:T(8,128)(2,1)} %shard_map.116), channel_id=1, source_target_pairs={{0,256},{32,288},{64,320},{96,352},{128,384},{160,416},{192,448},{... | collective-permute-start | bytes 884744 | tf_op jit(solution)/shard_map/ppermute | solution.py:288
  201.6 32.0 %all-to-all-start.3 = ((bf16[16,16,1024]{2,1,0:T(8,128)(2,1)}), bf16[16,16,1024]{2,1,0:T(8,128)(2,1)}, u32[]{:S(2)}, u32[]{:S(2)}) async-start(bf16[16,16,1024]{2,1,0:T(8,128)(2,1)} %shard_map.117), calls=%async_computation.3 | async-start | bytes 1048576 | tf_op jit(solution)/shard_map/all_to_all | solution.py:264
  233.6 57.3 %all-to-all-start.2 = ((bf16[16,16,2176]{2,1,0:T(8,128)(2,1)}), bf16[16,16,2176]{2,1,0:T(8,128)(2,1)S(1)}, u32[]{:S(2)}, u32[]{:S(2)}) async-start(bf16[16,16,2176]{2,1,0:T(8,128)(2,1)} %bitcast.39), calls=%async_computation.2 | async-start | bytes 2228224 | tf_op jit(solution)/shard_map/all_to_all | solution.py:264
  239.7 14.3 %collective-permute-start.8 = (bf16[8,2,16,1024]{3,2,1,0:T(8,128)(2,1)}, bf16[8,2,16,1024]{3,2,1,0:T(8,128)(2,1)S(1)}, u32[]{:S(2)}, u32[]{:S(2)}) collective-permute-start(bf16[8,2,16,1024]{3,2,1,0:T(8,128)(2,1)} %bitcast.13.own), channel_id=1, source_target_pairs={{0,1},{1,0},{2,3},{3,2},{4,5},{5,4},{6,7},{7,6},{8,9},{9,8},{10,11... | collective-permute-start | bytes 1572872 | tf_op jit(solution)/shard_map/ppermute | solution.py:291
  243.5 35.3 %collective-permute-start.9 = (bf16[512,512]{1,0:T(8,128)(2,1)}, bf16[512,512]{1,0:T(8,128)(2,1)S(1)}, u32[]{:S(2)}, u32[]{:S(2)}) collective-permute-start(bf16[512,512]{1,0:T(8,128)(2,1)} %copy-done.13), channel_id=1, source_target_pairs={{0,256},{32,288},{64,320},{96,352},{128,384},{160,416},{192,448},{... | collective-permute-start | bytes 1572872 | tf_op jit(solution)/shard_map/ppermute | solution.py:288
  251.1 27.6 %copy-start.7 = (f32[2,1024,256]{2,1,0:T(8,128)S(1)}, f32[2,1024,256]{2,1,0:T(8,128)}, u32[]{:S(2)}) copy-start(f32[2,1024,256]{2,1,0:T(8,128)} %copy-done.6) | copy-start | bytes 6291460
  251.2 38.8 %collective-permute-start.10 = (bf16[256,1024]{1,0:T(8,128)(2,1)S(1)}, bf16[256,1024]{1,0:T(8,128)(2,1)S(1)}, u32[]{:S(2)}, u32[]{:S(2)}) collective-permute-start(bf16[256,1024]{1,0:T(8,128)(2,1)S(1)} %shard_map.120), channel_id=1, source_target_pairs={{0,256},{32,288},{64,320},{96,352},{128,384},{160,416},{192,448},{... | collective-permute-start | bytes 1572872 | tf_op jit(solution)/shard_map/ppermute | solution.py:288
  278.7 11.2 %copy-start.9 = (f32[256,1024]{1,0:T(8,128)S(1)}, f32[256,1024]{1,0:T(8,128)}, u32[]{:S(2)}) copy-start(f32[256,1024]{1,0:T(8,128)} %copy-done.8) | copy-start | bytes 3145732
  280.4 10.5 %copy-start.17 = (s32[1,2,1,16]{3,2,1,0:T(1,128)S(1)}, s32[1,2,1,16]{3,2,1,0:T(1,128)}, u32[]{:S(2)}) copy-start(s32[1,2,1,16]{3,2,1,0:T(1,128)} %param.10) | copy-start | bytes 388
  280.4 10.5 %copy-start.18 = (bf16[1,2,128]{2,1,0:T(2,128)(2,1)S(1)}, bf16[1,2,128]{2,1,0:T(2,128)(2,1)}, u32[]{:S(2)}) copy-start(bf16[1,2,128]{2,1,0:T(2,128)(2,1)} %param.9) | copy-start | bytes 1540
  (11 other events, 17.6 us)

commit v5 on v4

--- a/solution.py
+++ b/solution.py
@@ -65,18 +65,23 @@
         out_ref[:, d] = packed.reshape(experts, slots, width)
 
 
-def unpack_body(counts_ref, probs_ref, filled, out_ref, prob_ref, slots_ref, sem):
-    copy = pltpu.make_async_copy(filled, slots_ref, sem)
-    copy.start()
-    experts, slots, _ = slots_ref.shape
-    dirs, rows, width = out_ref.shape
+def unpack_body(counts_ref, probs_ref, first, second, out_ref, prob_ref, first_ref, second_ref, sems):
+    copies = [
+        pltpu.make_async_copy(first, first_ref, sems.at[0]),
+        pltpu.make_async_copy(second, second_ref, sems.at[1]),
+    ]
+    for c in copies:
+        c.start()
+    experts, slots, width = second_ref.shape
+    dirs, rows, _ = out_ref.shape
     masks = [
         slot_choice(counts_ref[d : d + 1, :], slots, rows).astype(BF) for d in range(dirs)
     ]
-    copy.wait()
-    terms = slots_ref[:, :, dirs * width :].reshape(experts * slots, LANES)
-    for d in range(dirs):
-        part = slots_ref[:, :, d * width : (d + 1) * width].reshape(experts * slots, width)
+    for c in copies:
+        c.wait()
+    terms = first_ref[:, :, width:].reshape(experts * slots, LANES)
+    for d, ref in enumerate((first_ref, second_ref)):
+        part = ref[:, :, :width].reshape(experts * slots, width)
         out_ref[d] = dot(masks[d], part, 0, 0).astype(BF)
         found = dot(terms, masks[d], 0, 0)[d : d + 1, :]
         prob_ref[d : d + 1, :] = (found / probs_ref[d : d + 1, :].astype(F32)).astype(BF)
@@ -158,29 +163,27 @@
     down_ref[...] = dot(act_t[...], flat(half), 1, 0).astype(BF)
 
 
-def row_terms(d, gate_sides, up_sides, prob, out_ref, swapped):
-    blocks, _, slots, lanes = out_ref.shape
-    width = gate_sides[0].shape[0]
-    dirs = lanes // width
-    half = blocks * dirs * slots
+def row_terms(d, gate_sides, up_sides, prob, first_ref, second_ref, swapped):
+    blocks, _, slots, width = second_ref.shape
+    half = 2 * blocks * slots
     hidden = gate_sides[0].shape[1]
     lane = lax.broadcasted_iota(jnp.int32, (blocks, slots, LANES), 2)
+    kind = second_ref.dtype
     for side in range(2):
         use = side ^ swapped
         part = d[side * half : (side + 1) * half]
         term = dot(part[:, :hidden], gate_sides[use], 1, 1) + dot(part[:, hidden:], up_sides[use], 1, 1)
-        term = term.astype(out_ref.dtype).reshape(blocks, dirs, slots, width)
+        term = term.astype(kind).reshape(blocks, 2, slots, width)
+        first_ref[:, side, :, :width] = term[:, 0]
+        second_ref[:, side] = term[:, 1]
         spread = jnp.broadcast_to(prob[side * half : (side + 1) * half], (half, LANES))
-        spread = spread.reshape(blocks, dirs, slots, LANES)
-        extra = jnp.zeros((blocks, slots, LANES), F32)
-        for k in range(dirs):
-            out_ref[:, side, :, k * width : (k + 1) * width] = term[:, k]
-            extra = jnp.where(lane == k, spread[:, k], extra)
-        out_ref[:, side, :, dirs * width :] = extra.astype(out_ref.dtype)
+        spread = spread.reshape(blocks, 2, slots, LANES)
+        extra = jnp.where(lane == 0, spread[:, 0], jnp.where(lane == 1, spread[:, 1], 0.0))
+        first_ref[:, side, :, width:] = extra.astype(kind)
 
 
 def slope_body(
-    own, other, wd, wdo, act, silu, slope, wg, wgo, wu, wuo, d_ref, prob_ref, row_ref, low, high, sems
+    own, other, wd, wdo, act, silu, slope, wg, wgo, wu, wuo, d_ref, prob_ref, first_ref, second_ref, low, high, sems
 ):
     copies = row_copies(own, other, low, high, sems)
     for c in copies:
@@ -196,7 +199,7 @@
     d_ref[...] = d
     prob = jnp.sum(act[...].astype(F32) * back, axis=1, keepdims=True)
     prob_ref[...] = jnp.broadcast_to(prob, prob_ref.shape)
-    row_terms(d, weight_sides(same, wg, wgo), weight_sides(same, wu, wuo), prob, row_ref, 1)
+    row_terms(d, weight_sides(same, wg, wgo), weight_sides(same, wu, wuo), prob, first_ref, second_ref, 1)
 
 
 def piece_body(counts_ref, values_ref, other_ref, out_ref):
@@ -241,14 +244,21 @@
     up_ref[...] = (keep[1] + both[:, hidden:]).astype(BF)
 
 
-def keep_body(
-    own, other, x_t, act_t, d, prob, wg, wgo, wu, wuo, row_ref, grad_ref, down_ref, half, sems
-):
+def row_keep_body(d, prob, wg, wgo, wu, wuo, first_ref, second_ref):
     same = keeps_low()
-    waits = half_copies(own, other, same, half, sems)
     row_terms(
-        d[...], weight_sides(same, wg, wgo), weight_sides(same, wu, wuo), prob[:, 0:1], row_ref, 0
-    )
+        d[...],
+        weight_sides(same, wg, wgo),
+        weight_sides(same, wu, wuo),
+        prob[:, 0:1],
+        first_ref,
+        second_ref,
+        0,
+    )
+
+
+def keep_body(own, other, x_t, act_t, d, grad_ref, down_ref, half, sems):
+    waits = half_copies(own, other, keeps_low(), half, sems)
     both = dot(x_t[...], d[...], 1, 0)
     hidden = grad_ref.shape[2]
     grad_ref[0] = both[:, :hidden]
@@ -290,7 +300,7 @@
     def swap(array):
         return lax.ppermute(array, "tensor", [(0, 1), (1, 0)])
 
-    late = ("hidden", "down", "slope", "keep", "turn", "final", "unpack")
+    late = ("hidden", "down", "slope", "rowkeep", "keep", "turn", "final", "unpack")
 
     def kernel(name, body, outs, args, flops, in_place=(), scratch=()):
         limit = 24 * 1024 * 1024 if name in late else None
@@ -299,7 +309,8 @@
 
     side_rows = pltpu.VMEM((2, experts // 2, dirs * slots, width), BF)
     sems = pltpu.SemaphoreType.DMA
-    carried = (experts // 2, 2, slots, dirs * width + LANES)
+    firsts = (experts // 2, 2, slots, width + LANES)
+    seconds = (experts // 2, 2, slots, width)
 
     (x_send,) = kernel("packx", pack_body, [packed], (count_rows, acts[0]), work)
     x_own = dispatch(x_send).reshape(sided.shape)
@@ -343,16 +354,29 @@
         (side_rows, sems((2,))),
     )
     down_got = mirror(down_send)
-    d, prob, row_send = kernel(
+    d, prob, first_send, second_send = kernel(
         "slope",
         slope_body,
-        [shape((total, 2 * hidden), BF), shape((total, LANES), F32), shape(carried, BF)],
+        [
+            shape((total, 2 * hidden), BF),
+            shape((total, LANES), F32),
+            shape(firsts, BF),
+            shape(seconds, BF),
+        ],
         (g_own, g_other, wd, wdo, act, silu, slope, wg, wgo, wu, wuo),
         4 * one,
         (0, 1),
         (side_rows, side_rows, sems((4,))),
     )
-    row_got = swap(row_send)
+    first_got = swap(first_send)
+    second_got = swap(second_send)
+    first_keep, second_keep = kernel(
+        "rowkeep",
+        row_keep_body,
+        [shape(firsts, F32), shape(seconds, F32)],
+        (d, prob, wg, wgo, wu, wuo),
+        2 * one,
+    )
     d_got = mirror(d)
     (m_t,) = kernel(
         "turn",
@@ -363,12 +387,12 @@
         (0, 1),
         (pltpu.VMEM((2, experts // 2, dirs, slots, width), BF), sems((4,))),
     )
-    row_keep, grad_keep, down_keep = kernel(
+    grad_keep, down_keep = kernel(
         "keep",
         keep_body,
-        [shape(carried, F32), shape((2, width, hidden), F32), shape((hidden, width), F32)],
-        (g_own, g_other, x_keep_t, act_t, d, prob, wg, wgo, wu, wuo),
-        5 * one,
+        [shape((2, width, hidden), F32), shape((hidden, width), F32)],
+        (g_own, g_other, x_keep_t, act_t, d),
+        3 * one,
         (0, 1),
         (side_rows, sems((2,))),
     )
@@ -379,16 +403,21 @@
         (m_t, d_got, grad_keep),
         2 * one,
     )
-    row_sum = (row_keep + row_got.astype(F32)).astype(BF).reshape(experts, *carried[2:])
-    row_back = dispatch(row_sum)
+
+    def returned(keep, got):
+        summed = (keep + got.astype(F32)).astype(BF).reshape(experts, *keep.shape[2:])
+        return dispatch(summed)
+
+    first_back = returned(first_keep, first_got)
+    second_back = returned(second_keep, second_got)
     act_grad, prob_grad = kernel(
         "unpack",
         unpack_body,
         [shape((dirs, rows, width), BF), shape((dirs, rows), BF)],
-        (count_rows, probs[0], row_back),
+        (count_rows, probs[0], first_back, second_back),
         work,
-        (2,),
-        (pltpu.VMEM(row_back.shape, BF), sems(())),
+        (2, 3),
+        (pltpu.VMEM(first_back.shape, BF), pltpu.VMEM(second_back.shape, BF), sems((2,))),
     )
     return (
         act_grad[None],

time: 294 us -> 273 us (0.929)
  the two profiles are of different devices: /device:TPU:13 before, /device:TPU:4 now
where the time goes in v5:
time: 273 us; the launch traced here: 272 us
  waiting for transfers between devices  134 us (49%)
  starting transfers between devices  102 us (37%)
  Pallas kernels  26.8 us (10%)
  other arithmetic  4.22 us (2%)
  local copies, waits for them, and re-layouts  3.49 us (1%)
    ppermute x6, waiting for transfers between devices, mirror(): lax.ppermute(array, 'pipe', [(i, (i + pipes // 2) % pipes) for i in range...  70.7 us
    all_to_all x5, waiting for transfers between devices, dispatch(): lax.all_to_all(array, ('expert', 'tensor'), 0, 0, axis_index_groups=group...  52.4 us
    all_to_all x5, starting transfers between devices, dispatch(): lax.all_to_all(array, ('expert', 'tensor'), 0, 0, axis_index_groups=group...  38.3 us
    ppermute x6, starting transfers between devices, mirror(): lax.ppermute(array, 'pipe', [(i, (i + pipes // 2) % pipes) for i in range...  38.2 us
    pallas_call x12, Pallas kernels, call(): pl.pallas_call(body, out_shape=tuple(outs), in_specs=in_specs, out_specs=...  26.8 us
    ppermute x6, starting transfers between devices, swap(): return lax.ppermute(array, 'tensor', [(0, 1), (1, 0)])  26 us
    ppermute x6, waiting for transfers between devices, swap(): return lax.ppermute(array, 'tensor', [(0, 1), (1, 0)])  11.1 us
  transfers between devices with their start and end apart: 17, of which 10 were waited for; matrix products, arithmetic and copies ran while one was open for 2% of the time, Pallas kernels for 8%

profile of v5, /device:TPU:4, one launch (start us, length us, event | category | flops | bytes accessed | tf_op | source)
XLA Modules:
  0.0 272.1 jit_solution(9038606759019983400)
XLA Ops:
  3.2 11.8 %all-to-all-start.1 = ((bf16[16,2,16,1024]{3,2,1,0:T(8,128)(2,1)}), bf16[16,2,16,1024]{3,2,1,0:T(8,128)(2,1)}, u32[]{:S(2)}, u32[]{:S(2)}) async-start(bf16[16,2,16,1024]{3,2,1,0:T(8,128)(2,1)} %shard_map.111), calls=%async_computation.1 | async-start | bytes 2097152 | tf_op jit(solution)/shard_map/all_to_all | solution.py:274
  17.7 24.7 %all-to-all-done.1 = bf16[16,2,16,1024]{3,2,1,0:T(8,128)(2,1)} async-done(((bf16[16,2,16,1024]{3,2,1,0:T(8,128)(2,1)}), bf16[16,2,16,1024]{3,2,1,0:T(8,128)(2,1)}, u32[]{:S(2)}, u32[]{:S(2)}) %all-to-all-start.1) | async-done | bytes 1048608 | tf_op jit(solution)/shard_map/all_to_all | solution.py:274
  42.3 5.1 %all-to-all-start = ((bf16[16,2,16,1024]{3,2,1,0:T(8,128)(2,1)}), bf16[16,2,16,1024]{3,2,1,0:T(8,128)(2,1)S(1)}, u32[]{:S(2)}, u32[]{:S(2)}) async-start(bf16[16,2,16,1024]{3,2,1,0:T(8,128)(2,1)} %shard_map.110), calls=%async_computation | async-start | bytes 2097152 | tf_op jit(solution)/shard_map/all_to_all | solution.py:274
  47.4 5.7 %collective-permute-start.2 = (bf16[8,2,32,1024]{3,2,1,0:T(8,128)(2,1)}, bf16[8,2,32,1024]{3,2,1,0:T(8,128)(2,1)}, u32[]{:S(2)}, u32[]{:S(2)}) collective-permute-start(bf16[8,2,32,1024]{3,2,1,0:T(8,128)(2,1)} %bitcast.6.own), channel_id=1, source_target_pairs={{0,1},{1,0},{2,3},{3,2},{4,5},{5,4},{6,7},{7,6},{8,9},{9,8},{10,11... | collective-permute-start | bytes 3145736 | tf_op jit(solution)/shard_map/ppermute | solution.py:301
  55.7 18.4 %all-to-all-done = bf16[16,2,16,1024]{3,2,1,0:T(8,128)(2,1)S(1)} async-done(((bf16[16,2,16,1024]{3,2,1,0:T(8,128)(2,1)}), bf16[16,2,16,1024]{3,2,1,0:T(8,128)(2,1)S(1)}, u32[]{:S(2)}, u32[]{:S(2)}) %all-to-all-start) | async-done | bytes 1048608 | tf_op jit(solution)/shard_map/all_to_all | solution.py:274
  74.1 5.5 %collective-permute-start = (bf16[8,2,32,1024]{3,2,1,0:T(8,128)(2,1)S(1)}, bf16[8,2,32,1024]{3,2,1,0:T(8,128)(2,1)S(1)}, u32[]{:S(2)}, u32[]{:S(2)}) collective-permute-start(bf16[8,2,32,1024]{3,2,1,0:T(8,128)(2,1)S(1)} %bitcast.20), channel_id=1, source_target_pairs={{0,1},{1,0},{2,3},{3,2},{4,5},{5,4},{6,7},{7,6},{8,9},{9,8},{10,11... | collective-permute-start | bytes 3145736 | tf_op jit(solution)/shard_map/ppermute | solution.py:301
  85.5 7.7 %collective-permute-start.8 = (bf16[144,1024]{1,0:T(8,128)(2,1)}, bf16[144,1024]{1,0:T(8,128)(2,1)}, u32[]{:S(2)}, u32[]{:S(2)}) collective-permute-start(bf16[144,1024]{1,0:T(8,128)(2,1)} %shard_map.116), channel_id=1, source_target_pairs={{0,256},{32,288},{64,320},{96,352},{128,384},{160,416},{192,448},{... | collective-permute-start | bytes 884744 | tf_op jit(solution)/shard_map/ppermute | solution.py:298
  95.3 7.7 %collective-permute-start.4 = (bf16[1024,256]{1,0:T(8,128)(2,1)S(1)}, bf16[1024,256]{1,0:T(8,128)(2,1)}, u32[]{:S(2)}, u32[]{:S(2)}) collective-permute-start(bf16[1024,256]{1,0:T(8,128)(2,1)S(1)} %bitcast.28), channel_id=1, source_target_pairs={{0,256},{32,288},{64,320},{96,352},{128,384},{160,416},{192,448},{... | collective-permute-start | bytes 1572872 | tf_op jit(solution)/shard_map/ppermute | solution.py:298
  103.2 10.8 %collective-permute-start.1 = (bf16[256,1024]{1,0:T(8,128)(2,1)}, bf16[256,1024]{1,0:T(8,128)(2,1)}, u32[]{:S(2)}, u32[]{:S(2)}) collective-permute-start(bf16[256,1024]{1,0:T(8,128)(2,1)} %bitcast.32), channel_id=1, source_target_pairs={{0,256},{32,288},{64,320},{96,352},{128,384},{160,416},{192,448},{... | collective-permute-start | bytes 1572872 | tf_op jit(solution)/shard_map/ppermute | solution.py:298
  116.2 8.1 %all-to-all-start.4 = ((bf16[16,16,1024]{2,1,0:T(8,128)(2,1)}), bf16[16,16,1024]{2,1,0:T(8,128)(2,1)}, u32[]{:S(2)}, u32[]{:S(2)}) async-start(bf16[16,16,1024]{2,1,0:T(8,128)(2,1)} %shard_map.117), calls=%async_computation.4 | async-start | bytes 1048576 | tf_op jit(solution)/shard_map/all_to_all | solution.py:274
  124.3 25.3 %collective-permute-done.4.wuo = bf16[1024,256]{1,0:T(8,128)(2,1)} collective-permute-done((bf16[1024,256]{1,0:T(8,128)(2,1)S(1)}, bf16[1024,256]{1,0:T(8,128)(2,1)}, u32[]{:S(2)}, u32[]{:S(2)}) %collective-permute-start.4) | collective-permute-done | bytes 524320 | tf_op jit(solution)/shard_map/ppermute | solution.py:298
  149.6 4.2 %shard_map.112 = (bf16[512,256]{1,0:T(8,128)(2,1)S(1)}, bf16[256,512]{1,0:T(8,128)(2,1)S(1)}, f32[512,256]{1,0:T(8,128)S(1)}, f32[512,256]{1,0:T(8,128)S(1)}, bf16[1024,512]{1,0:T(8,128)(2,1)S(1)}) custom-call(bf16[8,2,32,1024]{3,2,1,0:T(8,128)(2,1)} %bitcast.6.own, bf16[8,2,32,1024]{3,2,1,0:T(8,128)(2,1)} %collective-permute-done.2.other, ...), custom_call_target="tpu_custom_call" | custom-call | flops 1073741824 | bytes 6815744 | tf_op jit(solution)/shard_map/pallas_call | solution.py:22
  154.7 16.0 %collective-permute-done.1.wdo = bf16[256,1024]{1,0:T(8,128)(2,1)} collective-permute-done((bf16[256,1024]{1,0:T(8,128)(2,1)}, bf16[256,1024]{1,0:T(8,128)(2,1)}, u32[]{:S(2)}, u32[]{:S(2)}) %collective-permute-start.1) | collective-permute-done | bytes 524320 | tf_op jit(solution)/shard_map/ppermute | solution.py:298
  170.8 4.8 %shard_map.113 = (bf16[512,512]{1,0:T(8,128)(2,1)S(1)}, f32[512,128]{1,0:T(8,128)S(1)}, bf16[8,2,16,1152]{3,2,1,0:T(8,128)(2,1)}, bf16[8,2,16,1024]{3,2,1,0:T(8,128)(2,1)S(1)}) custom-call(bf16[8,2,32,1024]{3,2,1,0:T(8,128)(2,1)S(1)} %bitcast.21, bf16[8,2,32,1024]{3,2,1,0:T(8,128)(2,1)S(1)} %collective-permute-done.other, bf16[256,1024]{1,0:T(8,128)(2,1)S(1)} %bitcast.33, ...), custom_call_target="tpu_custom_call" | custom-call | flops 1073741824 | bytes 8454144 | tf_op jit(solution)/shard_map/pallas_call | solution.py:22
  175.6 4.7 %collective-permute-start.6 = (bf16[8,2,16,1024]{3,2,1,0:T(8,128)(2,1)S(1)}, bf16[8,2,16,1024]{3,2,1,0:T(8,128)(2,1)S(1)}, u32[]{:S(2)}, u32[]{:S(2)}) collective-permute-start(bf16[8,2,16,1024]{3,2,1,0:T(8,128)(2,1)S(1)} %get-tuple-element.30), channel_id=1, source_target_pairs={{0,1},{1,0},{2,3},{3,2},{4,5},{5,4},{6,7},{7,6},{8,9},{9,8},{10,11... | collective-permute-start | bytes 1572872 | tf_op jit(solution)/shard_map/ppermute | solution.py:301
  185.2 7.8 %collective-permute-done.6 = bf16[8,2,16,1024]{3,2,1,0:T(8,128)(2,1)S(1)} collective-permute-done((bf16[8,2,16,1024]{3,2,1,0:T(8,128)(2,1)S(1)}, bf16[8,2,16,1024]{3,2,1,0:T(8,128)(2,1)S(1)}, u32[]{:S(2)}, u32[]{:S(2)}) %collective-permute-start.6) | collective-permute-done | bytes 524320 | tf_op jit(solution)/shard_map/ppermute | solution.py:301
  194.0 8.2 %all-to-all-start.3 = ((bf16[16,16,1024]{2,1,0:T(8,128)(2,1)}), bf16[16,16,1024]{2,1,0:T(8,128)(2,1)S(1)}, u32[]{:S(2)}, u32[]{:S(2)}) async-start(bf16[16,16,1024]{2,1,0:T(8,128)(2,1)} %bitcast.10), calls=%async_computation.3 | async-start | bytes 1048576 | tf_op jit(solution)/shard_map/all_to_all | solution.py:274
  204.5 9.3 %all-to-all-done.3.second = bf16[16,16,1024]{2,1,0:T(8,128)(2,1)S(1)} async-done(((bf16[16,16,1024]{2,1,0:T(8,128)(2,1)}), bf16[16,16,1024]{2,1,0:T(8,128)(2,1)S(1)}, u32[]{:S(2)}, u32[]{:S(2)}) %all-to-all-start.3) | async-done | bytes 524320 | tf_op jit(solution)/shard_map/all_to_all | solution.py:274
  213.8 5.2 %all-to-all-start.2 = ((bf16[16,16,1152]{2,1,0:T(8,128)(2,1)}), bf16[16,16,1152]{2,1,0:T(8,128)(2,1)S(1)}, u32[]{:S(2)}, u32[]{:S(2)}) async-start(bf16[16,16,1152]{2,1,0:T(8,128)(2,1)} %bitcast.42), calls=%async_computation.2 | async-start | bytes 1179648 | tf_op jit(solution)/shard_map/all_to_all | solution.py:274
  219.1 6.3 %collective-permute-start.9 = (bf16[8,2,16,1024]{3,2,1,0:T(8,128)(2,1)}, bf16[8,2,16,1024]{3,2,1,0:T(8,128)(2,1)S(1)}, u32[]{:S(2)}, u32[]{:S(2)}) collective-permute-start(bf16[8,2,16,1024]{3,2,1,0:T(8,128)(2,1)} %bitcast.14.own), channel_id=1, source_target_pairs={{0,1},{1,0},{2,3},{3,2},{4,5},{5,4},{6,7},{7,6},{8,9},{9,8},{10,11... | collective-permute-start | bytes 1572872 | tf_op jit(solution)/shard_map/ppermute | solution.py:301
  225.4 6.6 %collective-permute-start.10 = (bf16[512,512]{1,0:T(8,128)(2,1)}, bf16[512,512]{1,0:T(8,128)(2,1)S(1)}, u32[]{:S(2)}, u32[]{:S(2)}) collective-permute-start(bf16[512,512]{1,0:T(8,128)(2,1)} %copy-done.2), channel_id=1, source_target_pairs={{0,256},{32,288},{64,320},{96,352},{128,384},{160,416},{192,448},{... | collective-permute-start | bytes 1572872 | tf_op jit(solution)/shard_map/ppermute | solution.py:298
  232.6 3.3 %collective-permute-start.11 = (bf16[256,1024]{1,0:T(8,128)(2,1)S(1)}, bf16[256,1024]{1,0:T(8,128)(2,1)S(1)}, u32[]{:S(2)}, u32[]{:S(2)}) collective-permute-start(bf16[256,1024]{1,0:T(8,128)(2,1)S(1)} %shard_map.121), channel_id=1, source_target_pairs={{0,256},{32,288},{64,320},{96,352},{128,384},{160,416},{192,448},{... | collective-permute-start | bytes 1572872 | tf_op jit(solution)/shard_map/ppermute | solution.py:298
  238.6 24.4 %collective-permute-done.10.d = bf16[512,512]{1,0:T(8,128)(2,1)S(1)} collective-permute-done((bf16[512,512]{1,0:T(8,128)(2,1)}, bf16[512,512]{1,0:T(8,128)(2,1)S(1)}, u32[]{:S(2)}, u32[]{:S(2)}) %collective-permute-start.10) | collective-permute-done | bytes 524320 | tf_op jit(solution)/shard_map/ppermute | solution.py:298
  264.7 4.7 %collective-permute-done.11 = bf16[256,1024]{1,0:T(8,128)(2,1)S(1)} collective-permute-done((bf16[256,1024]{1,0:T(8,128)(2,1)S(1)}, bf16[256,1024]{1,0:T(8,128)(2,1)S(1)}, u32[]{:S(2)}, u32[]{:S(2)}) %collective-permute-start.11) | collective-permute-done | bytes 524320 | tf_op jit(solution)/shard_map/ppermute | solution.py:298
  (50 shorter events, 34.9 us)
Async XLA Ops:
  3.2 39.1 %all-to-all-start.1 = ((bf16[16,2,16,1024]{3,2,1,0:T(8,128)(2,1)}), bf16[16,2,16,1024]{3,2,1,0:T(8,128)(2,1)}, u32[]{:S(2)}, u32[]{:S(2)}) async-start(bf16[16,2,16,1024]{3,2,1,0:T(8,128)(2,1)} %shard_map.111), calls=%async_computation.1 | async-start | bytes 2097152 | tf_op jit(solution)/shard_map/all_to_all | solution.py:274
  17.7 35.4 %copy-start.10 = (bf16[1,2,128,1024]{3,2,1,0:T(8,128)(2,1)S(1)}, bf16[1,2,128,1024]{3,2,1,0:T(8,128)(2,1)}, u32[]{:S(2)}) copy-start(bf16[1,2,128,1024]{3,2,1,0:T(8,128)(2,1)} %param.7) | copy-start | bytes 1572868
  42.3 31.8 %all-to-all-start = ((bf16[16,2,16,1024]{3,2,1,0:T(8,128)(2,1)}), bf16[16,2,16,1024]{3,2,1,0:T(8,128)(2,1)S(1)}, u32[]{:S(2)}, u32[]{:S(2)}) async-start(bf16[16,2,16,1024]{3,2,1,0:T(8,128)(2,1)} %shard_map.110), calls=%async_computation | async-start | bytes 2097152 | tf_op jit(solution)/shard_map/all_to_all | solution.py:274
  47.4 45.8 %copy-start = (bf16[1,1,1024,256]{3,2,1,0:T(8,128)(2,1)S(1)}, bf16[1,1,1024,256]{3,2,1,0:T(8,128)(2,1)}, u32[]{:S(2)}) copy-start(bf16[1,1,1024,256]{3,2,1,0:T(8,128)(2,1)} %param.11) | copy-start | bytes 1572868
  47.4 47.8 %copy-start.1 = (bf16[1,1,1024,256]{3,2,1,0:T(8,128)(2,1)S(1)}, bf16[1,1,1024,256]{3,2,1,0:T(8,128)(2,1)}, u32[]{:S(2)}) copy-start(bf16[1,1,1024,256]{3,2,1,0:T(8,128)(2,1)} %param.12) | copy-start | bytes 1572868
  47.4 102.2 %collective-permute-start.2 = (bf16[8,2,32,1024]{3,2,1,0:T(8,128)(2,1)}, bf16[8,2,32,1024]{3,2,1,0:T(8,128)(2,1)}, u32[]{:S(2)}, u32[]{:S(2)}) collective-permute-start(bf16[8,2,32,1024]{3,2,1,0:T(8,128)(2,1)} %bitcast.6.own), channel_id=1, source_target_pairs={{0,1},{1,0},{2,3},{3,2},{4,5},{5,4},{6,7},{7,6},{8,9},{9,8},{10,11... | collective-permute-start | bytes 3145736 | tf_op jit(solution)/shard_map/ppermute | solution.py:301
  53.8 29.1 %collective-permute-start.7 = (bf16[128,1024]{1,0:T(8,128)(2,1)}, bf16[128,1024]{1,0:T(8,128)(2,1)S(1)}, u32[]{:S(2)}, u32[]{:S(2)}) collective-permute-start(bf16[128,1024]{1,0:T(8,128)(2,1)} %slice_bitcast_fusion), channel_id=1, source_target_pairs={{0,1},{1,0},{2,3},{3,2},{4,5},{5,4},{6,7},{7,6},{8,9},{9,8},{10,11... | collective-permute-start | bytes 786440 | tf_op jit(solution)/shard_map/ppermute | solution.py:301
  74.1 96.6 %collective-permute-start = (bf16[8,2,32,1024]{3,2,1,0:T(8,128)(2,1)S(1)}, bf16[8,2,32,1024]{3,2,1,0:T(8,128)(2,1)S(1)}, u32[]{:S(2)}, u32[]{:S(2)}) collective-permute-start(bf16[8,2,32,1024]{3,2,1,0:T(8,128)(2,1)S(1)} %bitcast.20), channel_id=1, source_target_pairs={{0,1},{1,0},{2,3},{3,2},{4,5},{5,4},{6,7},{7,6},{8,9},{9,8},{10,11... | collective-permute-start | bytes 3145736 | tf_op jit(solution)/shard_map/ppermute | solution.py:301
  85.5 17.7 %collective-permute-start.8 = (bf16[144,1024]{1,0:T(8,128)(2,1)}, bf16[144,1024]{1,0:T(8,128)(2,1)}, u32[]{:S(2)}, u32[]{:S(2)}) collective-permute-start(bf16[144,1024]{1,0:T(8,128)(2,1)} %shard_map.116), channel_id=1, source_target_pairs={{0,256},{32,288},{64,320},{96,352},{128,384},{160,416},{192,448},{... | collective-permute-start | bytes 884744 | tf_op jit(solution)/shard_map/ppermute | solution.py:298
  93.2 31.1 %collective-permute-start.3 = (bf16[1024,256]{1,0:T(8,128)(2,1)S(1)}, bf16[1024,256]{1,0:T(8,128)(2,1)}, u32[]{:S(2)}, u32[]{:S(2)}) collective-permute-start(bf16[1024,256]{1,0:T(8,128)(2,1)S(1)} %bitcast.24), channel_id=1, source_target_pairs={{0,256},{32,288},{64,320},{96,352},{128,384},{160,416},{192,448},{... | collective-permute-start | bytes 1572872 | tf_op jit(solution)/shard_map/ppermute | solution.py:298
  95.3 54.3 %collective-permute-start.4 = (bf16[1024,256]{1,0:T(8,128)(2,1)S(1)}, bf16[1024,256]{1,0:T(8,128)(2,1)}, u32[]{:S(2)}, u32[]{:S(2)}) collective-permute-start(bf16[1024,256]{1,0:T(8,128)(2,1)S(1)} %bitcast.28), channel_id=1, source_target_pairs={{0,256},{32,288},{64,320},{96,352},{128,384},{160,416},{192,448},{... | collective-permute-start | bytes 1572872 | tf_op jit(solution)/shard_map/ppermute | solution.py:298
  103.2 67.5 %collective-permute-start.1 = (bf16[256,1024]{1,0:T(8,128)(2,1)}, bf16[256,1024]{1,0:T(8,128)(2,1)}, u32[]{:S(2)}, u32[]{:S(2)}) collective-permute-start(bf16[256,1024]{1,0:T(8,128)(2,1)} %bitcast.32), channel_id=1, source_target_pairs={{0,256},{32,288},{64,320},{96,352},{128,384},{160,416},{192,448},{... | collective-permute-start | bytes 1572872 | tf_op jit(solution)/shard_map/ppermute | solution.py:298
  116.2 77.8 %all-to-all-start.4 = ((bf16[16,16,1024]{2,1,0:T(8,128)(2,1)}), bf16[16,16,1024]{2,1,0:T(8,128)(2,1)}, u32[]{:S(2)}, u32[]{:S(2)}) async-start(bf16[16,16,1024]{2,1,0:T(8,128)(2,1)} %shard_map.117), calls=%async_computation.4 | async-start | bytes 1048576 | tf_op jit(solution)/shard_map/all_to_all | solution.py:274
  124.3 46.5 %copy-start.7 = (bf16[1,1,256,1024]{3,2,1,0:T(8,128)(2,1)S(1)}, bf16[1,1,256,1024]{3,2,1,0:T(8,128)(2,1)}, u32[]{:S(2)}) copy-start(bf16[1,1,256,1024]{3,2,1,0:T(8,128)(2,1)} %param.13) | copy-start | bytes 1572868
  175.6 8.6 %copy-start.2 = (bf16[512,512]{1,0:T(8,128)(2,1)}, bf16[512,512]{1,0:T(8,128)(2,1)S(1)}, u32[]{:S(2)}) copy-start(bf16[512,512]{1,0:T(8,128)(2,1)S(1)} %get-tuple-element.25.d) | copy-start | bytes 1572868
  175.6 17.4 %collective-permute-start.6 = (bf16[8,2,16,1024]{3,2,1,0:T(8,128)(2,1)S(1)}, bf16[8,2,16,1024]{3,2,1,0:T(8,128)(2,1)S(1)}, u32[]{:S(2)}, u32[]{:S(2)}) collective-permute-start(bf16[8,2,16,1024]{3,2,1,0:T(8,128)(2,1)S(1)} %get-tuple-element.30), channel_id=1, source_target_pairs={{0,1},{1,0},{2,3},{3,2},{4,5},{5,4},{6,7},{7,6},{8,9},{9,8},{10,11... | collective-permute-start | bytes 1572872 | tf_op jit(solution)/shard_map/ppermute | solution.py:301
  180.3 21.9 %collective-permute-start.5 = (bf16[8,2,16,1152]{3,2,1,0:T(8,128)(2,1)}, bf16[8,2,16,1152]{3,2,1,0:T(8,128)(2,1)}, u32[]{:S(2)}, u32[]{:S(2)}) collective-permute-start(bf16[8,2,16,1152]{3,2,1,0:T(8,128)(2,1)} %get-tuple-element.28), channel_id=1, source_target_pairs={{0,1},{1,0},{2,3},{3,2},{4,5},{5,4},{6,7},{7,6},{8,9},{9,8},{10,11... | collective-permute-start | bytes 1769480 | tf_op jit(solution)/shard_map/ppermute | solution.py:301
  194.0 19.9 %all-to-all-start.3 = ((bf16[16,16,1024]{2,1,0:T(8,128)(2,1)}), bf16[16,16,1024]{2,1,0:T(8,128)(2,1)S(1)}, u32[]{:S(2)}, u32[]{:S(2)}) async-start(bf16[16,16,1024]{2,1,0:T(8,128)(2,1)} %bitcast.10), calls=%async_computation.3 | async-start | bytes 1048576 | tf_op jit(solution)/shard_map/all_to_all | solution.py:274
  213.8 56.5 %all-to-all-start.2 = ((bf16[16,16,1152]{2,1,0:T(8,128)(2,1)}), bf16[16,16,1152]{2,1,0:T(8,128)(2,1)S(1)}, u32[]{:S(2)}, u32[]{:S(2)}) async-start(bf16[16,16,1152]{2,1,0:T(8,128)(2,1)} %bitcast.42), calls=%async_computation.2 | async-start | bytes 1179648 | tf_op jit(solution)/shard_map/all_to_all | solution.py:274
  219.1 16.8 %collective-permute-start.9 = (bf16[8,2,16,1024]{3,2,1,0:T(8,128)(2,1)}, bf16[8,2,16,1024]{3,2,1,0:T(8,128)(2,1)S(1)}, u32[]{:S(2)}, u32[]{:S(2)}) collective-permute-start(bf16[8,2,16,1024]{3,2,1,0:T(8,128)(2,1)} %bitcast.14.own), channel_id=1, source_target_pairs={{0,1},{1,0},{2,3},{3,2},{4,5},{5,4},{6,7},{7,6},{8,9},{9,8},{10,11... | collective-permute-start | bytes 1572872 | tf_op jit(solution)/shard_map/ppermute | solution.py:301
  225.4 37.6 %collective-permute-start.10 = (bf16[512,512]{1,0:T(8,128)(2,1)}, bf16[512,512]{1,0:T(8,128)(2,1)S(1)}, u32[]{:S(2)}, u32[]{:S(2)}) collective-permute-start(bf16[512,512]{1,0:T(8,128)(2,1)} %copy-done.2), channel_id=1, source_target_pairs={{0,256},{32,288},{64,320},{96,352},{128,384},{160,416},{192,448},{... | collective-permute-start | bytes 1572872 | tf_op jit(solution)/shard_map/ppermute | solution.py:298
  232.6 36.8 %collective-permute-start.11 = (bf16[256,1024]{1,0:T(8,128)(2,1)S(1)}, bf16[256,1024]{1,0:T(8,128)(2,1)S(1)}, u32[]{:S(2)}, u32[]{:S(2)}) collective-permute-start(bf16[256,1024]{1,0:T(8,128)(2,1)S(1)} %shard_map.121), channel_id=1, source_target_pairs={{0,256},{32,288},{64,320},{96,352},{128,384},{160,416},{192,448},{... | collective-permute-start | bytes 1572872 | tf_op jit(solution)/shard_map/ppermute | solution.py:298
  264.7 5.7 %copy-start.8 = (s32[1,2,1,16]{3,2,1,0:T(1,128)S(1)}, s32[1,2,1,16]{3,2,1,0:T(1,128)}, u32[]{:S(2)}) copy-start(s32[1,2,1,16]{3,2,1,0:T(1,128)} %param.10) | copy-start | bytes 388
  264.7 5.7 %copy-start.9 = (bf16[1,2,128]{2,1,0:T(2,128)(2,1)S(1)}, bf16[1,2,128]{2,1,0:T(2,128)(2,1)}, u32[]{:S(2)}) copy-start(bf16[1,2,128]{2,1,0:T(2,128)(2,1)} %param.9) | copy-start | bytes 1540
  (5 other events, 12.3 us)

commit v6 on v5

--- a/solution.py
+++ b/solution.py
@@ -257,15 +257,17 @@
     )
 
 
-def keep_body(own, other, x_t, act_t, d, grad_ref, down_ref, half, sems):
-    waits = half_copies(own, other, keeps_low(), half, sems)
+def down_keep_body(own, other, act_t, down_ref, half, sems):
+    for c in half_copies(own, other, keeps_low(), half, sems):
+        c.wait()
+    down_ref[...] = dot(act_t[...], flat(half), 1, 0)
+
+
+def grad_keep_body(x_t, d, grad_ref):
     both = dot(x_t[...], d[...], 1, 0)
     hidden = grad_ref.shape[2]
     grad_ref[0] = both[:, :hidden]
     grad_ref[1] = both[:, hidden:]
-    for c in waits:
-        c.wait()
-    down_ref[...] = dot(act_t[...], flat(half), 1, 0)
 
 
 def dispatch(array):
@@ -300,7 +302,7 @@
     def swap(array):
         return lax.ppermute(array, "tensor", [(0, 1), (1, 0)])
 
-    late = ("hidden", "down", "slope", "rowkeep", "keep", "turn", "final", "unpack")
+    late = ("hidden", "down", "slope", "rowkeep", "downkeep", "gradkeep", "turn", "final", "unpack")
 
     def kernel(name, body, outs, args, flops, in_place=(), scratch=()):
         limit = 24 * 1024 * 1024 if name in late else None
@@ -387,14 +389,17 @@
         (0, 1),
         (pltpu.VMEM((2, experts // 2, dirs, slots, width), BF), sems((4,))),
     )
-    grad_keep, down_keep = kernel(
-        "keep",
-        keep_body,
-        [shape((2, width, hidden), F32), shape((hidden, width), F32)],
-        (g_own, g_other, x_keep_t, act_t, d),
-        3 * one,
+    (down_keep,) = kernel(
+        "downkeep",
+        down_keep_body,
+        [shape((hidden, width), F32)],
+        (g_own, g_other, act_t),
+        one,
         (0, 1),
         (side_rows, sems((2,))),
+    )
+    (grad_keep,) = kernel(
+        "gradkeep", grad_keep_body, [shape((2, width, hidden), F32)], (x_keep_t, d), 2 * one
     )
     gate_grad, up_grad = kernel(
         "final",

time: 273 us -> 273 us (level)
    pallas_call x12 -> x13, Pallas kernels: 26.8 us -> 26.8 us  [call(): pl.pallas_call(body, out_shape=tuple(outs), in_specs=in_specs, out_specs=...]
where the time goes in v6:
time: 273 us; the launch traced here: 272 us
  waiting for transfers between devices  134 us (49%)
  starting transfers between devices  102 us (37%)
  Pallas kernels  26.8 us (10%)
  local copies, waits for them, and re-layouts  4.27 us (2%)
  other arithmetic  4.22 us (2%)
    ppermute x6, waiting for transfers between devices, mirror(): lax.ppermute(array, 'pipe', [(i, (i + pipes // 2) % pipes) for i in range...  70 us
    all_to_all x5, waiting for transfers between devices, dispatch(): lax.all_to_all(array, ('expert', 'tensor'), 0, 0, axis_index_groups=group...  52.4 us
    all_to_all x5, starting transfers between devices, dispatch(): lax.all_to_all(array, ('expert', 'tensor'), 0, 0, axis_index_groups=group...  38.3 us
    ppermute x6, starting transfers between devices, mirror(): lax.ppermute(array, 'pipe', [(i, (i + pipes // 2) % pipes) for i in range...  38 us
    pallas_call x13, Pallas kernels, call(): pl.pallas_call(body, out_shape=tuple(outs), in_specs=in_specs, out_specs=...  26.8 us
    ppermute x6, starting transfers between devices, swap(): return lax.ppermute(array, 'tensor', [(0, 1), (1, 0)])  26 us
    ppermute x6, waiting for transfers between devices, swap(): return lax.ppermute(array, 'tensor', [(0, 1), (1, 0)])  11.1 us
  transfers between devices with their start and end apart: 17, of which 10 were waited for; matrix products, arithmetic and copies ran while one was open for 2% of the time, Pallas kernels for 8%

profile of v6, /device:TPU:4, one launch (start us, length us, event | category | flops | bytes accessed | tf_op | source)
XLA Modules:
  0.0 272.1 jit_solution(10040922619957879857)
XLA Ops:
  3.2 11.8 %all-to-all-start.1 = ((bf16[16,2,16,1024]{3,2,1,0:T(8,128)(2,1)}), bf16[16,2,16,1024]{3,2,1,0:T(8,128)(2,1)}, u32[]{:S(2)}, u32[]{:S(2)}) async-start(bf16[16,2,16,1024]{3,2,1,0:T(8,128)(2,1)} %shard_map.111), calls=%async_computation.1 | async-start | bytes 2097152 | tf_op jit(solution)/shard_map/all_to_all | solution.py:276
  17.7 24.7 %all-to-all-done.1 = bf16[16,2,16,1024]{3,2,1,0:T(8,128)(2,1)} async-done(((bf16[16,2,16,1024]{3,2,1,0:T(8,128)(2,1)}), bf16[16,2,16,1024]{3,2,1,0:T(8,128)(2,1)}, u32[]{:S(2)}, u32[]{:S(2)}) %all-to-all-start.1) | async-done | bytes 1048608 | tf_op jit(solution)/shard_map/all_to_all | solution.py:276
  42.3 5.1 %all-to-all-start = ((bf16[16,2,16,1024]{3,2,1,0:T(8,128)(2,1)}), bf16[16,2,16,1024]{3,2,1,0:T(8,128)(2,1)S(1)}, u32[]{:S(2)}, u32[]{:S(2)}) async-start(bf16[16,2,16,1024]{3,2,1,0:T(8,128)(2,1)} %shard_map.110), calls=%async_computation | async-start | bytes 2097152 | tf_op jit(solution)/shard_map/all_to_all | solution.py:276
  47.4 5.7 %collective-permute-start.2 = (bf16[8,2,32,1024]{3,2,1,0:T(8,128)(2,1)}, bf16[8,2,32,1024]{3,2,1,0:T(8,128)(2,1)}, u32[]{:S(2)}, u32[]{:S(2)}) collective-permute-start(bf16[8,2,32,1024]{3,2,1,0:T(8,128)(2,1)} %bitcast.6.own), channel_id=1, source_target_pairs={{0,1},{1,0},{2,3},{3,2},{4,5},{5,4},{6,7},{7,6},{8,9},{9,8},{10,11... | collective-permute-start | bytes 3145736 | tf_op jit(solution)/shard_map/ppermute | solution.py:303
  55.7 18.4 %all-to-all-done = bf16[16,2,16,1024]{3,2,1,0:T(8,128)(2,1)S(1)} async-done(((bf16[16,2,16,1024]{3,2,1,0:T(8,128)(2,1)}), bf16[16,2,16,1024]{3,2,1,0:T(8,128)(2,1)S(1)}, u32[]{:S(2)}, u32[]{:S(2)}) %all-to-all-start) | async-done | bytes 1048608 | tf_op jit(solution)/shard_map/all_to_all | solution.py:276
  74.1 5.5 %collective-permute-start = (bf16[8,2,32,1024]{3,2,1,0:T(8,128)(2,1)S(1)}, bf16[8,2,32,1024]{3,2,1,0:T(8,128)(2,1)S(1)}, u32[]{:S(2)}, u32[]{:S(2)}) collective-permute-start(bf16[8,2,32,1024]{3,2,1,0:T(8,128)(2,1)S(1)} %bitcast.20), channel_id=1, source_target_pairs={{0,1},{1,0},{2,3},{3,2},{4,5},{5,4},{6,7},{7,6},{8,9},{9,8},{10,11... | collective-permute-start | bytes 3145736 | tf_op jit(solution)/shard_map/ppermute | solution.py:303
  79.7 3.3 %collective-permute-done.7.other_ref = bf16[128,1024]{1,0:T(8,128)(2,1)S(1)} collective-permute-done((bf16[128,1024]{1,0:T(8,128)(2,1)}, bf16[128,1024]{1,0:T(8,128)(2,1)S(1)}, u32[]{:S(2)}, u32[]{:S(2)}) %collective-permute-start.7) | collective-permute-done | bytes 262176 | tf_op jit(solution)/shard_map/ppermute | solution.py:303
  85.5 7.7 %collective-permute-start.8 = (bf16[144,1024]{1,0:T(8,128)(2,1)}, bf16[144,1024]{1,0:T(8,128)(2,1)}, u32[]{:S(2)}, u32[]{:S(2)}) collective-permute-start(bf16[144,1024]{1,0:T(8,128)(2,1)} %shard_map.116), channel_id=1, source_target_pairs={{0,256},{32,288},{64,320},{96,352},{128,384},{160,416},{192,448},{... | collective-permute-start | bytes 884744 | tf_op jit(solution)/shard_map/ppermute | solution.py:300
  95.3 7.7 %collective-permute-start.4 = (bf16[1024,256]{1,0:T(8,128)(2,1)S(1)}, bf16[1024,256]{1,0:T(8,128)(2,1)}, u32[]{:S(2)}, u32[]{:S(2)}) collective-permute-start(bf16[1024,256]{1,0:T(8,128)(2,1)S(1)} %bitcast.28), channel_id=1, source_target_pairs={{0,256},{32,288},{64,320},{96,352},{128,384},{160,416},{192,448},{... | collective-permute-start | bytes 1572872 | tf_op jit(solution)/shard_map/ppermute | solution.py:300
  103.2 10.8 %collective-permute-start.1 = (bf16[256,1024]{1,0:T(8,128)(2,1)}, bf16[256,1024]{1,0:T(8,128)(2,1)}, u32[]{:S(2)}, u32[]{:S(2)}) collective-permute-start(bf16[256,1024]{1,0:T(8,128)(2,1)} %bitcast.32), channel_id=1, source_target_pairs={{0,256},{32,288},{64,320},{96,352},{128,384},{160,416},{192,448},{... | collective-permute-start | bytes 1572872 | tf_op jit(solution)/shard_map/ppermute | solution.py:300
  116.2 8.1 %all-to-all-start.4 = ((bf16[16,16,1024]{2,1,0:T(8,128)(2,1)}), bf16[16,16,1024]{2,1,0:T(8,128)(2,1)}, u32[]{:S(2)}, u32[]{:S(2)}) async-start(bf16[16,16,1024]{2,1,0:T(8,128)(2,1)} %shard_map.117), calls=%async_computation.4 | async-start | bytes 1048576 | tf_op jit(solution)/shard_map/all_to_all | solution.py:276
  124.3 25.3 %collective-permute-done.4.wuo = bf16[1024,256]{1,0:T(8,128)(2,1)} collective-permute-done((bf16[1024,256]{1,0:T(8,128)(2,1)S(1)}, bf16[1024,256]{1,0:T(8,128)(2,1)}, u32[]{:S(2)}, u32[]{:S(2)}) %collective-permute-start.4) | collective-permute-done | bytes 524320 | tf_op jit(solution)/shard_map/ppermute | solution.py:300
  149.6 4.2 %shard_map.112 = (bf16[512,256]{1,0:T(8,128)(2,1)S(1)}, bf16[256,512]{1,0:T(8,128)(2,1)S(1)}, f32[512,256]{1,0:T(8,128)S(1)}, f32[512,256]{1,0:T(8,128)S(1)}, bf16[1024,512]{1,0:T(8,128)(2,1)S(1)}) custom-call(bf16[8,2,32,1024]{3,2,1,0:T(8,128)(2,1)} %bitcast.6.own, bf16[8,2,32,1024]{3,2,1,0:T(8,128)(2,1)} %collective-permute-done.2.other, ...), custom_call_target="tpu_custom_call" | custom-call | flops 1073741824 | bytes 6815744 | tf_op jit(solution)/shard_map/pallas_call | solution.py:22
  154.7 16.0 %collective-permute-done.1.wdo = bf16[256,1024]{1,0:T(8,128)(2,1)} collective-permute-done((bf16[256,1024]{1,0:T(8,128)(2,1)}, bf16[256,1024]{1,0:T(8,128)(2,1)}, u32[]{:S(2)}, u32[]{:S(2)}) %collective-permute-start.1) | collective-permute-done | bytes 524320 | tf_op jit(solution)/shard_map/ppermute | solution.py:300
  170.8 4.8 %shard_map.113 = (bf16[512,512]{1,0:T(8,128)(2,1)S(1)}, f32[512,128]{1,0:T(8,128)S(1)}, bf16[8,2,16,1152]{3,2,1,0:T(8,128)(2,1)}, bf16[8,2,16,1024]{3,2,1,0:T(8,128)(2,1)S(1)}) custom-call(bf16[8,2,32,1024]{3,2,1,0:T(8,128)(2,1)S(1)} %bitcast.21, bf16[8,2,32,1024]{3,2,1,0:T(8,128)(2,1)S(1)} %collective-permute-done.other, bf16[256,1024]{1,0:T(8,128)(2,1)S(1)} %bitcast.33, ...), custom_call_target="tpu_custom_call" | custom-call | flops 1073741824 | bytes 8454144 | tf_op jit(solution)/shard_map/pallas_call | solution.py:22
  175.6 4.7 %collective-permute-start.6 = (bf16[8,2,16,1024]{3,2,1,0:T(8,128)(2,1)S(1)}, bf16[8,2,16,1024]{3,2,1,0:T(8,128)(2,1)S(1)}, u32[]{:S(2)}, u32[]{:S(2)}) collective-permute-start(bf16[8,2,16,1024]{3,2,1,0:T(8,128)(2,1)S(1)} %get-tuple-element.28), channel_id=1, source_target_pairs={{0,1},{1,0},{2,3},{3,2},{4,5},{5,4},{6,7},{7,6},{8,9},{9,8},{10,11... | collective-permute-start | bytes 1572872 | tf_op jit(solution)/shard_map/ppermute | solution.py:303
  185.2 7.8 %collective-permute-done.6 = bf16[8,2,16,1024]{3,2,1,0:T(8,128)(2,1)S(1)} collective-permute-done((bf16[8,2,16,1024]{3,2,1,0:T(8,128)(2,1)S(1)}, bf16[8,2,16,1024]{3,2,1,0:T(8,128)(2,1)S(1)}, u32[]{:S(2)}, u32[]{:S(2)}) %collective-permute-start.6) | collective-permute-done | bytes 524320 | tf_op jit(solution)/shard_map/ppermute | solution.py:303
  194.0 8.2 %all-to-all-start.3 = ((bf16[16,16,1024]{2,1,0:T(8,128)(2,1)}), bf16[16,16,1024]{2,1,0:T(8,128)(2,1)S(1)}, u32[]{:S(2)}, u32[]{:S(2)}) async-start(bf16[16,16,1024]{2,1,0:T(8,128)(2,1)} %bitcast.10), calls=%async_computation.3 | async-start | bytes 1048576 | tf_op jit(solution)/shard_map/all_to_all | solution.py:276
  204.5 9.3 %all-to-all-done.3.second = bf16[16,16,1024]{2,1,0:T(8,128)(2,1)S(1)} async-done(((bf16[16,16,1024]{2,1,0:T(8,128)(2,1)}), bf16[16,16,1024]{2,1,0:T(8,128)(2,1)S(1)}, u32[]{:S(2)}, u32[]{:S(2)}) %all-to-all-start.3) | async-done | bytes 524320 | tf_op jit(solution)/shard_map/all_to_all | solution.py:276
  213.8 5.2 %all-to-all-start.2 = ((bf16[16,16,1152]{2,1,0:T(8,128)(2,1)}), bf16[16,16,1152]{2,1,0:T(8,128)(2,1)S(1)}, u32[]{:S(2)}, u32[]{:S(2)}) async-start(bf16[16,16,1152]{2,1,0:T(8,128)(2,1)} %bitcast.42), calls=%async_computation.2 | async-start | bytes 1179648 | tf_op jit(solution)/shard_map/all_to_all | solution.py:276
  219.1 6.3 %collective-permute-start.9 = (bf16[8,2,16,1024]{3,2,1,0:T(8,128)(2,1)}, bf16[8,2,16,1024]{3,2,1,0:T(8,128)(2,1)S(1)}, u32[]{:S(2)}, u32[]{:S(2)}) collective-permute-start(bf16[8,2,16,1024]{3,2,1,0:T(8,128)(2,1)} %bitcast.14.own), channel_id=1, source_target_pairs={{0,1},{1,0},{2,3},{3,2},{4,5},{5,4},{6,7},{7,6},{8,9},{9,8},{10,11... | collective-permute-start | bytes 1572872 | tf_op jit(solution)/shard_map/ppermute | solution.py:303
  225.4 6.6 %collective-permute-start.10 = (bf16[512,512]{1,0:T(8,128)(2,1)}, bf16[512,512]{1,0:T(8,128)(2,1)S(1)}, u32[]{:S(2)}, u32[]{:S(2)}) collective-permute-start(bf16[512,512]{1,0:T(8,128)(2,1)} %copy-done.2), channel_id=1, source_target_pairs={{0,256},{32,288},{64,320},{96,352},{128,384},{160,416},{192,448},{... | collective-permute-start | bytes 1572872 | tf_op jit(solution)/shard_map/ppermute | solution.py:300
  239.3 23.7 %collective-permute-done.10.d = bf16[512,512]{1,0:T(8,128)(2,1)S(1)} collective-permute-done((bf16[512,512]{1,0:T(8,128)(2,1)}, bf16[512,512]{1,0:T(8,128)(2,1)S(1)}, u32[]{:S(2)}, u32[]{:S(2)}) %collective-permute-start.10) | collective-permute-done | bytes 524320 | tf_op jit(solution)/shard_map/ppermute | solution.py:300
  264.7 4.8 %collective-permute-done.11 = bf16[256,1024]{1,0:T(8,128)(2,1)S(1)} collective-permute-done((bf16[256,1024]{1,0:T(8,128)(2,1)S(1)}, bf16[256,1024]{1,0:T(8,128)(2,1)S(1)}, u32[]{:S(2)}, u32[]{:S(2)}) %collective-permute-start.11) | collective-permute-done | bytes 524320 | tf_op jit(solution)/shard_map/ppermute | solution.py:300
  (51 shorter events, 35.6 us)
Async XLA Ops:
  3.2 39.1 %all-to-all-start.1 = ((bf16[16,2,16,1024]{3,2,1,0:T(8,128)(2,1)}), bf16[16,2,16,1024]{3,2,1,0:T(8,128)(2,1)}, u32[]{:S(2)}, u32[]{:S(2)}) async-start(bf16[16,2,16,1024]{3,2,1,0:T(8,128)(2,1)} %shard_map.111), calls=%async_computation.1 | async-start | bytes 2097152 | tf_op jit(solution)/shard_map/all_to_all | solution.py:276
  17.7 35.4 %copy-start.10 = (bf16[1,2,128,1024]{3,2,1,0:T(8,128)(2,1)S(1)}, bf16[1,2,128,1024]{3,2,1,0:T(8,128)(2,1)}, u32[]{:S(2)}) copy-start(bf16[1,2,128,1024]{3,2,1,0:T(8,128)(2,1)} %param.7) | copy-start | bytes 1572868
  42.3 31.8 %all-to-all-start = ((bf16[16,2,16,1024]{3,2,1,0:T(8,128)(2,1)}), bf16[16,2,16,1024]{3,2,1,0:T(8,128)(2,1)S(1)}, u32[]{:S(2)}, u32[]{:S(2)}) async-start(bf16[16,2,16,1024]{3,2,1,0:T(8,128)(2,1)} %shard_map.110), calls=%async_computation | async-start | bytes 2097152 | tf_op jit(solution)/shard_map/all_to_all | solution.py:276
  47.4 45.8 %copy-start = (bf16[1,1,1024,256]{3,2,1,0:T(8,128)(2,1)S(1)}, bf16[1,1,1024,256]{3,2,1,0:T(8,128)(2,1)}, u32[]{:S(2)}) copy-start(bf16[1,1,1024,256]{3,2,1,0:T(8,128)(2,1)} %param.11) | copy-start | bytes 1572868
  47.4 47.8 %copy-start.1 = (bf16[1,1,1024,256]{3,2,1,0:T(8,128)(2,1)S(1)}, bf16[1,1,1024,256]{3,2,1,0:T(8,128)(2,1)}, u32[]{:S(2)}) copy-start(bf16[1,1,1024,256]{3,2,1,0:T(8,128)(2,1)} %param.12) | copy-start | bytes 1572868
  47.4 102.2 %collective-permute-start.2 = (bf16[8,2,32,1024]{3,2,1,0:T(8,128)(2,1)}, bf16[8,2,32,1024]{3,2,1,0:T(8,128)(2,1)}, u32[]{:S(2)}, u32[]{:S(2)}) collective-permute-start(bf16[8,2,32,1024]{3,2,1,0:T(8,128)(2,1)} %bitcast.6.own), channel_id=1, source_target_pairs={{0,1},{1,0},{2,3},{3,2},{4,5},{5,4},{6,7},{7,6},{8,9},{9,8},{10,11... | collective-permute-start | bytes 3145736 | tf_op jit(solution)/shard_map/ppermute | solution.py:303
  53.8 29.1 %collective-permute-start.7 = (bf16[128,1024]{1,0:T(8,128)(2,1)}, bf16[128,1024]{1,0:T(8,128)(2,1)S(1)}, u32[]{:S(2)}, u32[]{:S(2)}) collective-permute-start(bf16[128,1024]{1,0:T(8,128)(2,1)} %slice_bitcast_fusion), channel_id=1, source_target_pairs={{0,1},{1,0},{2,3},{3,2},{4,5},{5,4},{6,7},{7,6},{8,9},{9,8},{10,11... | collective-permute-start | bytes 786440 | tf_op jit(solution)/shard_map/ppermute | solution.py:303
  74.1 96.6 %collective-permute-start = (bf16[8,2,32,1024]{3,2,1,0:T(8,128)(2,1)S(1)}, bf16[8,2,32,1024]{3,2,1,0:T(8,128)(2,1)S(1)}, u32[]{:S(2)}, u32[]{:S(2)}) collective-permute-start(bf16[8,2,32,1024]{3,2,1,0:T(8,128)(2,1)S(1)} %bitcast.20), channel_id=1, source_target_pairs={{0,1},{1,0},{2,3},{3,2},{4,5},{5,4},{6,7},{7,6},{8,9},{9,8},{10,11... | collective-permute-start | bytes 3145736 | tf_op jit(solution)/shard_map/ppermute | solution.py:303
  85.5 17.7 %collective-permute-start.8 = (bf16[144,1024]{1,0:T(8,128)(2,1)}, bf16[144,1024]{1,0:T(8,128)(2,1)}, u32[]{:S(2)}, u32[]{:S(2)}) collective-permute-start(bf16[144,1024]{1,0:T(8,128)(2,1)} %shard_map.116), channel_id=1, source_target_pairs={{0,256},{32,288},{64,320},{96,352},{128,384},{160,416},{192,448},{... | collective-permute-start | bytes 884744 | tf_op jit(solution)/shard_map/ppermute | solution.py:300
  93.2 31.1 %collective-permute-start.3 = (bf16[1024,256]{1,0:T(8,128)(2,1)S(1)}, bf16[1024,256]{1,0:T(8,128)(2,1)}, u32[]{:S(2)}, u32[]{:S(2)}) collective-permute-start(bf16[1024,256]{1,0:T(8,128)(2,1)S(1)} %bitcast.24), channel_id=1, source_target_pairs={{0,256},{32,288},{64,320},{96,352},{128,384},{160,416},{192,448},{... | collective-permute-start | bytes 1572872 | tf_op jit(solution)/shard_map/ppermute | solution.py:300
  95.3 54.3 %collective-permute-start.4 = (bf16[1024,256]{1,0:T(8,128)(2,1)S(1)}, bf16[1024,256]{1,0:T(8,128)(2,1)}, u32[]{:S(2)}, u32[]{:S(2)}) collective-permute-start(bf16[1024,256]{1,0:T(8,128)(2,1)S(1)} %bitcast.28), channel_id=1, source_target_pairs={{0,256},{32,288},{64,320},{96,352},{128,384},{160,416},{192,448},{... | collective-permute-start | bytes 1572872 | tf_op jit(solution)/shard_map/ppermute | solution.py:300
  103.2 67.5 %collective-permute-start.1 = (bf16[256,1024]{1,0:T(8,128)(2,1)}, bf16[256,1024]{1,0:T(8,128)(2,1)}, u32[]{:S(2)}, u32[]{:S(2)}) collective-permute-start(bf16[256,1024]{1,0:T(8,128)(2,1)} %bitcast.32), channel_id=1, source_target_pairs={{0,256},{32,288},{64,320},{96,352},{128,384},{160,416},{192,448},{... | collective-permute-start | bytes 1572872 | tf_op jit(solution)/shard_map/ppermute | solution.py:300
  116.2 77.8 %all-to-all-start.4 = ((bf16[16,16,1024]{2,1,0:T(8,128)(2,1)}), bf16[16,16,1024]{2,1,0:T(8,128)(2,1)}, u32[]{:S(2)}, u32[]{:S(2)}) async-start(bf16[16,16,1024]{2,1,0:T(8,128)(2,1)} %shard_map.117), calls=%async_computation.4 | async-start | bytes 1048576 | tf_op jit(solution)/shard_map/all_to_all | solution.py:276
  124.3 46.5 %copy-start.7 = (bf16[1,1,256,1024]{3,2,1,0:T(8,128)(2,1)S(1)}, bf16[1,1,256,1024]{3,2,1,0:T(8,128)(2,1)}, u32[]{:S(2)}) copy-start(bf16[1,1,256,1024]{3,2,1,0:T(8,128)(2,1)} %param.13) | copy-start | bytes 1572868
  175.6 8.6 %copy-start.2 = (bf16[512,512]{1,0:T(8,128)(2,1)}, bf16[512,512]{1,0:T(8,128)(2,1)S(1)}, u32[]{:S(2)}) copy-start(bf16[512,512]{1,0:T(8,128)(2,1)S(1)} %get-tuple-element.23.d) | copy-start | bytes 1572868
  175.6 17.4 %collective-permute-start.6 = (bf16[8,2,16,1024]{3,2,1,0:T(8,128)(2,1)S(1)}, bf16[8,2,16,1024]{3,2,1,0:T(8,128)(2,1)S(1)}, u32[]{:S(2)}, u32[]{:S(2)}) collective-permute-start(bf16[8,2,16,1024]{3,2,1,0:T(8,128)(2,1)S(1)} %get-tuple-element.28), channel_id=1, source_target_pairs={{0,1},{1,0},{2,3},{3,2},{4,5},{5,4},{6,7},{7,6},{8,9},{9,8},{10,11... | collective-permute-start | bytes 1572872 | tf_op jit(solution)/shard_map/ppermute | solution.py:303
  180.3 21.9 %collective-permute-start.5 = (bf16[8,2,16,1152]{3,2,1,0:T(8,128)(2,1)}, bf16[8,2,16,1152]{3,2,1,0:T(8,128)(2,1)}, u32[]{:S(2)}, u32[]{:S(2)}) collective-permute-start(bf16[8,2,16,1152]{3,2,1,0:T(8,128)(2,1)} %get-tuple-element.26), channel_id=1, source_target_pairs={{0,1},{1,0},{2,3},{3,2},{4,5},{5,4},{6,7},{7,6},{8,9},{9,8},{10,11... | collective-permute-start | bytes 1769480 | tf_op jit(solution)/shard_map/ppermute | solution.py:303
  194.0 19.9 %all-to-all-start.3 = ((bf16[16,16,1024]{2,1,0:T(8,128)(2,1)}), bf16[16,16,1024]{2,1,0:T(8,128)(2,1)S(1)}, u32[]{:S(2)}, u32[]{:S(2)}) async-start(bf16[16,16,1024]{2,1,0:T(8,128)(2,1)} %bitcast.10), calls=%async_computation.3 | async-start | bytes 1048576 | tf_op jit(solution)/shard_map/all_to_all | solution.py:276
  213.8 56.5 %all-to-all-start.2 = ((bf16[16,16,1152]{2,1,0:T(8,128)(2,1)}), bf16[16,16,1152]{2,1,0:T(8,128)(2,1)S(1)}, u32[]{:S(2)}, u32[]{:S(2)}) async-start(bf16[16,16,1152]{2,1,0:T(8,128)(2,1)} %bitcast.42), calls=%async_computation.2 | async-start | bytes 1179648 | tf_op jit(solution)/shard_map/all_to_all | solution.py:276
  219.1 16.7 %collective-permute-start.9 = (bf16[8,2,16,1024]{3,2,1,0:T(8,128)(2,1)}, bf16[8,2,16,1024]{3,2,1,0:T(8,128)(2,1)S(1)}, u32[]{:S(2)}, u32[]{:S(2)}) collective-permute-start(bf16[8,2,16,1024]{3,2,1,0:T(8,128)(2,1)} %bitcast.14.own), channel_id=1, source_target_pairs={{0,1},{1,0},{2,3},{3,2},{4,5},{5,4},{6,7},{7,6},{8,9},{9,8},{10,11... | collective-permute-start | bytes 1572872 | tf_op jit(solution)/shard_map/ppermute | solution.py:303
  225.4 37.6 %collective-permute-start.10 = (bf16[512,512]{1,0:T(8,128)(2,1)}, bf16[512,512]{1,0:T(8,128)(2,1)S(1)}, u32[]{:S(2)}, u32[]{:S(2)}) collective-permute-start(bf16[512,512]{1,0:T(8,128)(2,1)} %copy-done.2), channel_id=1, source_target_pairs={{0,256},{32,288},{64,320},{96,352},{128,384},{160,416},{192,448},{... | collective-permute-start | bytes 1572872 | tf_op jit(solution)/shard_map/ppermute | solution.py:300
  232.6 36.9 %collective-permute-start.11 = (bf16[256,1024]{1,0:T(8,128)(2,1)S(1)}, bf16[256,1024]{1,0:T(8,128)(2,1)S(1)}, u32[]{:S(2)}, u32[]{:S(2)}) collective-permute-start(bf16[256,1024]{1,0:T(8,128)(2,1)S(1)} %shard_map.122), channel_id=1, source_target_pairs={{0,256},{32,288},{64,320},{96,352},{128,384},{160,416},{192,448},{... | collective-permute-start | bytes 1572872 | tf_op jit(solution)/shard_map/ppermute | solution.py:300
  264.7 5.7 %copy-start.8 = (s32[1,2,1,16]{3,2,1,0:T(1,128)S(1)}, s32[1,2,1,16]{3,2,1,0:T(1,128)}, u32[]{:S(2)}) copy-start(s32[1,2,1,16]{3,2,1,0:T(1,128)} %param.10) | copy-start | bytes 388
  264.7 5.7 %copy-start.9 = (bf16[1,2,128]{2,1,0:T(2,128)(2,1)S(1)}, bf16[1,2,128]{2,1,0:T(2,128)(2,1)}, u32[]{:S(2)}) copy-start(bf16[1,2,128]{2,1,0:T(2,128)(2,1)} %param.9) | copy-start | bytes 1540
  (5 other events, 5.2 us)

commit v7 on v6

--- a/solution.py
+++ b/solution.py
@@ -34,15 +34,15 @@
     return jax.ShapeDtypeStruct(dims, kind)
 
 
-def slot_choice(count_row, slots, rows):
+def slot_choice(count_row, slots, rows, offset=0):
     experts = count_row.shape[1]
     total = experts * slots
     owner = lax.broadcasted_iota(jnp.int32, (total, experts), 0) // slots
     expert = lax.broadcasted_iota(jnp.int32, (total, experts), 1)
     count = jnp.sum(jnp.where(expert == owner, count_row, 0), axis=1, keepdims=True)
     start = jnp.sum(jnp.where(expert < owner, count_row, 0), axis=1, keepdims=True)
-    place = lax.broadcasted_iota(jnp.int32, (total, 1), 0) % slots
-    target = jnp.where(place < count, start + place, -1)
+    place = lax.broadcasted_iota(jnp.int32, (total, 1), 0) % slots + offset
+    target = jnp.where((place >= 0) & (place < count), start + place, -1)
     return lax.broadcasted_iota(jnp.int32, (total, rows), 1) == target
 
 
@@ -72,18 +72,27 @@
     ]
     for c in copies:
         c.start()
-    experts, slots, width = second_ref.shape
+    experts, rest, width = second_ref.shape
+    few = first_ref.shape[1]
     dirs, rows, _ = out_ref.shape
-    masks = [
-        slot_choice(counts_ref[d : d + 1, :], slots, rows).astype(BF) for d in range(dirs)
-    ]
-    for c in copies:
-        c.wait()
-    terms = first_ref[:, :, width:].reshape(experts * slots, LANES)
-    for d, ref in enumerate((first_ref, second_ref)):
-        part = ref[:, :, :width].reshape(experts * slots, width)
-        out_ref[d] = dot(masks[d], part, 0, 0).astype(BF)
-        found = dot(terms, masks[d], 0, 0)[d : d + 1, :]
+
+    def mask(d, slots, offset):
+        return slot_choice(counts_ref[d : d + 1, :], slots, rows, offset)
+
+    early = mask(0, few, 0).astype(BF)
+    place = lax.broadcasted_iota(jnp.int32, (experts * rest, 1), 0) % rest
+    late = (mask(0, rest, few) & (place < few)).astype(BF)
+    other = mask(1, rest, -few).astype(BF)
+    halves = [[mask(d, few, part * few).astype(BF) for part in range(2)] for d in range(dirs)]
+    for c in copies:
+        c.wait()
+    head = first_ref[:, :, :width].reshape(experts * few, width)
+    tail = second_ref[...].reshape(experts * rest, width)
+    terms = first_ref[:, :, width:].reshape(experts * few, LANES)
+    out_ref[0] = (dot(early, head, 0, 0) + dot(late, tail, 0, 0)).astype(BF)
+    out_ref[1] = dot(other, tail, 0, 0).astype(BF)
+    for d in range(dirs):
+        found = sum(dot(terms, halves[d][part], 0, 0)[2 * d + part :][:1] for part in range(2))
         prob_ref[d : d + 1, :] = (found / probs_ref[d : d + 1, :].astype(F32)).astype(BF)
 
 
@@ -164,21 +173,25 @@
 
 
 def row_terms(d, gate_sides, up_sides, prob, first_ref, second_ref, swapped):
-    blocks, _, slots, width = second_ref.shape
+    blocks, _, few, _ = first_ref.shape
+    width = second_ref.shape[3]
+    slots = 2 * few
     half = 2 * blocks * slots
     hidden = gate_sides[0].shape[1]
-    lane = lax.broadcasted_iota(jnp.int32, (blocks, slots, LANES), 2)
+    lane = lax.broadcasted_iota(jnp.int32, (blocks, few, LANES), 2)
     kind = second_ref.dtype
     for side in range(2):
         use = side ^ swapped
         part = d[side * half : (side + 1) * half]
         term = dot(part[:, :hidden], gate_sides[use], 1, 1) + dot(part[:, hidden:], up_sides[use], 1, 1)
-        term = term.astype(kind).reshape(blocks, 2, slots, width)
-        first_ref[:, side, :, :width] = term[:, 0]
-        second_ref[:, side] = term[:, 1]
+        term = term.reshape(blocks, 2 * slots, width)
+        first_ref[:, side, :, :width] = term[:, :few].astype(kind)
+        second_ref[:, side] = term[:, few:].astype(kind)
         spread = jnp.broadcast_to(prob[side * half : (side + 1) * half], (half, LANES))
-        spread = spread.reshape(blocks, 2, slots, LANES)
-        extra = jnp.where(lane == 0, spread[:, 0], jnp.where(lane == 1, spread[:, 1], 0.0))
+        spread = spread.reshape(blocks, 2 * slots, LANES)
+        extra = jnp.zeros((blocks, few, LANES), F32)
+        for k in range(4):
+            extra = jnp.where(lane == k, spread[:, k * few : (k + 1) * few], extra)
         first_ref[:, side, :, width:] = extra.astype(kind)
 
 
@@ -311,8 +324,9 @@
 
     side_rows = pltpu.VMEM((2, experts // 2, dirs * slots, width), BF)
     sems = pltpu.SemaphoreType.DMA
-    firsts = (experts // 2, 2, slots, width + LANES)
-    seconds = (experts // 2, 2, slots, width)
+    few = slots // 2
+    firsts = (experts // 2, 2, few, width + LANES)
+    seconds = (experts // 2, 2, dirs * slots - few, width)
 
     (x_send,) = kernel("packx", pack_body, [packed], (count_rows, acts[0]), work)
     x_own = dispatch(x_send).reshape(sided.shape)

time: 273 us -> 271 us (level)
  waiting for transfers between devices: 134 us -> 131 us
    all_to_all x5, waiting for transfers between devices: 52.4 us -> 47.8 us  [dispatch(): lax.all_to_all(array, ('expert', 'tensor'), 0, 0, axis_index_groups=group...]
    ppermute x6, waiting for transfers between devices: 70 us -> 73.4 us  [mirror(): lax.ppermute(array, 'pipe', [(i, (i + pipes // 2) % pipes) for i in range...]
  transfers between devices with their start and end apart: 17 -> 17, of which waited for: 10 -> 11; matrix products, arithmetic and copies ran while one was open for 2% -> 2% of each run, Pallas kernels for 8% -> 8%
where the time goes in v7:
time: 271 us; the launch traced here: 270 us
  waiting for transfers between devices  131 us (48%)
  starting transfers between devices  102 us (38%)
  Pallas kernels  27.5 us (10%)
  local copies, waits for them, and re-layouts  4.75 us (2%)
  other arithmetic  4.47 us (2%)
    ppermute x6, waiting for transfers between devices, mirror(): lax.ppermute(array, 'pipe', [(i, (i + pipes // 2) % pipes) for i in range...  73.4 us
    all_to_all x5, waiting for transfers between devices, dispatch(): lax.all_to_all(array, ('expert', 'tensor'), 0, 0, axis_index_groups=group...  47.8 us
    all_to_all x5, starting transfers between devices, dispatch(): lax.all_to_all(array, ('expert', 'tensor'), 0, 0, axis_index_groups=group...  39.3 us
    ppermute x6, starting transfers between devices, mirror(): lax.ppermute(array, 'pipe', [(i, (i + pipes // 2) % pipes) for i in range...  38 us
    pallas_call x13, Pallas kernels, call(): pl.pallas_call(body, out_shape=tuple(outs), in_specs=in_specs, out_specs=...  27.5 us
    ppermute x6, starting transfers between devices, swap(): return lax.ppermute(array, 'tensor', [(0, 1), (1, 0)])  24.4 us
    ppermute x6, waiting for transfers between devices, swap(): return lax.ppermute(array, 'tensor', [(0, 1), (1, 0)])  9.77 us
  transfers between devices with their start and end apart: 17, of which 11 were waited for; matrix products, arithmetic and copies ran while one was open for 2% of the time, Pallas kernels for 8%

profile of v7, /device:TPU:4, one launch (start us, length us, event | category | flops | bytes accessed | tf_op | source)
XLA Modules:
  0.0 270.3 jit_solution(11479812436056042964)
XLA Ops:
  3.2 11.8 %all-to-all-start.1 = ((bf16[16,2,16,1024]{3,2,1,0:T(8,128)(2,1)}), bf16[16,2,16,1024]{3,2,1,0:T(8,128)(2,1)}, u32[]{:S(2)}, u32[]{:S(2)}) async-start(bf16[16,2,16,1024]{3,2,1,0:T(8,128)(2,1)} %shard_map.111), calls=%async_computation.1 | async-start | bytes 2097152 | tf_op jit(solution)/shard_map/all_to_all | solution.py:289
  17.7 24.6 %all-to-all-done.1 = bf16[16,2,16,1024]{3,2,1,0:T(8,128)(2,1)} async-done(((bf16[16,2,16,1024]{3,2,1,0:T(8,128)(2,1)}), bf16[16,2,16,1024]{3,2,1,0:T(8,128)(2,1)}, u32[]{:S(2)}, u32[]{:S(2)}) %all-to-all-start.1) | async-done | bytes 1048608 | tf_op jit(solution)/shard_map/all_to_all | solution.py:289
  42.3 5.1 %all-to-all-start = ((bf16[16,2,16,1024]{3,2,1,0:T(8,128)(2,1)}), bf16[16,2,16,1024]{3,2,1,0:T(8,128)(2,1)S(1)}, u32[]{:S(2)}, u32[]{:S(2)}) async-start(bf16[16,2,16,1024]{3,2,1,0:T(8,128)(2,1)} %shard_map.110), calls=%async_computation | async-start | bytes 2097152 | tf_op jit(solution)/shard_map/all_to_all | solution.py:289
  47.4 5.5 %collective-permute-start.2 = (bf16[8,2,32,1024]{3,2,1,0:T(8,128)(2,1)}, bf16[8,2,32,1024]{3,2,1,0:T(8,128)(2,1)}, u32[]{:S(2)}, u32[]{:S(2)}) collective-permute-start(bf16[8,2,32,1024]{3,2,1,0:T(8,128)(2,1)} %bitcast.6.own), channel_id=1, source_target_pairs={{0,1},{1,0},{2,3},{3,2},{4,5},{5,4},{6,7},{7,6},{8,9},{9,8},{10,11... | collective-permute-start | bytes 3145736 | tf_op jit(solution)/shard_map/ppermute | solution.py:316
  55.6 18.5 %all-to-all-done = bf16[16,2,16,1024]{3,2,1,0:T(8,128)(2,1)S(1)} async-done(((bf16[16,2,16,1024]{3,2,1,0:T(8,128)(2,1)}), bf16[16,2,16,1024]{3,2,1,0:T(8,128)(2,1)S(1)}, u32[]{:S(2)}, u32[]{:S(2)}) %all-to-all-start) | async-done | bytes 1048608 | tf_op jit(solution)/shard_map/all_to_all | solution.py:289
  74.1 5.5 %collective-permute-start = (bf16[8,2,32,1024]{3,2,1,0:T(8,128)(2,1)S(1)}, bf16[8,2,32,1024]{3,2,1,0:T(8,128)(2,1)S(1)}, u32[]{:S(2)}, u32[]{:S(2)}) collective-permute-start(bf16[8,2,32,1024]{3,2,1,0:T(8,128)(2,1)S(1)} %bitcast.20), channel_id=1, source_target_pairs={{0,1},{1,0},{2,3},{3,2},{4,5},{5,4},{6,7},{7,6},{8,9},{9,8},{10,11... | collective-permute-start | bytes 3145736 | tf_op jit(solution)/shard_map/ppermute | solution.py:316
  85.3 7.7 %collective-permute-start.8 = (bf16[144,1024]{1,0:T(8,128)(2,1)}, bf16[144,1024]{1,0:T(8,128)(2,1)S(1)}, u32[]{:S(2)}, u32[]{:S(2)}) collective-permute-start(bf16[144,1024]{1,0:T(8,128)(2,1)} %shard_map.116), channel_id=1, source_target_pairs={{0,256},{32,288},{64,320},{96,352},{128,384},{160,416},{192,448},{... | collective-permute-start | bytes 884744 | tf_op jit(solution)/shard_map/ppermute | solution.py:313
  95.1 7.7 %collective-permute-start.4 = (bf16[1024,256]{1,0:T(8,128)(2,1)S(1)}, bf16[1024,256]{1,0:T(8,128)(2,1)}, u32[]{:S(2)}, u32[]{:S(2)}) collective-permute-start(bf16[1024,256]{1,0:T(8,128)(2,1)S(1)} %bitcast.28), channel_id=1, source_target_pairs={{0,256},{32,288},{64,320},{96,352},{128,384},{160,416},{192,448},{... | collective-permute-start | bytes 1572872 | tf_op jit(solution)/shard_map/ppermute | solution.py:313
  103.1 10.7 %collective-permute-start.1 = (bf16[256,1024]{1,0:T(8,128)(2,1)}, bf16[256,1024]{1,0:T(8,128)(2,1)}, u32[]{:S(2)}, u32[]{:S(2)}) collective-permute-start(bf16[256,1024]{1,0:T(8,128)(2,1)} %bitcast.32), channel_id=1, source_target_pairs={{0,256},{32,288},{64,320},{96,352},{128,384},{160,416},{192,448},{... | collective-permute-start | bytes 1572872 | tf_op jit(solution)/shard_map/ppermute | solution.py:313
  116.0 8.1 %all-to-all-start.4 = ((bf16[16,16,1024]{2,1,0:T(8,128)(2,1)}), bf16[16,16,1024]{2,1,0:T(8,128)(2,1)}, u32[]{:S(2)}, u32[]{:S(2)}) async-start(bf16[16,16,1024]{2,1,0:T(8,128)(2,1)} %shard_map.117), calls=%async_computation.4 | async-start | bytes 1048576 | tf_op jit(solution)/shard_map/all_to_all | solution.py:289
  124.1 25.4 %collective-permute-done.4.wuo = bf16[1024,256]{1,0:T(8,128)(2,1)} collective-permute-done((bf16[1024,256]{1,0:T(8,128)(2,1)S(1)}, bf16[1024,256]{1,0:T(8,128)(2,1)}, u32[]{:S(2)}, u32[]{:S(2)}) %collective-permute-start.4) | collective-permute-done | bytes 524320 | tf_op jit(solution)/shard_map/ppermute | solution.py:313
  149.4 4.2 %shard_map.112 = (bf16[512,256]{1,0:T(8,128)(2,1)S(1)}, bf16[256,512]{1,0:T(8,128)(2,1)S(1)}, f32[512,256]{1,0:T(8,128)S(1)}, f32[512,256]{1,0:T(8,128)S(1)}, bf16[1024,512]{1,0:T(8,128)(2,1)S(1)}) custom-call(bf16[8,2,32,1024]{3,2,1,0:T(8,128)(2,1)} %bitcast.6.own, bf16[8,2,32,1024]{3,2,1,0:T(8,128)(2,1)} %collective-permute-done.2.other, ...), custom_call_target="tpu_custom_call" | custom-call | flops 1073741824 | bytes 6815744 | tf_op jit(solution)/shard_map/pallas_call | solution.py:22
  154.6 16.0 %collective-permute-done.1.wdo = bf16[256,1024]{1,0:T(8,128)(2,1)} collective-permute-done((bf16[256,1024]{1,0:T(8,128)(2,1)}, bf16[256,1024]{1,0:T(8,128)(2,1)}, u32[]{:S(2)}, u32[]{:S(2)}) %collective-permute-start.1) | collective-permute-done | bytes 524320 | tf_op jit(solution)/shard_map/ppermute | solution.py:313
  170.6 4.9 %shard_map.113 = (bf16[512,512]{1,0:T(8,128)(2,1)S(1)}, f32[512,128]{1,0:T(8,128)S(1)}, bf16[8,2,8,1152]{3,2,1,0:T(8,128)(2,1)S(1)}, bf16[8,2,24,1024]{3,2,1,0:T(8,128)(2,1)}) custom-call(bf16[8,2,32,1024]{3,2,1,0:T(8,128)(2,1)S(1)} %bitcast.21, bf16[8,2,32,1024]{3,2,1,0:T(8,128)(2,1)S(1)} %collective-permute-done.other, bf16[256,1024]{1,0:T(8,128)(2,1)S(1)} %bitcast.33, ...), custom_call_target="tpu_custom_call" | custom-call | flops 1073741824 | bytes 8421376 | tf_op jit(solution)/shard_map/pallas_call | solution.py:22
  175.6 4.7 %collective-permute-start.5 = (bf16[8,2,8,1152]{3,2,1,0:T(8,128)(2,1)S(1)}, bf16[8,2,8,1152]{3,2,1,0:T(8,128)(2,1)S(1)}, u32[]{:S(2)}, u32[]{:S(2)}) collective-permute-start(bf16[8,2,8,1152]{3,2,1,0:T(8,128)(2,1)S(1)} %get-tuple-element.26), channel_id=1, source_target_pairs={{0,1},{1,0},{2,3},{3,2},{4,5},{5,4},{6,7},{7,6},{8,9},{9,8},{10,11... | collective-permute-start | bytes 884744 | tf_op jit(solution)/shard_map/ppermute | solution.py:316
  184.1 3.9 %collective-permute-done.5 = bf16[8,2,8,1152]{3,2,1,0:T(8,128)(2,1)S(1)} collective-permute-done((bf16[8,2,8,1152]{3,2,1,0:T(8,128)(2,1)S(1)}, bf16[8,2,8,1152]{3,2,1,0:T(8,128)(2,1)S(1)}, u32[]{:S(2)}, u32[]{:S(2)}) %collective-permute-start.5) | collective-permute-done | bytes 294944 | tf_op jit(solution)/shard_map/ppermute | solution.py:316
  188.8 8.2 %all-to-all-start.2 = ((bf16[16,8,1152]{2,1,0:T(8,128)(2,1)}), bf16[16,8,1152]{2,1,0:T(8,128)(2,1)S(1)}, u32[]{:S(2)}, u32[]{:S(2)}) async-start(bf16[16,8,1152]{2,1,0:T(8,128)(2,1)} %bitcast.9), calls=%async_computation.2 | async-start | bytes 589824 | tf_op jit(solution)/shard_map/all_to_all | solution.py:289
  202.5 4.6 %all-to-all-done.2.first = bf16[16,8,1152]{2,1,0:T(8,128)(2,1)S(1)} async-done(((bf16[16,8,1152]{2,1,0:T(8,128)(2,1)}), bf16[16,8,1152]{2,1,0:T(8,128)(2,1)S(1)}, u32[]{:S(2)}, u32[]{:S(2)}) %all-to-all-start.2) | async-done | bytes 294944 | tf_op jit(solution)/shard_map/all_to_all | solution.py:289
  207.8 6.2 %all-to-all-start.3 = ((bf16[16,24,1024]{2,1,0:T(8,128)(2,1)}), bf16[16,24,1024]{2,1,0:T(8,128)(2,1)S(1)}, u32[]{:S(2)}, u32[]{:S(2)}) async-start(bf16[16,24,1024]{2,1,0:T(8,128)(2,1)} %bitcast.42), calls=%async_computation.3 | async-start | bytes 1572864 | tf_op jit(solution)/shard_map/all_to_all | solution.py:289
  214.0 4.8 %collective-permute-start.9 = (bf16[8,2,16,1024]{3,2,1,0:T(8,128)(2,1)}, bf16[8,2,16,1024]{3,2,1,0:T(8,128)(2,1)S(1)}, u32[]{:S(2)}, u32[]{:S(2)}) collective-permute-start(bf16[8,2,16,1024]{3,2,1,0:T(8,128)(2,1)} %bitcast.14.own), channel_id=1, source_target_pairs={{0,1},{1,0},{2,3},{3,2},{4,5},{5,4},{6,7},{7,6},{8,9},{9,8},{10,11... | collective-permute-start | bytes 1572872 | tf_op jit(solution)/shard_map/ppermute | solution.py:316
  218.9 6.6 %collective-permute-start.10 = (bf16[512,512]{1,0:T(8,128)(2,1)S(1)}, bf16[512,512]{1,0:T(8,128)(2,1)S(1)}, u32[]{:S(2)}, u32[]{:S(2)}) collective-permute-start(bf16[512,512]{1,0:T(8,128)(2,1)S(1)} %copy-done.3), channel_id=1, source_target_pairs={{0,256},{32,288},{64,320},{96,352},{128,384},{160,416},{192,448},{... | collective-permute-start | bytes 1572872 | tf_op jit(solution)/shard_map/ppermute | solution.py:313
  227.0 3.3 %collective-permute-start.11 = (bf16[256,1024]{1,0:T(8,128)(2,1)S(1)}, bf16[256,1024]{1,0:T(8,128)(2,1)S(1)}, u32[]{:S(2)}, u32[]{:S(2)}) collective-permute-start(bf16[256,1024]{1,0:T(8,128)(2,1)S(1)} %shard_map.122), channel_id=1, source_target_pairs={{0,256},{32,288},{64,320},{96,352},{128,384},{160,416},{192,448},{... | collective-permute-start | bytes 1572872 | tf_op jit(solution)/shard_map/ppermute | solution.py:313
  233.6 23.6 %collective-permute-done.10.d = bf16[512,512]{1,0:T(8,128)(2,1)S(1)} collective-permute-done((bf16[512,512]{1,0:T(8,128)(2,1)S(1)}, bf16[512,512]{1,0:T(8,128)(2,1)S(1)}, u32[]{:S(2)}, u32[]{:S(2)}) %collective-permute-start.10) | collective-permute-done | bytes 524320 | tf_op jit(solution)/shard_map/ppermute | solution.py:313
  258.9 8.2 %collective-permute-done.11 = bf16[256,1024]{1,0:T(8,128)(2,1)S(1)} collective-permute-done((bf16[256,1024]{1,0:T(8,128)(2,1)S(1)}, bf16[256,1024]{1,0:T(8,128)(2,1)S(1)}, u32[]{:S(2)}, u32[]{:S(2)}) %collective-permute-start.11) | collective-permute-done | bytes 524320 | tf_op jit(solution)/shard_map/ppermute | solution.py:313
  (63 shorter events, 39.5 us)
Async XLA Ops:
  3.2 39.1 %all-to-all-start.1 = ((bf16[16,2,16,1024]{3,2,1,0:T(8,128)(2,1)}), bf16[16,2,16,1024]{3,2,1,0:T(8,128)(2,1)}, u32[]{:S(2)}, u32[]{:S(2)}) async-start(bf16[16,2,16,1024]{3,2,1,0:T(8,128)(2,1)} %shard_map.111), calls=%async_computation.1 | async-start | bytes 2097152 | tf_op jit(solution)/shard_map/all_to_all | solution.py:289
  15.0 37.9 %copy-start.15 = (bf16[1,2,128,1024]{3,2,1,0:T(8,128)(2,1)S(1)}, bf16[1,2,128,1024]{3,2,1,0:T(8,128)(2,1)}, u32[]{:S(2)}) copy-start(bf16[1,2,128,1024]{3,2,1,0:T(8,128)(2,1)} %param.7) | copy-start | bytes 1572868
  17.7 75.3 %copy-start = (bf16[1,1,1024,256]{3,2,1,0:T(8,128)(2,1)S(1)}, bf16[1,1,1024,256]{3,2,1,0:T(8,128)(2,1)}, u32[]{:S(2)}) copy-start(bf16[1,1,1024,256]{3,2,1,0:T(8,128)(2,1)} %param.11) | copy-start | bytes 1572868
  17.7 77.4 %copy-start.1 = (bf16[1,1,1024,256]{3,2,1,0:T(8,128)(2,1)S(1)}, bf16[1,1,1024,256]{3,2,1,0:T(8,128)(2,1)}, u32[]{:S(2)}) copy-start(bf16[1,1,1024,256]{3,2,1,0:T(8,128)(2,1)} %param.12) | copy-start | bytes 1572868
  42.3 31.8 %all-to-all-start = ((bf16[16,2,16,1024]{3,2,1,0:T(8,128)(2,1)}), bf16[16,2,16,1024]{3,2,1,0:T(8,128)(2,1)S(1)}, u32[]{:S(2)}, u32[]{:S(2)}) async-start(bf16[16,2,16,1024]{3,2,1,0:T(8,128)(2,1)} %shard_map.110), calls=%async_computation | async-start | bytes 2097152 | tf_op jit(solution)/shard_map/all_to_all | solution.py:289
  47.4 102.0 %collective-permute-start.2 = (bf16[8,2,32,1024]{3,2,1,0:T(8,128)(2,1)}, bf16[8,2,32,1024]{3,2,1,0:T(8,128)(2,1)}, u32[]{:S(2)}, u32[]{:S(2)}) collective-permute-start(bf16[8,2,32,1024]{3,2,1,0:T(8,128)(2,1)} %bitcast.6.own), channel_id=1, source_target_pairs={{0,1},{1,0},{2,3},{3,2},{4,5},{5,4},{6,7},{7,6},{8,9},{9,8},{10,11... | collective-permute-start | bytes 3145736 | tf_op jit(solution)/shard_map/ppermute | solution.py:316
  53.7 29.1 %collective-permute-start.7 = (bf16[128,1024]{1,0:T(8,128)(2,1)}, bf16[128,1024]{1,0:T(8,128)(2,1)S(1)}, u32[]{:S(2)}, u32[]{:S(2)}) collective-permute-start(bf16[128,1024]{1,0:T(8,128)(2,1)} %slice_bitcast_fusion), channel_id=1, source_target_pairs={{0,1},{1,0},{2,3},{3,2},{4,5},{5,4},{6,7},{7,6},{8,9},{9,8},{10,11... | collective-permute-start | bytes 786440 | tf_op jit(solution)/shard_map/ppermute | solution.py:316
  74.1 96.5 %collective-permute-start = (bf16[8,2,32,1024]{3,2,1,0:T(8,128)(2,1)S(1)}, bf16[8,2,32,1024]{3,2,1,0:T(8,128)(2,1)S(1)}, u32[]{:S(2)}, u32[]{:S(2)}) collective-permute-start(bf16[8,2,32,1024]{3,2,1,0:T(8,128)(2,1)S(1)} %bitcast.20), channel_id=1, source_target_pairs={{0,1},{1,0},{2,3},{3,2},{4,5},{5,4},{6,7},{7,6},{8,9},{9,8},{10,11... | collective-permute-start | bytes 3145736 | tf_op jit(solution)/shard_map/ppermute | solution.py:316
  85.3 17.7 %collective-permute-start.8 = (bf16[144,1024]{1,0:T(8,128)(2,1)}, bf16[144,1024]{1,0:T(8,128)(2,1)S(1)}, u32[]{:S(2)}, u32[]{:S(2)}) collective-permute-start(bf16[144,1024]{1,0:T(8,128)(2,1)} %shard_map.116), channel_id=1, source_target_pairs={{0,256},{32,288},{64,320},{96,352},{128,384},{160,416},{192,448},{... | collective-permute-start | bytes 884744 | tf_op jit(solution)/shard_map/ppermute | solution.py:313
  93.1 31.0 %collective-permute-start.3 = (bf16[1024,256]{1,0:T(8,128)(2,1)S(1)}, bf16[1024,256]{1,0:T(8,128)(2,1)}, u32[]{:S(2)}, u32[]{:S(2)}) collective-permute-start(bf16[1024,256]{1,0:T(8,128)(2,1)S(1)} %bitcast.24), channel_id=1, source_target_pairs={{0,256},{32,288},{64,320},{96,352},{128,384},{160,416},{192,448},{... | collective-permute-start | bytes 1572872 | tf_op jit(solution)/shard_map/ppermute | solution.py:313
  95.1 54.3 %collective-permute-start.4 = (bf16[1024,256]{1,0:T(8,128)(2,1)S(1)}, bf16[1024,256]{1,0:T(8,128)(2,1)}, u32[]{:S(2)}, u32[]{:S(2)}) collective-permute-start(bf16[1024,256]{1,0:T(8,128)(2,1)S(1)} %bitcast.28), channel_id=1, source_target_pairs={{0,256},{32,288},{64,320},{96,352},{128,384},{160,416},{192,448},{... | collective-permute-start | bytes 1572872 | tf_op jit(solution)/shard_map/ppermute | solution.py:313
  103.1 10.7 %copy-start.16 = (bf16[144,1024]{1,0:T(8,128)(2,1)}, bf16[144,1024]{1,0:T(8,128)(2,1)S(1)}, u32[]{:S(2)}) copy-start(bf16[144,1024]{1,0:T(8,128)(2,1)S(1)} %collective-permute-done.8.piece_ref) | copy-start | bytes 884740
  103.1 67.5 %collective-permute-start.1 = (bf16[256,1024]{1,0:T(8,128)(2,1)}, bf16[256,1024]{1,0:T(8,128)(2,1)}, u32[]{:S(2)}, u32[]{:S(2)}) collective-permute-start(bf16[256,1024]{1,0:T(8,128)(2,1)} %bitcast.32), channel_id=1, source_target_pairs={{0,256},{32,288},{64,320},{96,352},{128,384},{160,416},{192,448},{... | collective-permute-start | bytes 1572872 | tf_op jit(solution)/shard_map/ppermute | solution.py:313
  116.0 72.9 %all-to-all-start.4 = ((bf16[16,16,1024]{2,1,0:T(8,128)(2,1)}), bf16[16,16,1024]{2,1,0:T(8,128)(2,1)}, u32[]{:S(2)}, u32[]{:S(2)}) async-start(bf16[16,16,1024]{2,1,0:T(8,128)(2,1)} %shard_map.117), calls=%async_computation.4 | async-start | bytes 1048576 | tf_op jit(solution)/shard_map/all_to_all | solution.py:289
  124.1 46.6 %copy-start.12 = (bf16[1,1,256,1024]{3,2,1,0:T(8,128)(2,1)S(1)}, bf16[1,1,256,1024]{3,2,1,0:T(8,128)(2,1)}, u32[]{:S(2)}) copy-start(bf16[1,1,256,1024]{3,2,1,0:T(8,128)(2,1)} %param.13) | copy-start | bytes 1572868
  154.6 21.0 %copy-start.9 = (bf16[256,512]{1,0:T(8,128)(2,1)}, bf16[256,512]{1,0:T(8,128)(2,1)S(1)}, u32[]{:S(2)}) copy-start(bf16[256,512]{1,0:T(8,128)(2,1)S(1)} %get-tuple-element.34.act_t) | copy-start | bytes 786436
  175.6 12.5 %collective-permute-start.5 = (bf16[8,2,8,1152]{3,2,1,0:T(8,128)(2,1)S(1)}, bf16[8,2,8,1152]{3,2,1,0:T(8,128)(2,1)S(1)}, u32[]{:S(2)}, u32[]{:S(2)}) collective-permute-start(bf16[8,2,8,1152]{3,2,1,0:T(8,128)(2,1)S(1)} %get-tuple-element.26), channel_id=1, source_target_pairs={{0,1},{1,0},{2,3},{3,2},{4,5},{5,4},{6,7},{7,6},{8,9},{9,8},{10,11... | collective-permute-start | bytes 884744 | tf_op jit(solution)/shard_map/ppermute | solution.py:316
  180.2 19.5 %collective-permute-start.6 = (bf16[8,2,24,1024]{3,2,1,0:T(8,128)(2,1)}, bf16[8,2,24,1024]{3,2,1,0:T(8,128)(2,1)}, u32[]{:S(2)}, u32[]{:S(2)}) collective-permute-start(bf16[8,2,24,1024]{3,2,1,0:T(8,128)(2,1)} %get-tuple-element.28), channel_id=1, source_target_pairs={{0,1},{1,0},{2,3},{3,2},{4,5},{5,4},{6,7},{7,6},{8,9},{9,8},{10,11... | collective-permute-start | bytes 2359304 | tf_op jit(solution)/shard_map/ppermute | solution.py:316
  188.8 18.2 %all-to-all-start.2 = ((bf16[16,8,1152]{2,1,0:T(8,128)(2,1)}), bf16[16,8,1152]{2,1,0:T(8,128)(2,1)S(1)}, u32[]{:S(2)}, u32[]{:S(2)}) async-start(bf16[16,8,1152]{2,1,0:T(8,128)(2,1)} %bitcast.9), calls=%async_computation.2 | async-start | bytes 589824 | tf_op jit(solution)/shard_map/all_to_all | solution.py:289
  202.5 16.4 %copy-start.3 = (bf16[512,512]{1,0:T(8,128)(2,1)S(1)}, bf16[512,512]{1,0:T(8,128)(2,1)}, u32[]{:S(2)}) copy-start(bf16[512,512]{1,0:T(8,128)(2,1)} %copy-done.2) | copy-start | bytes 1572868
  207.8 60.2 %all-to-all-start.3 = ((bf16[16,24,1024]{2,1,0:T(8,128)(2,1)}), bf16[16,24,1024]{2,1,0:T(8,128)(2,1)S(1)}, u32[]{:S(2)}, u32[]{:S(2)}) async-start(bf16[16,24,1024]{2,1,0:T(8,128)(2,1)} %bitcast.42), calls=%async_computation.3 | async-start | bytes 1572864 | tf_op jit(solution)/shard_map/all_to_all | solution.py:289
  214.0 16.3 %collective-permute-start.9 = (bf16[8,2,16,1024]{3,2,1,0:T(8,128)(2,1)}, bf16[8,2,16,1024]{3,2,1,0:T(8,128)(2,1)S(1)}, u32[]{:S(2)}, u32[]{:S(2)}) collective-permute-start(bf16[8,2,16,1024]{3,2,1,0:T(8,128)(2,1)} %bitcast.14.own), channel_id=1, source_target_pairs={{0,1},{1,0},{2,3},{3,2},{4,5},{5,4},{6,7},{7,6},{8,9},{9,8},{10,11... | collective-permute-start | bytes 1572872 | tf_op jit(solution)/shard_map/ppermute | solution.py:316
  218.9 38.3 %collective-permute-start.10 = (bf16[512,512]{1,0:T(8,128)(2,1)S(1)}, bf16[512,512]{1,0:T(8,128)(2,1)S(1)}, u32[]{:S(2)}, u32[]{:S(2)}) collective-permute-start(bf16[512,512]{1,0:T(8,128)(2,1)S(1)} %copy-done.3), channel_id=1, source_target_pairs={{0,256},{32,288},{64,320},{96,352},{128,384},{160,416},{192,448},{... | collective-permute-start | bytes 1572872 | tf_op jit(solution)/shard_map/ppermute | solution.py:313
  227.0 40.1 %collective-permute-start.11 = (bf16[256,1024]{1,0:T(8,128)(2,1)S(1)}, bf16[256,1024]{1,0:T(8,128)(2,1)S(1)}, u32[]{:S(2)}, u32[]{:S(2)}) collective-permute-start(bf16[256,1024]{1,0:T(8,128)(2,1)S(1)} %shard_map.122), channel_id=1, source_target_pairs={{0,256},{32,288},{64,320},{96,352},{128,384},{160,416},{192,448},{... | collective-permute-start | bytes 1572872 | tf_op jit(solution)/shard_map/ppermute | solution.py:313
  (11 other events, 49.3 us)
